TPU v7x, 512 devices: a whole 4x8x8 slice. The times are simulated.
512 devices in a mesh: section: 8 (over z_hi, core), expert: 64 (over y, x, z_lo).
Axes of the slice: x: 4, y: 8, z: 8 (z_hi: 4, z_lo: 2; z = z_hi * 2 + z_lo), core: 2. Of those that a mesh axis runs over, the one named last changes fastest.
Arguments:
- tokens: bfloat16 [8, 16384, 1024], P('section', 'expert'), may hold values from -6 to 6
- gates: float32 [8, 16384], P('section', 'expert'), may hold values from 0.2 to 1
- routes: int32 [8, 16384, 1], P('section', 'expert'), may hold values from 0 to 63; in each aligned block of 256 rows (0 to 255, 256 to 511, ..., all dimensions but the last counted through in order) at most 8 rows name the same one
- capacity: int32 [8, 64], P('section', 'expert'), may hold values from 128 to 512
- mem_lengths: int32 [8, 64], P('section', 'expert'), may hold values from 64 to 256
- mem_keys: bfloat16 [8, 8192, 1024], P('section', 'expert')
- mem_values: bfloat16 [8, 8192, 1024], P('section', 'expert'), may hold values from -6 to 6
- q_weight: bfloat16 [8, 1024, 1024], P('section', 'expert'), may hold values from -0.1875 to 0.1875
- out_weight: bfloat16 [8, 1024, 1024], P('section', 'expert'), may hold values from -0.75 to 0.75
- w_in: bfloat16 [8, 64, 1024, 1408], P('section', 'expert'), may hold values from -0.1875 to 0.1875
Outputs:
- expert_hidden: bfloat16 [8, 16384, 1408], P('section', 'expert')
Inputs may be any that keep to these rules, and one draw needn't show every extreme that they name: `routes`: among the 256 rows of one device at most 8 name one expert.
All inputs are finite; a program needn't handle non-finite values.
Results may differ from a plain program's by a relative error of at most 0.013.
Values may be sent and summed in bfloat16 or wider, within the bound.
No kernel may reach another device: no remote copies, remote signals or barrier semaphores. Data moves between devices by JAX's collectives and lax.ppermute only.
A program may use at most 64 MiB of HBM per device.

v0:
```python
import jax
import jax.numpy as jnp
from jax import lax
from jax.sharding import PartitionSpec as P

HEADS = 16


def from_behind(x, axis, by):
    peers = lax.axis_size(axis)
    pairs = [(i, i + by) for i in range(peers) if 0 <= i + by < peers]
    return lax.ppermute(x, axis, pairs)


def carried_in(x, axis, combine, identity):
    peers, place = (lax.axis_size(axis), lax.axis_index(axis))
    everything = lax.all_gather(x, axis)
    start = jnp.broadcast_to(jnp.asarray(identity, x.dtype), x.shape)

    def lap(k, before):
        reached = k < place
        new = combine(before, everything[k])
        return jnp.where(reached, new, before)

    return lax.fori_loop(0, peers, lap, start)


def row_folder(left, piece):
    return jnp.dot(left, piece, preferred_element_type=jnp.float32)


def attend_block(query, keys, values, length):
    rows = query.shape[0]
    span = keys.shape[0]
    heads = HEADS
    qh = query.reshape(rows, heads, -1)
    kh = keys.reshape(span, heads, -1)
    vh = values.reshape(span, heads, -1)
    scores = jnp.einsum("qhd,khd->hqk", qh, kh, preferred_element_type=jnp.float32) / jnp.sqrt(
        jnp.float32(qh.shape[2])
    )
    valid = jnp.arange(span, dtype=jnp.int32) < length
    scores = jnp.where(valid[None, None, :], scores, jnp.float32(-1e30))
    scores = scores - jnp.max(scores, axis=-1, keepdims=True)
    weights = jnp.exp(scores)
    probs = (weights / jnp.sum(weights, axis=-1, keepdims=True)).astype(jnp.bfloat16)
    context = jnp.einsum("hqk,khd->qhd", probs, vh, preferred_element_type=jnp.float32)
    return context.reshape(rows, -1).astype(jnp.bfloat16)


def shards(
    tokens, gates, routes, capacity, mem_lengths, mem_keys, mem_values, q_weight, out_weight, w_in
):
    sections = lax.axis_size("section")
    half = sections // 2
    experts = lax.axis_size("expert")
    inputs = tokens[0]
    tok_dev = inputs.shape[0]
    width = inputs.shape[1]
    cap = max(8, 2 * tok_dev // experts)
    remote = from_behind((mem_keys[0], mem_values[0]), "section", half)
    keys = jnp.concatenate([remote[0], mem_keys[0]], axis=0)
    values = jnp.concatenate([remote[1], mem_values[0]], axis=0)
    query = row_folder(inputs, lax.all_gather(q_weight[0], "expert", axis=0, tiled=True)).astype(
        jnp.bfloat16
    )
    context = attend_block(query, keys, values, mem_lengths[0, 0])
    attn_out = row_folder(context, lax.all_gather(out_weight[0], "expert", axis=0, tiled=True))
    decoding = lax.axis_index("section") >= half
    mixed = jnp.where(
        decoding, (inputs.astype(jnp.float32) + attn_out).astype(jnp.bfloat16), inputs
    )
    route = routes[0, :, 0]
    onehot = (route[:, None] == jnp.arange(experts, dtype=jnp.int32)[None, :]).astype(jnp.int32)
    lrank = jnp.sum((jnp.cumsum(onehot, axis=0) - onehot) * onehot, axis=1)
    counts = jnp.sum(onehot, axis=0)
    slot = route * cap + lrank
    placing = (slot[:, None] == jnp.arange(experts * cap, dtype=jnp.int32)[None, :]).astype(
        jnp.bfloat16
    )
    w_local = w_in[0, 0]
    offsets = carried_in(
        counts, "expert", lambda earlier, later: earlier + later, jnp.zeros_like(counts)
    )
    limits = lax.all_gather(capacity[0], "expert", axis=0, tiled=True)
    grank = jnp.sum(onehot * offsets[None, :], axis=1) + lrank
    kept = grank < jnp.sum(onehot * limits[None, :], axis=1)
    sending = jnp.where(kept[:, None], mixed, jnp.zeros_like(mixed))
    buffer = jnp.einsum("ts,td->sd", placing, sending, preferred_element_type=jnp.float32).astype(
        jnp.bfloat16
    )
    received = lax.all_to_all(
        buffer.reshape(experts, cap, width), "expert", split_axis=0, concat_axis=0, tiled=True
    )
    acts = jnp.maximum(
        jnp.dot(
            received.reshape(experts * cap, width), w_local, preferred_element_type=jnp.float32
        ),
        0.0,
    )
    acts = acts.astype(jnp.bfloat16).reshape(experts, cap, -1)
    back = lax.all_to_all(acts, "expert", split_axis=0, concat_axis=0, tiled=True)
    picked = jnp.dot(placing, back.reshape(experts * cap, -1), preferred_element_type=jnp.float32)
    result = (picked * gates[0][:, None]).astype(jnp.bfloat16)
    return result[None, :, :]


def solution(mesh):
    in_specs = (
        P("section", "expert", None),
        P("section", "expert"),
        P("section", "expert", None),
        P("section", "expert"),
        P("section", "expert"),
        P("section", "expert", None),
        P("section", "expert", None),
        P("section", "expert", None),
        P("section", "expert", None),
        P("section", "expert", None, None),
    )
    out_specs = P("section", "expert", None)
    return jax.shard_map(shards, mesh=mesh, in_specs=in_specs, out_specs=out_specs, check_vma=False)
```

profile of v0, /device:TPU:6, one launch (start us, length us, event | category | flops | bytes accessed | tf_op | source)
XLA Modules:
  0.0 688.5 jit_solution(10100261019925258688)
XLA Ops:
  6.5 0.7 all-gather.7.cloned.1.call-update
  7.3 0.0 all-gather.9.cloned.1.call-start
  7.3 11.1 %collective-permute-start.1 = (bf16[128,1024]{1,0:T(8,128)(2,1)}, bf16[128,1024]{1,0:T(8,128)(2,1)S(1)}, u32[]{:S(2)}, u32[]{:S(2)}) collective-permute-start(bf16[128,1024]{1,0:T(8,128)(2,1)} %bitcast.81), channel_id=1, source_target_pairs={{0,256},{64,320},{128,384},{192,448},{1,257},{65,321},{129,385},{1... | collective-permute-start | bytes 786440 | tf_op jit(solution)/shard_map/ppermute | solution.py:12
  18.4 1.3 collective-permute-start
  19.7 0.0 all-gather.9.cloned.1.call-update
  20.4 0.8 convert_reduce_fusion
  21.2 1.3 dynamic-slice
  23.1 0.7 bitcast_dynamic-update-slice_fusion
  23.8 0.3 dynamic-update-slice
  24.1 308.2 %all-reduce.2 = (s32[64]{0:T(128)S(1)}, s32[4096]{0:T(1024)S(1)}) all-reduce(s32[64]{0:T(128)S(1)} %bitcast_dynamic-update-slice_fusion, s32[4096]{0:T(1024)S(1)} %dynamic-update-slice), channel_id=3, replica_groups=mesh['section'=8,'expert'=64] {'expert'}, use_global_device_ids=true, to_apply=%add.1 | all-reduce | flops 4160 | bytes 33280
  332.3 0.1 reshape.73
  332.4 2.6 while.14
  335.6 0.7 fusion.54
  336.3 0.6 reduce-window.6
  336.9 0.2 slice_reduce_fusion
  337.2 0.8 fusion.53
  338.0 0.7 multiply_add_fusion
  338.6 1.8 copy.22
  340.4 1.8 copy.19
  342.2 0.9 copy.21
  343.1 0.8 copy.18
  343.9 3.3 fusion.22
  347.2 1.2 copy.20
  348.5 1.8 fusion.41
  350.3 1.7 fusion.60
  352.0 1.3 fusion.28
  353.3 257.8 %all-gather.9.cloned.1.call-done = bf16[1,1024,1024]{2,1,0:T(8,128)(2,1)} async-done(((bf16[1,16,1024]{2,1,0:T(8,128)(2,1)}), bf16[1,1024,1024]{2,1,0:T(8,128)(2,1)}) %all-gather.9.cloned.1.call-update) | async-done | bytes 2097168 | tf_op jit(solution)/shard_map/all_gather | solution.py:68
  611.1 3.8 fusion.18
  614.9 34.5 %all_to_all.10 = bf16[64,8,1024]{2,1,0:T(8,128)(2,1)S(1)} all-to-all(bf16[64,8,1024]{2,1,0:T(8,128)(2,1)} %fusion.18), channel_id=1, replica_groups=mesh['section'=8,'expert'=64] {'expert'}, dimensions={0} | all-to-all | bytes 2097152 | tf_op jit(solution)/shard_map/all_to_all | solution.py:92
  649.4 1.8 fusion.4
  651.2 28.9 %all_to_all.11 = bf16[64,8,1408]{2,1,0:T(8,128)(2,1)S(1)} all-to-all(bf16[64,8,1408]{2,1,0:T(8,128)(2,1)S(1)} %fusion.4), channel_id=1, replica_groups=mesh['section'=8,'expert'=64] {'expert'}, dimensions={0} | all-to-all | bytes 2883584 | tf_op jit(solution)/shard_map/all_to_all | solution.py:102
  680.1 1.5 fusion.8
  (85 shorter events, 1.2 us)
Async XLA Ops:
  6.5 642.9 %copy-start = (bf16[1,1,1024,1408]{3,2,1,0:T(8,128)(2,1)S(1)}, bf16[1,1,1024,1408]{3,2,1,0:T(8,128)(2,1)}, u32[]{:S(2)}) copy-start(bf16[1,1,1024,1408]{3,2,1,0:T(8,128)(2,1)} %param.21) | copy-start | bytes 8650756
  6.5 337.4 %all-gather.7.cloned.1.call-start = ((), (), s32[]{:S(2)}) async-start(), calls=%async_computation.2 | async-start | bytes 2129920 | tf_op jit(solution)/shard_map/all_gather | solution.py:64
  7.3 603.8 %all-gather.9.cloned.1.call-start = ((), (), s32[]{:S(2)}) async-start(), calls=%async_computation.3 | async-start | bytes 2129920 | tf_op jit(solution)/shard_map/all_gather | solution.py:68
  7.3 334.9 %collective-permute-start.1 = (bf16[128,1024]{1,0:T(8,128)(2,1)}, bf16[128,1024]{1,0:T(8,128)(2,1)S(1)}, u32[]{:S(2)}, u32[]{:S(2)}) collective-permute-start(bf16[128,1024]{1,0:T(8,128)(2,1)} %bitcast.81), channel_id=1, source_target_pairs={{0,256},{64,320},{128,384},{192,448},{1,257},{65,321},{129,385},{1... | collective-permute-start | bytes 786440 | tf_op jit(solution)/shard_map/ppermute | solution.py:12
  18.4 324.7 %collective-permute-start = (bf16[128,1024]{1,0:T(8,128)(2,1)}, bf16[128,1024]{1,0:T(8,128)(2,1)S(1)}, u32[]{:S(2)}, u32[]{:S(2)}) collective-permute-start(bf16[128,1024]{1,0:T(8,128)(2,1)} %bitcast.82), channel_id=1, source_target_pairs={{0,256},{64,320},{128,384},{192,448},{1,257},{65,321},{129,385},{1... | collective-permute-start | bytes 786440 | tf_op jit(solution)/shard_map/ppermute | solution.py:12
  350.3 1.7 copy-start.1
  350.3 1.7 copy-start.2
  352.0 259.1 %copy-start.3 = (bf16[1,256,1024]{2,1,0:T(8,128)(2,1)S(1)}, bf16[1,256,1024]{2,1,0:T(8,128)(2,1)}, u32[]{:S(2)}) copy-start(bf16[1,256,1024]{2,1,0:T(8,128)(2,1)} %param.12) | copy-start | bytes 1572868
  651.2 28.9 %copy-start.4 = (f32[1,256]{1,0:T(1,128)S(1)}, f32[1,256]{1,0:T(1,128)}, u32[]{:S(2)}) copy-start(f32[1,256]{1,0:T(1,128)} %param.13) | copy-start | bytes 3076
Sparse Core Ops, SparseCore 0:
  9.4 299.3 all-gather.6
  310.9 300.1 all-gather.8
where the time goes:
time: 690 us; the launch traced here: 688 us
  blocking collectives  372 us (54%)
  waiting for transfers between devices  258 us (37%)
  between operations  15.5 us (2%)
  matrix products  13.5 us (2%)
  starting transfers between devices  12.4 us (2%)
  local copies, waits for them, and re-layouts  9.02 us (1%)
    unnamed x1, blocking collectives  308 us
    all_gather x1, waiting for transfers between devices, shards(): lax.all_gather(out_weight[0], 'expert', axis=0, tiled=True)  258 us
    all_to_all x1, blocking collectives, shards(): lax.all_to_all(buffer.reshape(experts, cap, width), 'expert', split_axis=...  34.5 us
    all_to_all x1, blocking collectives, shards(): lax.all_to_all(acts, 'expert', split_axis=0, concat_axis=0, tiled=True)  28.9 us
  transfers between devices with their start and end apart: 4, of which 1 were waited for; matrix products, arithmetic and copies ran while one was open for 3% of the time, Pallas kernels for 0%

commit v1 on v0

v1 whole, which is shorter than its diff:
```python
import jax
import jax.numpy as jnp
from jax import lax
from jax.sharding import Mesh, PartitionSpec as P

HEADS = 16
EMPTY = 1e30
AXES = ("y", "x", "z")


def gathered(x, axis):
    peers = lax.axis_size(axis)
    return lax.all_to_all(jnp.broadcast_to(x[None], (peers, *x.shape)), axis, 0, 0, tiled=True)


def attend_block(query, keys, values, length):
    rows = query.shape[0]
    span = keys.shape[0]
    qh = query.reshape(rows, HEADS, -1)
    kh = keys.reshape(span, HEADS, -1)
    vh = values.reshape(span, HEADS, -1)
    scores = jnp.einsum("qhd,khd->hqk", qh, kh, preferred_element_type=jnp.float32) / jnp.sqrt(
        jnp.float32(qh.shape[2])
    )
    valid = jnp.arange(span, dtype=jnp.int32) < length
    scores = jnp.where(valid[None, None, :], scores, jnp.float32(-1e30))
    scores = scores - jnp.max(scores, axis=-1, keepdims=True)
    weights = jnp.exp(scores)
    probs = (weights / jnp.sum(weights, axis=-1, keepdims=True)).astype(jnp.bfloat16)
    context = jnp.einsum("hqk,khd->qhd", probs, vh, preferred_element_type=jnp.float32)
    return context.reshape(rows, -1).astype(jnp.bfloat16)


def shards(
    tokens, gates, routes, capacity, mem_lengths, mem_keys, mem_values, q_weight, out_weight, w_in
):
    sections = lax.axis_size("section")
    half = sections // 2
    experts = lax.axis_size(AXES)
    inputs = tokens[0]
    tok_dev, width = inputs.shape
    cap = max(8, 2 * tok_dev // experts)
    pairs = [(i, i + half) for i in range(half)]
    keys_far, values_far = lax.ppermute((mem_keys[0], mem_values[0]), "section", pairs)
    keys = jnp.concatenate([keys_far, mem_keys[0]], axis=0)
    values = jnp.concatenate([values_far, mem_values[0]], axis=0)

    both = jnp.stack([q_weight[0], out_weight[0]])
    both = gathered(gathered(both, "y"), ("x", "z"))
    both = both.transpose(2, 1, 0, 3, 4).reshape(2, width, width)
    wq, wo = both[0], both[1]

    query = jnp.dot(inputs, wq, preferred_element_type=jnp.float32).astype(jnp.bfloat16)
    context = attend_block(query, keys, values, mem_lengths[0, 0])
    attn_out = jnp.dot(context, wo, preferred_element_type=jnp.float32)
    decoding = lax.axis_index("section") >= half
    mixed = jnp.where(
        decoding, (inputs.astype(jnp.float32) + attn_out).astype(jnp.bfloat16), inputs
    )

    route = routes[0, :, 0]
    same = route[:, None] == route[None, :]
    earlier = jnp.arange(tok_dev)[None, :] < jnp.arange(tok_dev)[:, None]
    lrank = jnp.sum((same & earlier).astype(jnp.int32), axis=1)
    slot = route * cap + lrank
    placed = slot[:, None] == jnp.arange(experts * cap, dtype=jnp.int32)[None, :]
    placing = placed.astype(jnp.bfloat16)
    buffer = jnp.einsum("ts,td->sd", placing, mixed, preferred_element_type=jnp.float32).astype(
        jnp.bfloat16
    )
    used = jnp.any(placed, axis=0)
    buffer = jnp.where(used[:, None], buffer, jnp.bfloat16(EMPTY))
    received = lax.all_to_all(
        buffer.reshape(experts, cap, width), AXES, split_axis=0, concat_axis=0, tiled=True
    )
    filled = received[:, :, 0].astype(jnp.float32) < EMPTY / 2
    counts = jnp.sum(filled.astype(jnp.int32), axis=1)
    before = jnp.sum(
        jnp.where(jnp.arange(experts)[None, :] < jnp.arange(experts)[:, None], counts[None, :], 0),
        axis=1,
    )
    rank = before[:, None] + jnp.arange(cap, dtype=jnp.int32)[None, :]
    kept = filled & (rank < capacity[0, 0])
    acts = jnp.maximum(
        jnp.dot(
            received.reshape(experts * cap, width), w_in[0, 0], preferred_element_type=jnp.float32
        ),
        0.0,
    )
    acts = jnp.where(kept.reshape(-1)[:, None], acts, 0.0).astype(jnp.bfloat16)
    back = lax.all_to_all(
        acts.reshape(experts, cap, -1), AXES, split_axis=0, concat_axis=0, tiled=True
    )
    picked = jnp.dot(placing, back.reshape(experts * cap, -1), preferred_element_type=jnp.float32)
    result = (picked * gates[0][:, None]).astype(jnp.bfloat16)
    return result[None, :, :]


def solution(mesh):
    sections, experts = mesh.shape["section"], mesh.shape["expert"]
    x, z = 4, 2
    grid = Mesh(
        mesh.devices.reshape(sections, experts // (x * z), x, z), ("section", "y", "x", "z")
    )
    in_specs = (
        P("section", AXES, None),
        P("section", AXES),
        P("section", AXES, None),
        P("section", AXES),
        P("section", AXES),
        P("section", AXES, None),
        P("section", AXES, None),
        P("section", AXES, None),
        P("section", AXES, None),
        P("section", AXES, None, None),
    )
    out_specs = P("section", AXES, None)
    return jax.shard_map(shards, mesh=grid, in_specs=in_specs, out_specs=out_specs, check_vma=False)
```

time: 690 us -> 201 us (0.29)
  blocking collectives: 372 us -> 65.5 us
  waiting for transfers between devices: 258 us -> 63.3 us
  starting transfers between devices: 12.4 us -> 38.7 us
  between operations: 15.5 us -> 1.48 us
    unnamed x1 -> x0, blocking collectives: 308 us -> none
    all_gather x2 -> x0, waiting for transfers between devices: 258 us -> none  [the longest x1 258 us: shards(): lax.all_gather(out_weight[0], 'expert', axis=0, tiled=True)]
    ppermute x2, waiting for transfers between devices: 0.01 us -> 37.7 us  [shards(): lax.ppermute((mem_keys[0], mem_values[0]), 'section', pairs)]
    all_to_all x0 -> x2, starting transfers between devices: none -> 26 us  [the longest x1 19.3 us: shards(): lax.all_to_all(buffer.reshape(experts, cap, width), AXES, split_axis=0, c...]
    all_to_all x0 -> x2, waiting for transfers between devices: none -> 25.5 us  [the longest x1 25.5 us: shards(): lax.all_to_all(buffer.reshape(experts, cap, width), AXES, split_axis=0, c...]
  transfers between devices with their start and end apart: 4 -> 4, of which waited for: 1 -> 3; matrix products, arithmetic and copies ran while one was open for 3% -> 3% of each run, Pallas kernels for 0% -> 0%
where the time goes in v1:
time: 201 us; the launch traced here: 200 us
  blocking collectives  65.5 us (33%)
  waiting for transfers between devices  63.3 us (31%)
  starting transfers between devices  38.7 us (19%)
  local copies, waits for them, and re-layouts  12.1 us (6%)
  matrix products  11.2 us (6%)
  other arithmetic  7.47 us (4%)
    all_to_all x1, blocking collectives, shards(): lax.all_to_all(acts.reshape(experts, cap, -1), AXES, split_axis=0, concat...  41.2 us
    ppermute x2, waiting for transfers between devices, shards(): lax.ppermute((mem_keys[0], mem_values[0]), 'section', pairs)  37.7 us
    all_to_all x1, waiting for transfers between devices, shards(): lax.all_to_all(buffer.reshape(experts, cap, width), AXES, split_axis=0, c...  25.5 us
    all_to_all x1, blocking collectives, gathered(): lax.all_to_all(jnp.broadcast_to(x[None], (peers, *x.shape)), axis, 0, 0,...  24.4 us
    all_to_all x1, starting transfers between devices, shards(): lax.all_to_all(buffer.reshape(experts, cap, width), AXES, split_axis=0, c...  19.3 us
    ppermute x2, starting transfers between devices, shards(): lax.ppermute((mem_keys[0], mem_values[0]), 'section', pairs)  12.7 us
    all_to_all x1, starting transfers between devices, gathered(): lax.all_to_all(jnp.broadcast_to(x[None], (peers, *x.shape)), axis, 0, 0,...  6.72 us
  transfers between devices with their start and end apart: 4, of which 3 were waited for; matrix products, arithmetic and copies ran while one was open for 3% of the time, Pallas kernels for 0%

profile of v1, /device:TPU:6, one launch (start us, length us, event | category | flops | bytes accessed | tf_op | source)
XLA Modules:
  0.0 199.7 jit_solution(6741214633543317800)
XLA Ops:
  0.0 0.9 pad_maximum_fusion
  1.0 24.4 %all_to_all.20 = bf16[8,2,16,1024]{3,2,1,0:T(8,128)(2,1)S(1)} all-to-all(bf16[8,2,16,1024]{3,2,1,0:T(8,128)(2,1)S(1)} %broadcast_in_dim.76), channel_id=1, replica_groups=mesh['section'=8,'y'=8,'x'=4,'z'=2] {'y'}, dimensions={0} | all-to-all | bytes 1048576 | tf_op jit(solution)/shard_map/all_to_all | solution.py:13
  25.4 2.5 %broadcast_in_dim.77 = bf16[8,8,2,16,1024]{4,3,1,2,0:T(8,128)(2,1)} broadcast(bf16[8,2,16,1024]{3,2,0,1:T(8,128)(2,1)S(1)} %copy.36), dimensions={1,2,3,4} | broadcast | bytes 4718592 | tf_op jit(solution)/shard_map/broadcast_in_dim | solution.py:13
  27.9 6.7 %all-to-all-start.1 = ((bf16[8,8,2,16,1024]{4,3,1,2,0:T(8,128)(2,1)}), bf16[8,8,2,16,1024]{4,3,1,2,0:T(8,128)(2,1)}, u32[]{:S(2)}, u32[]{:S(2)}) async-start(bf16[8,8,2,16,1024]{4,3,1,2,0:T(8,128)(2,1)} %broadcast_in_dim.77), calls=%async_computation.1 | async-start | bytes 8388608 | tf_op jit(solution)/shard_map/all_to_all | solution.py:13
  34.7 10.7 %collective-permute-start.1 = (bf16[128,1024]{1,0:T(8,128)(2,1)S(1)}, bf16[128,1024]{1,0:T(8,128)(2,1)}, u32[]{:S(2)}, u32[]{:S(2)}) collective-permute-start(bf16[128,1024]{1,0:T(8,128)(2,1)S(1)} %bitcast.57), channel_id=1, source_target_pairs={{0,256},{64,320},{128,384},{192,448},{1,257},{65,321},{129,385},{1... | collective-permute-start | bytes 786440 | tf_op jit(solution)/shard_map/ppermute | solution.py:44
  45.4 2.0 collective-permute-start
  47.4 0.2 convert_reduce_fusion.1
  47.6 0.2 copy.39
  47.7 1.8 copy.35
  50.2 0.1 fusion.30
  50.4 35.9 %collective-permute-done.1 = bf16[128,1024]{1,0:T(8,128)(2,1)} collective-permute-done((bf16[128,1024]{1,0:T(8,128)(2,1)S(1)}, bf16[128,1024]{1,0:T(8,128)(2,1)}, u32[]{:S(2)}, u32[]{:S(2)}) %collective-permute-start.1) | collective-permute-done | bytes 262176 | tf_op jit(solution)/shard_map/ppermute | solution.py:44
  86.3 1.1 copy.38
  87.4 1.8 collective-permute-done
  89.2 1.8 copy.34
  91.0 2.6 %copy.43 = bf16[8,8,2,16,1024]{4,3,0,1,2:T(8,128)(2,1)S(1)} copy(bf16[8,8,2,16,1024]{4,3,1,2,0:T(8,128)(2,1)} %all-to-all-done.1) | data formatting | bytes 8388608 | tf_op jit(solution)/shard_map/all_to_all | solution.py:13
  93.6 1.8 fusion.40
  95.4 0.8 convolution_convert_fusion.1
  96.2 0.8 fusion.24
  97.0 1.8 fusion.41
  98.8 1.3 fusion.18
  100.1 3.8 %fusion.16 = bf16[64,8,1024]{2,1,0:T(8,128)(2,1)} fusion(pred[512]{0:T(512)(128)(4,1)S(1)} %fusion.30, bf16[256,1024]{0,1:T(8,128)(2,1)} %bitcast.63, bf16[1024,1024]{1,0:T(8,128)(2,1)} %bitcast.52, bf16[1,256,1024]{2,1,0:T(8,128)(2,1)S(1)} %copy-done.6, pred[]{:T(512)S(6)} %ge.3, s32[256]{0:T(256)S(1)} %multiply_add_fusion), kind=kOutput, calls=%fused_computation.21 | convolution fusion | flops 807534592 | bytes 4195841 | tf_op jit(solution)/shard_map/ts,td->sd/dot_general | solution.py:68
  104.0 19.3 %all-to-all-start.2 = ((bf16[64,8,1024]{2,1,0:T(8,128)(2,1)}), bf16[64,8,1024]{2,1,0:T(8,128)(2,1)}, u32[]{:S(2)}, u32[]{:S(2)}) async-start(bf16[64,8,1024]{2,1,0:T(8,128)(2,1)} %fusion.16), calls=%async_computation.2 | async-start | bytes 2097152 | tf_op jit(solution)/shard_map/all_to_all | solution.py:73
  123.9 25.5 %all-to-all-done.2 = bf16[64,8,1024]{2,1,0:T(8,128)(2,1)} async-done(((bf16[64,8,1024]{2,1,0:T(8,128)(2,1)}), bf16[64,8,1024]{2,1,0:T(8,128)(2,1)}, u32[]{:S(2)}, u32[]{:S(2)}) %all-to-all-start.2) | async-done | bytes 1048608 | tf_op jit(solution)/shard_map/all_to_all | solution.py:73
  149.4 2.1 %convert_reduce_fusion = s32[64]{0:T(128)S(1)} fusion(bf16[64,8,1024]{2,1,0:T(8,128)(2,1)} %all-to-all-done.2), kind=kLoop, calls=%fused_computation.40 | loop fusion | flops 1984 | bytes 1280 | tf_op jit(solution)/shard_map/reduce_sum | solution.py:77
  151.5 0.1 select_reduce_fusion
  151.7 0.1 add_compare_fusion
  151.7 0.1 lt.76
  151.8 2.1 %fusion.35 = pred[64,8]{1,0:T(8,128)(4,1)S(1)} fusion(bf16[64,8,1024]{2,1,0:T(8,128)(2,1)} %all-to-all-done.2), kind=kLoop, calls=%fused_computation.51 | loop fusion | flops 1024 | bytes 1536 | tf_op jit(solution)/shard_map/lt | solution.py:76
  153.9 0.1 lt.70
  154.0 3.0 %fusion.5 = bf16[64,8,1408]{2,1,0:T(8,128)(2,1)S(1)} fusion(bf16[1,1,1024,1408]{3,2,1,0:T(8,128)(2,1)S(1)} %copy-done, pred[512]{0:T(512)(128)(4,1)S(1)} %and.12, bf16[64,8,1024]{2,1,0:T(8,128)(2,1)} %all-to-all-done.2), kind=kOutput, calls=%fused_computation.11 | convolution fusion | flops 1478557696 | bytes 5374464 | tf_op jit(solution)/shard_map/dot_general | solution.py:85
  157.1 41.2 %all_to_all.21 = bf16[64,8,1408]{2,1,0:T(8,128)(2,1)S(1)} all-to-all(bf16[64,8,1408]{2,1,0:T(8,128)(2,1)S(1)} %fusion.5), channel_id=1, replica_groups=mesh['section'=8,'y'=8,'x'=4,'z'=2] {'y','x','z'}, dimensions={0} | all-to-all | bytes 2883584 | tf_op jit(solution)/shard_map/all_to_all | solution.py:91
  198.2 1.5 fusion.9
  (22 shorter events, 0.1 us)
Async XLA Ops:
  0.0 154.0 %copy-start = (bf16[1,1,1024,1408]{3,2,1,0:T(8,128)(2,1)S(1)}, bf16[1,1,1024,1408]{3,2,1,0:T(8,128)(2,1)}, u32[]{:S(2)}) copy-start(bf16[1,1,1024,1408]{3,2,1,0:T(8,128)(2,1)} %param.19) | copy-start | bytes 8650756
  27.9 6.7 %copy-start.1 = (bf16[1,128,1024]{2,1,0:T(8,128)(2,1)S(1)}, bf16[1,128,1024]{2,1,0:T(8,128)(2,1)}, u32[]{:S(2)}) copy-start(bf16[1,128,1024]{2,1,0:T(8,128)(2,1)} %param.15) | copy-start | bytes 786436
  27.9 19.4 %copy-start.4 = (s32[1,256,1]{1,2,0:T(1,128)S(1)}, s32[1,256,1]{1,2,0:T(1,128)}, u32[]{:S(2)}) copy-start(s32[1,256,1]{1,2,0:T(1,128)} %param.12) | copy-start | bytes 3076
  27.9 63.1 %all-to-all-start.1 = ((bf16[8,8,2,16,1024]{4,3,1,2,0:T(8,128)(2,1)}), bf16[8,8,2,16,1024]{4,3,1,2,0:T(8,128)(2,1)}, u32[]{:S(2)}, u32[]{:S(2)}) async-start(bf16[8,8,2,16,1024]{4,3,1,2,0:T(8,128)(2,1)} %broadcast_in_dim.77), calls=%async_computation.1 | async-start | bytes 8388608 | tf_op jit(solution)/shard_map/all_to_all | solution.py:13
  34.7 51.6 %collective-permute-start.1 = (bf16[128,1024]{1,0:T(8,128)(2,1)S(1)}, bf16[128,1024]{1,0:T(8,128)(2,1)}, u32[]{:S(2)}, u32[]{:S(2)}) collective-permute-start(bf16[128,1024]{1,0:T(8,128)(2,1)S(1)} %bitcast.57), channel_id=1, source_target_pairs={{0,256},{64,320},{128,384},{192,448},{1,257},{65,321},{129,385},{1... | collective-permute-start | bytes 786440 | tf_op jit(solution)/shard_map/ppermute | solution.py:44
  45.4 43.8 %collective-permute-start = (bf16[128,1024]{1,0:T(8,128)(2,1)}, bf16[128,1024]{1,0:T(8,128)(2,1)}, u32[]{:S(2)}, u32[]{:S(2)}) collective-permute-start(bf16[128,1024]{1,0:T(8,128)(2,1)} %bitcast.2), channel_id=1, source_target_pairs={{0,256},{64,320},{128,384},{192,448},{1,257},{65,321},{129,385},{1... | collective-permute-start | bytes 786440 | tf_op jit(solution)/shard_map/ppermute | solution.py:44
  93.6 1.8 copy-start.5
  97.0 1.8 copy-start.2
  97.0 1.8 copy-start.3
  98.8 1.3 copy-start.6
  104.0 45.5 %all-to-all-start.2 = ((bf16[64,8,1024]{2,1,0:T(8,128)(2,1)}), bf16[64,8,1024]{2,1,0:T(8,128)(2,1)}, u32[]{:S(2)}, u32[]{:S(2)}) async-start(bf16[64,8,1024]{2,1,0:T(8,128)(2,1)} %fusion.16), calls=%async_computation.2 | async-start | bytes 2097152 | tf_op jit(solution)/shard_map/all_to_all | solution.py:73
  157.1 41.2 %copy-start.7 = (f32[1,256]{1,0:T(1,128)S(1)}, f32[1,256]{1,0:T(1,128)}, u32[]{:S(2)}) copy-start(f32[1,256]{1,0:T(1,128)} %param.11) | copy-start | bytes 3076

commit v2 on v1

--- a/solution.py
+++ b/solution.py
@@ -42,13 +42,16 @@
     cap = max(8, 2 * tok_dev // experts)
     pairs = [(i, i + half) for i in range(half)]
     keys_far, values_far = lax.ppermute((mem_keys[0], mem_values[0]), "section", pairs)
+    spread = gathered(jnp.stack([q_weight[0], out_weight[0]]), "y")
+    spread, keys_far, values_far = lax.optimization_barrier((spread, keys_far, values_far))
     keys = jnp.concatenate([keys_far, mem_keys[0]], axis=0)
     values = jnp.concatenate([values_far, mem_values[0]], axis=0)
 
-    both = jnp.stack([q_weight[0], out_weight[0]])
-    both = gathered(gathered(both, "y"), ("x", "z"))
-    both = both.transpose(2, 1, 0, 3, 4).reshape(2, width, width)
-    wq, wo = both[0], both[1]
+    wq = gathered(spread[:, 0], ("x", "z"))
+    wq, out_spread = lax.optimization_barrier((wq, spread[:, 1]))
+    wo = gathered(out_spread, ("x", "z"))
+    wq = wq.transpose(1, 0, 2, 3).reshape(width, width)
+    wo = wo.transpose(1, 0, 2, 3).reshape(width, width)
 
     query = jnp.dot(inputs, wq, preferred_element_type=jnp.float32).astype(jnp.bfloat16)
     context = attend_block(query, keys, values, mem_lengths[0, 0])

time: 201 us -> 202 us (level); the launches traced: 200 us -> 198 us
  waiting for transfers between devices: 63.3 us -> 44.9 us
  blocking collectives: 65.5 us -> 82.2 us
    ppermute x2, waiting for transfers between devices: 37.7 us -> 8.47 us  [shards(): lax.ppermute((mem_keys[0], mem_values[0]), 'section', pairs)]
    all_to_all x1, blocking collectives: 24.4 us -> 40.4 us  [gathered(): lax.all_to_all(jnp.broadcast_to(x[None], (peers, *x.shape)), axis, 0, 0,...]
    all_to_all x1 -> x2, waiting for transfers between devices: 0.01 us -> 10 us  [gathered(): lax.all_to_all(jnp.broadcast_to(x[None], (peers, *x.shape)), axis, 0, 0,...]
    all_to_all x1, starting transfers between devices: 19.3 us -> 10.5 us  [shards(): lax.all_to_all(buffer.reshape(experts, cap, width), AXES, split_axis=0, c...]
    all_to_all x1 -> x2, starting transfers between devices: 6.72 us -> 14 us  [gathered(): lax.all_to_all(jnp.broadcast_to(x[None], (peers, *x.shape)), axis, 0, 0,...]
    optimization_barrier x0 -> x3, local copies, waits for them, and re-layouts: none -> 4.73 us  [the longest x2 2.91 us: shards(): lax.optimization_barrier((spread, keys_far, values_far))]
    ppermute x2 -> x0, local copies, waits for them, and re-layouts: 2.91 us -> none  [shards(): lax.ppermute((mem_keys[0], mem_values[0]), 'section', pairs)]
  transfers between devices with their start and end apart: 4 -> 5, of which waited for: 3 -> 4; matrix products, arithmetic and copies ran while one was open for 3% -> 6% of each run, Pallas kernels for 0% -> 0%
where the time goes in v2:
time: 202 us; the launch traced here: 198 us
  blocking collectives  82.2 us (41%)
  waiting for transfers between devices  44.9 us (22%)
  starting transfers between devices  37.4 us (19%)
  local copies, waits for them, and re-layouts  13.5 us (7%)
  matrix products  11.2 us (6%)
  other arithmetic  7.41 us (4%)
    all_to_all x1, blocking collectives, shards(): lax.all_to_all(acts.reshape(experts, cap, -1), AXES, split_axis=0, concat...  41.9 us
    all_to_all x1, blocking collectives, gathered(): lax.all_to_all(jnp.broadcast_to(x[None], (peers, *x.shape)), axis, 0, 0,...  40.4 us
    all_to_all x1, waiting for transfers between devices, shards(): lax.all_to_all(buffer.reshape(experts, cap, width), AXES, split_axis=0, c...  26.4 us
    all_to_all x2, starting transfers between devices, gathered(): lax.all_to_all(jnp.broadcast_to(x[None], (peers, *x.shape)), axis, 0, 0,...  14 us
    ppermute x2, starting transfers between devices, shards(): lax.ppermute((mem_keys[0], mem_values[0]), 'section', pairs)  12.9 us
    all_to_all x1, starting transfers between devices, shards(): lax.all_to_all(buffer.reshape(experts, cap, width), AXES, split_axis=0, c...  10.5 us
    all_to_all x2, waiting for transfers between devices, gathered(): lax.all_to_all(jnp.broadcast_to(x[None], (peers, *x.shape)), axis, 0, 0,...  10 us
    ppermute x2, waiting for transfers between devices, shards(): lax.ppermute((mem_keys[0], mem_values[0]), 'section', pairs)  8.47 us
  transfers between devices with their start and end apart: 5, of which 4 were waited for; matrix products, arithmetic and copies ran while one was open for 6% of the time, Pallas kernels for 0%

profile of v2, /device:TPU:6, one launch (start us, length us, event | category | flops | bytes accessed | tf_op | source)
XLA Modules:
  0.0 198.1 jit_solution(11374324720027643427)
XLA Ops:
  0.0 0.9 pad_maximum_fusion
  0.9 0.9 broadcast_in_dim.82
  1.8 7.1 %all-to-all-start = ((bf16[8,2,16,1024]{3,2,1,0:T(8,128)(2,1)}), bf16[8,2,16,1024]{3,2,1,0:T(8,128)(2,1)S(1)}, u32[]{:S(2)}, u32[]{:S(2)}) async-start(bf16[8,2,16,1024]{3,2,1,0:T(8,128)(2,1)} %broadcast_in_dim.82), calls=%async_computation | async-start | bytes 1048576 | tf_op jit(solution)/shard_map/all_to_all | solution.py:13
  8.9 10.9 %collective-permute-start = (bf16[128,1024]{1,0:T(8,128)(2,1)}, bf16[128,1024]{1,0:T(8,128)(2,1)S(1)}, u32[]{:S(2)}, u32[]{:S(2)}) collective-permute-start(bf16[128,1024]{1,0:T(8,128)(2,1)} %bitcast.61), channel_id=1, source_target_pairs={{0,256},{64,320},{128,384},{192,448},{1,257},{65,321},{129,385},{1... | collective-permute-start | bytes 786440 | tf_op jit(solution)/shard_map/ppermute | solution.py:44
  19.8 2.0 %collective-permute-start.1 = (bf16[128,1024]{1,0:T(8,128)(2,1)}, bf16[128,1024]{1,0:T(8,128)(2,1)}, u32[]{:S(2)}, u32[]{:S(2)}) collective-permute-start(bf16[128,1024]{1,0:T(8,128)(2,1)} %bitcast.62), channel_id=1, source_target_pairs={{0,256},{64,320},{128,384},{192,448},{1,257},{65,321},{129,385},{1... | collective-permute-start | bytes 786440 | tf_op jit(solution)/shard_map/ppermute | solution.py:44
  21.8 5.0 %collective-permute-done = bf16[128,1024]{1,0:T(8,128)(2,1)S(1)} collective-permute-done((bf16[128,1024]{1,0:T(8,128)(2,1)}, bf16[128,1024]{1,0:T(8,128)(2,1)S(1)}, u32[]{:S(2)}, u32[]{:S(2)}) %collective-permute-start) | collective-permute-done | bytes 262176 | tf_op jit(solution)/shard_map/ppermute | solution.py:44
  26.8 0.7 copy-done.2
  27.5 3.4 %collective-permute-done.1 = bf16[128,1024]{1,0:T(8,128)(2,1)} collective-permute-done((bf16[128,1024]{1,0:T(8,128)(2,1)}, bf16[128,1024]{1,0:T(8,128)(2,1)}, u32[]{:S(2)}, u32[]{:S(2)}) %collective-permute-start.1) | collective-permute-done | bytes 262176 | tf_op jit(solution)/shard_map/ppermute | solution.py:44
  31.1 0.3 broadcast_in_dim.85
  31.3 40.4 %all_to_all.25 = bf16[8,8,16,1024]{3,2,1,0:T(8,128)(2,1)} all-to-all(bf16[8,8,16,1024]{3,2,1,0:T(8,128)(2,1)S(1)} %broadcast_in_dim.85), channel_id=1, replica_groups=mesh['section'=8,'y'=8,'x'=4,'z'=2] {'x','z'}, dimensions={0} | all-to-all | bytes 4194304 | tf_op jit(solution)/shard_map/all_to_all | solution.py:13
  71.7 1.6 broadcast_in_dim.87
  73.2 6.9 %all-to-all-start.2 = ((bf16[8,8,16,1024]{3,2,1,0:T(8,128)(2,1)}), bf16[8,8,16,1024]{3,2,1,0:T(8,128)(2,1)}, u32[]{:S(2)}, u32[]{:S(2)}) async-start(bf16[8,8,16,1024]{3,2,1,0:T(8,128)(2,1)} %broadcast_in_dim.87), calls=%async_computation.2 | async-start | bytes 4194304 | tf_op jit(solution)/shard_map/all_to_all | solution.py:13
  80.1 0.2 copy.38
  80.3 1.8 copy.35
  82.7 0.2 convert_reduce_fusion.1
  83.1 1.1 copy.37
  84.2 1.8 copy.34
  86.0 1.8 copy.36
  87.8 0.8 convolution_convert_fusion.1
  88.6 0.8 fusion.24
  89.4 1.7 fusion.40
  91.1 1.3 fusion.18
  92.4 10.0 %all-to-all-done.2 = bf16[8,8,16,1024]{3,2,1,0:T(8,128)(2,1)} async-done(((bf16[8,8,16,1024]{3,2,1,0:T(8,128)(2,1)}), bf16[8,8,16,1024]{3,2,1,0:T(8,128)(2,1)}, u32[]{:S(2)}, u32[]{:S(2)}) %all-to-all-start.2) | async-done | bytes 2097184 | tf_op jit(solution)/shard_map/all_to_all | solution.py:13
  102.5 3.2 %copy.40 = bf16[8,8,16,1024]{3,2,0,1:T(8,128)(2,1)} copy(bf16[8,8,16,1024]{3,2,1,0:T(8,128)(2,1)} %all-to-all-done.2) | data formatting | bytes 4194304 | tf_op jit(solution)/shard_map/all_to_all | solution.py:13
  105.7 3.8 %fusion.16 = bf16[64,8,1024]{2,1,0:T(8,128)(2,1)} fusion(pred[512]{0:T(512)(128)(4,1)S(1)} %fusion.30, bf16[256,1024]{0,1:T(8,128)(2,1)} %bitcast.68, bf16[1024,1024]{1,0:T(8,128)(2,1)} %bitcast.56, bf16[1,256,1024]{2,1,0:T(8,128)(2,1)S(1)} %copy-done.7, pred[]{:T(512)S(6)} %ge.3, s32[256]{0:T(256)S(1)} %multiply_add_fusion), kind=kOutput, calls=%fused_computation.20 | convolution fusion | flops 807534592 | bytes 4195841 | tf_op jit(solution)/shard_map/ts,td->sd/dot_general | solution.py:71
  109.5 10.5 %all-to-all-start.3 = ((bf16[64,8,1024]{2,1,0:T(8,128)(2,1)}), bf16[64,8,1024]{2,1,0:T(8,128)(2,1)}, u32[]{:S(2)}, u32[]{:S(2)}) async-start(bf16[64,8,1024]{2,1,0:T(8,128)(2,1)} %fusion.16), calls=%async_computation.3 | async-start | bytes 2097152 | tf_op jit(solution)/shard_map/all_to_all | solution.py:76
  120.7 26.4 %all-to-all-done.3 = bf16[64,8,1024]{2,1,0:T(8,128)(2,1)} async-done(((bf16[64,8,1024]{2,1,0:T(8,128)(2,1)}), bf16[64,8,1024]{2,1,0:T(8,128)(2,1)}, u32[]{:S(2)}, u32[]{:S(2)}) %all-to-all-start.3) | async-done | bytes 1048608 | tf_op jit(solution)/shard_map/all_to_all | solution.py:76
  147.1 2.1 %convert_reduce_fusion = s32[64]{0:T(128)S(1)} fusion(bf16[64,8,1024]{2,1,0:T(8,128)(2,1)} %all-to-all-done.3), kind=kLoop, calls=%fused_computation.39 | loop fusion | flops 1984 | bytes 1280 | tf_op jit(solution)/shard_map/reduce_sum | solution.py:80
  149.5 2.1 %fusion.35 = pred[64,8]{1,0:T(8,128)(4,1)S(1)} fusion(bf16[64,8,1024]{2,1,0:T(8,128)(2,1)} %all-to-all-done.3), kind=kLoop, calls=%fused_computation.52 | loop fusion | flops 1024 | bytes 1536 | tf_op jit(solution)/shard_map/lt | solution.py:79
  151.7 3.0 %fusion.5 = bf16[64,8,1408]{2,1,0:T(8,128)(2,1)S(1)} fusion(bf16[1,1,1024,1408]{3,2,1,0:T(8,128)(2,1)S(1)} %copy-done, pred[512]{0:T(512)(128)(4,1)S(1)} %and.12, bf16[64,8,1024]{2,1,0:T(8,128)(2,1)} %all-to-all-done.3), kind=kOutput, calls=%fused_computation.10 | convolution fusion | flops 1478557696 | bytes 5374464 | tf_op jit(solution)/shard_map/dot_general | solution.py:88
  154.8 41.9 %all_to_all.26 = bf16[64,8,1408]{2,1,0:T(8,128)(2,1)S(1)} all-to-all(bf16[64,8,1408]{2,1,0:T(8,128)(2,1)S(1)} %fusion.5), channel_id=1, replica_groups=mesh['section'=8,'y'=8,'x'=4,'z'=2] {'y','x','z'}, dimensions={0} | all-to-all | bytes 2883584 | tf_op jit(solution)/shard_map/all_to_all | solution.py:94
  196.6 1.5 fusion.9
  (27 shorter events, 0.7 us)
Async XLA Ops:
  0.0 151.7 %copy-start = (bf16[1,1,1024,1408]{3,2,1,0:T(8,128)(2,1)S(1)}, bf16[1,1,1024,1408]{3,2,1,0:T(8,128)(2,1)}, u32[]{:S(2)}) copy-start(bf16[1,1,1024,1408]{3,2,1,0:T(8,128)(2,1)} %param.19) | copy-start | bytes 8650756
  1.8 29.2 %all-to-all-start = ((bf16[8,2,16,1024]{3,2,1,0:T(8,128)(2,1)}), bf16[8,2,16,1024]{3,2,1,0:T(8,128)(2,1)S(1)}, u32[]{:S(2)}, u32[]{:S(2)}) async-start(bf16[8,2,16,1024]{3,2,1,0:T(8,128)(2,1)} %broadcast_in_dim.82), calls=%async_computation | async-start | bytes 1048576 | tf_op jit(solution)/shard_map/all_to_all | solution.py:13
  8.9 18.0 %collective-permute-start = (bf16[128,1024]{1,0:T(8,128)(2,1)}, bf16[128,1024]{1,0:T(8,128)(2,1)S(1)}, u32[]{:S(2)}, u32[]{:S(2)}) collective-permute-start(bf16[128,1024]{1,0:T(8,128)(2,1)} %bitcast.61), channel_id=1, source_target_pairs={{0,256},{64,320},{128,384},{192,448},{1,257},{65,321},{129,385},{1... | collective-permute-start | bytes 786440 | tf_op jit(solution)/shard_map/ppermute | solution.py:44
  19.8 11.2 %collective-permute-start.1 = (bf16[128,1024]{1,0:T(8,128)(2,1)}, bf16[128,1024]{1,0:T(8,128)(2,1)}, u32[]{:S(2)}, u32[]{:S(2)}) collective-permute-start(bf16[128,1024]{1,0:T(8,128)(2,1)} %bitcast.62), channel_id=1, source_target_pairs={{0,256},{64,320},{128,384},{192,448},{1,257},{65,321},{129,385},{1... | collective-permute-start | bytes 786440 | tf_op jit(solution)/shard_map/ppermute | solution.py:44
  26.8 0.7 copy-start.2
  71.7 8.4 %copy-start.1 = (bf16[1,128,1024]{2,1,0:T(8,128)(2,1)S(1)}, bf16[1,128,1024]{2,1,0:T(8,128)(2,1)}, u32[]{:S(2)}) copy-start(bf16[1,128,1024]{2,1,0:T(8,128)(2,1)} %param.15) | copy-start | bytes 786436
  73.2 9.5 %copy-start.5 = (s32[1,256,1]{1,2,0:T(1,128)S(1)}, s32[1,256,1]{1,2,0:T(1,128)}, u32[]{:S(2)}) copy-start(s32[1,256,1]{1,2,0:T(1,128)} %param.12) | copy-start | bytes 3076
  73.2 29.2 %all-to-all-start.2 = ((bf16[8,8,16,1024]{3,2,1,0:T(8,128)(2,1)}), bf16[8,8,16,1024]{3,2,1,0:T(8,128)(2,1)}, u32[]{:S(2)}, u32[]{:S(2)}) async-start(bf16[8,8,16,1024]{3,2,1,0:T(8,128)(2,1)} %broadcast_in_dim.87), calls=%async_computation.2 | async-start | bytes 4194304 | tf_op jit(solution)/shard_map/all_to_all | solution.py:13
  86.0 1.8 copy-start.6
  89.4 1.7 copy-start.3
  89.4 1.7 copy-start.4
  92.4 13.2 %copy-start.7 = (bf16[1,256,1024]{2,1,0:T(8,128)(2,1)S(1)}, bf16[1,256,1024]{2,1,0:T(8,128)(2,1)}, u32[]{:S(2)}) copy-start(bf16[1,256,1024]{2,1,0:T(8,128)(2,1)} %param.10) | copy-start | bytes 1572868
  109.5 37.6 %all-to-all-start.3 = ((bf16[64,8,1024]{2,1,0:T(8,128)(2,1)}), bf16[64,8,1024]{2,1,0:T(8,128)(2,1)}, u32[]{:S(2)}, u32[]{:S(2)}) async-start(bf16[64,8,1024]{2,1,0:T(8,128)(2,1)} %fusion.16), calls=%async_computation.3 | async-start | bytes 2097152 | tf_op jit(solution)/shard_map/all_to_all | solution.py:76
  154.7 41.9 %copy-start.8 = (f32[1,256]{1,0:T(1,128)S(1)}, f32[1,256]{1,0:T(1,128)}, u32[]{:S(2)}) copy-start(f32[1,256]{1,0:T(1,128)} %param.11) | copy-start | bytes 3076

commit v3 on v2

v3 whole, which is shorter than its diff:
```python
import functools

import jax
import jax.numpy as jnp
from jax import lax
from jax.experimental import pallas as pl
from jax.experimental.pallas import tpu as pltpu
from jax.sharding import Mesh, PartitionSpec as P

HEADS = 16
EMPTY = 1e30
AXES = ("y", "x", "z")
VMEM = pl.BlockSpec(memory_space=pltpu.VMEM)
SMEM = pl.BlockSpec(memory_space=pltpu.SMEM)
PARAMS = pltpu.CompilerParams(vmem_limit_bytes=48 << 20)


def gathered(x, axis):
    peers = lax.axis_size(axis)
    return lax.all_to_all(jnp.broadcast_to(x[None], (peers, *x.shape)), axis, 0, 0, tiled=True)


def attend_block(query, keys, values, length):
    rows = query.shape[0]
    span = keys.shape[0]
    qh = query.reshape(rows, HEADS, -1)
    kh = keys.reshape(span, HEADS, -1)
    vh = values.reshape(span, HEADS, -1)
    scores = jnp.einsum("qhd,khd->hqk", qh, kh, preferred_element_type=jnp.float32) / jnp.sqrt(
        jnp.float32(qh.shape[2])
    )
    valid = jnp.arange(span, dtype=jnp.int32) < length
    scores = jnp.where(valid[None, None, :], scores, jnp.float32(-1e30))
    scores = scores - jnp.max(scores, axis=-1, keepdims=True)
    weights = jnp.exp(scores)
    probs = (weights / jnp.sum(weights, axis=-1, keepdims=True)).astype(jnp.bfloat16)
    context = jnp.einsum("hqk,khd->qhd", probs, vh, preferred_element_type=jnp.float32)
    return context.reshape(rows, -1).astype(jnp.bfloat16)


def mix_kernel(decoding, context, tokens, weight, slot, out):
    many, few, rows, width = weight.shape
    block = many * rows
    total = jnp.zeros((context.shape[0], width), jnp.float32)
    for k in range(few):
        piece = weight[:, k].reshape(block, width)
        total += jnp.dot(
            context[:, k * block : (k + 1) * block], piece, preferred_element_type=jnp.float32
        )
    own = tokens[...]
    added = (own.astype(jnp.float32) + total).astype(jnp.bfloat16)
    mixed = jnp.where(decoding[0] > 0, added, own)
    slots = out.shape[0]
    index = lax.broadcasted_iota(jnp.int32, (slots, own.shape[0]), 0)
    placed = (index == slot[...]).astype(jnp.float32)
    used = jnp.sum(placed, axis=1, keepdims=True) > 0.5
    sent = jnp.dot(placed.astype(jnp.bfloat16), mixed, preferred_element_type=jnp.float32)
    out[...] = jnp.where(used, sent, EMPTY).astype(jnp.bfloat16)


def expert_kernel(capacity, received, weight, out):
    rows = received.shape[0]
    filled = received[:, 0:128].astype(jnp.float32)[:, 0:1] < EMPTY / 2
    later = lax.broadcasted_iota(jnp.int32, (rows, rows), 0)
    sooner = lax.broadcasted_iota(jnp.int32, (rows, rows), 1)
    before = (sooner < later).astype(jnp.float32).astype(jnp.bfloat16)
    ones = jnp.where(jnp.broadcast_to(filled, (rows, 128)), 1.0, 0.0).astype(jnp.bfloat16)
    rank = jnp.dot(before, ones, preferred_element_type=jnp.float32)[:, 0:1]
    kept = filled & (rank < capacity[0].astype(jnp.float32))
    hidden = jnp.dot(received[...], weight[...], preferred_element_type=jnp.float32)
    out[...] = jnp.where(kept, jnp.maximum(hidden, 0.0), 0.0).astype(jnp.bfloat16)


def shards(
    tokens, gates, routes, capacity, mem_lengths, mem_keys, mem_values, q_weight, out_weight, w_in
):
    sections = lax.axis_size("section")
    half = sections // 2
    step = half // 2
    experts = lax.axis_size(AXES)
    inputs = tokens[0]
    tok_dev, width = inputs.shape
    cap = max(8, 2 * tok_dev // experts)

    ahead = functools.partial(lax.ppermute, axis_name="section")
    keys_far = ahead(mem_keys[0], perm=[(s, s + step) for s in range(half)])
    values_far = ahead(mem_values[0], perm=[(s, (s - step) % sections) for s in range(half)])

    spread = gathered(jnp.stack([q_weight[0], out_weight[0]]), "y")
    spread, keys_far, values_far = lax.optimization_barrier((spread, keys_far, values_far))

    keys_far = ahead(keys_far, perm=[(s, s + step) for s in range(step, half + step)])
    turned = [(s - step) % sections for s in range(half)]
    values_far = ahead(values_far, perm=[(s, (s - step) % sections) for s in turned])
    mine = spread[:, 0]
    other = lax.ppermute(mine, "z", [(0, 1), (1, 0)])
    wq_mine = gathered(mine, "x")
    wq_mine, other, keys_far, values_far, out_spread = lax.optimization_barrier(
        (wq_mine, other, keys_far, values_far, spread[:, 1])
    )
    wq_other = gathered(other, "x")
    wq_mine, wq_other, out_spread = lax.optimization_barrier((wq_mine, wq_other, out_spread))
    wo = gathered(out_spread, ("x", "z"))
    low = lax.axis_index("z") == 0
    wq = jnp.stack([jnp.where(low, wq_mine, wq_other), jnp.where(low, wq_other, wq_mine)])
    wq = wq.transpose(2, 1, 0, 3, 4).reshape(width, width)

    keys = jnp.concatenate([keys_far, mem_keys[0]], axis=0)
    values = jnp.concatenate([values_far, mem_values[0]], axis=0)
    query = jnp.dot(inputs, wq, preferred_element_type=jnp.float32).astype(jnp.bfloat16)
    context = attend_block(query, keys, values, mem_lengths[0, 0])

    route = routes[0, :, 0]
    same = route[:, None] == route[None, :]
    earlier = jnp.arange(tok_dev)[None, :] < jnp.arange(tok_dev)[:, None]
    lrank = jnp.sum((same & earlier).astype(jnp.int32), axis=1)
    slot = route * cap + lrank
    decoding = (lax.axis_index("section") >= half).astype(jnp.int32)

    buffer = pl.pallas_call(
        mix_kernel,
        out_shape=jax.ShapeDtypeStruct((experts * cap, width), jnp.bfloat16),
        in_specs=[SMEM, VMEM, VMEM, VMEM, VMEM],
        out_specs=VMEM,
        compiler_params=PARAMS,
        name="mix",
    )(decoding[None], context, inputs, wo, slot[None, :])
    received = lax.all_to_all(
        buffer.reshape(experts, cap, width), AXES, split_axis=0, concat_axis=0, tiled=True
    )
    acts = pl.pallas_call(
        expert_kernel,
        out_shape=jax.ShapeDtypeStruct((experts * cap, w_in.shape[-1]), jnp.bfloat16),
        in_specs=[SMEM, VMEM, VMEM],
        out_specs=VMEM,
        compiler_params=PARAMS,
        name="expert",
    )(capacity[0], received.reshape(experts * cap, width), w_in[0, 0])
    back = lax.all_to_all(
        acts.reshape(experts, cap, -1), AXES, split_axis=0, concat_axis=0, tiled=True
    )
    placing = (slot[:, None] == jnp.arange(experts * cap, dtype=jnp.int32)[None, :]).astype(
        jnp.bfloat16
    )
    picked = jnp.dot(placing, back.reshape(experts * cap, -1), preferred_element_type=jnp.float32)
    result = (picked * gates[0][:, None]).astype(jnp.bfloat16)
    return result[None, :, :]


def solution(mesh):
    sections, experts = mesh.shape["section"], mesh.shape["expert"]
    x, z = 4, 2
    grid = Mesh(
        mesh.devices.reshape(sections, experts // (x * z), x, z), ("section", "y", "x", "z")
    )
    in_specs = (
        P("section", AXES, None),
        P("section", AXES),
        P("section", AXES, None),
        P("section", AXES),
        P("section", AXES),
        P("section", AXES, None),
        P("section", AXES, None),
        P("section", AXES, None),
        P("section", AXES, None),
        P("section", AXES, None, None),
    )
    out_specs = P("section", AXES, None)
    return jax.shard_map(shards, mesh=grid, in_specs=in_specs, out_specs=out_specs, check_vma=False)
```

time: 202 us -> 194 us (0.960); the launches traced: 198 us -> 192 us
  blocking collectives: 82.2 us -> 18 us
  waiting for transfers between devices: 44.9 us -> 97.6 us
  starting transfers between devices: 37.4 us -> 51.1 us
  matrix products: 11.2 us -> 4.31 us
  Pallas kernels: 0 us -> 5.79 us
  local copies, waits for them, and re-layouts: 13.5 us -> 9.15 us
  other arithmetic: 7.41 us -> 4.65 us
    all_to_all x1 -> x0, blocking collectives: 41.9 us -> none  [shards(): lax.all_to_all(acts.reshape(experts, cap, -1), AXES, split_axis=0, concat...]
    all_to_all x0 -> x1, waiting for transfers between devices: none -> 35.3 us  [shards(): lax.all_to_all(acts.reshape(experts, cap, -1), AXES, split_axis=0, concat...]
    all_to_all x1, blocking collectives: 40.4 us -> 18 us  [gathered(): lax.all_to_all(jnp.broadcast_to(x[None], (peers, *x.shape)), axis, 0, 0,...]
    ppermute x2 -> x5, waiting for transfers between devices: 8.47 us -> 23.2 us  [the longest x1 12.7 us: shards(): ahead(mem_values[0], perm=[(s, (s - step) % sections) for s in range(half)])]
    ppermute x2 -> x5, starting transfers between devices: 12.9 us -> 20.3 us  [the longest x1 6.14 us: shards(): ahead(values_far, perm=[(s, (s - step) % sections) for s in turned])]
    dot_general x2 -> x0, matrix products: 6.86 us -> none  [the longest x1 3.84 us: shards(): jnp.einsum('ts,td->sd', placing, mixed, preferred_element_type=jnp.float32)]
    all_to_all x0 -> x1, starting transfers between devices: none -> 6.8 us  [shards(): lax.all_to_all(acts.reshape(experts, cap, -1), AXES, split_axis=0, concat...]
    pallas_call x0 -> x2, Pallas kernels: none -> 5.79 us  [the longest x1 3.15 us: shards(): pl.pallas_call(expert_kernel, out_shape=jax.ShapeDtypeStruct((experts * c...]
  transfers between devices with their start and end apart: 5 -> 10, of which waited for: 4 -> 6; matrix products, arithmetic and copies ran while one was open for 6% -> 5% of each run, Pallas kernels for 0% -> 0%
where the time goes in v3:
time: 194 us; the launch traced here: 192 us
  waiting for transfers between devices  97.6 us (50%)
  starting transfers between devices  51.1 us (26%)
  blocking collectives  18 us (9%)
  local copies, waits for them, and re-layouts  9.15 us (5%)
  Pallas kernels  5.79 us (3%)
  other arithmetic  4.65 us (2%)
  matrix products  4.31 us (2%)
    all_to_all x1, waiting for transfers between devices, shards(): lax.all_to_all(acts.reshape(experts, cap, -1), AXES, split_axis=0, concat...  35.3 us
    all_to_all x1, waiting for transfers between devices, shards(): lax.all_to_all(buffer.reshape(experts, cap, width), AXES, split_axis=0, c...  26.6 us
    all_to_all x1, blocking collectives, gathered(): lax.all_to_all(jnp.broadcast_to(x[None], (peers, *x.shape)), axis, 0, 0,...  18 us
    all_to_all x3, starting transfers between devices, gathered(): lax.all_to_all(jnp.broadcast_to(x[None], (peers, *x.shape)), axis, 0, 0,...  17.5 us
    ppermute x1, waiting for transfers between devices, shards(): ahead(mem_values[0], perm=[(s, (s - step) % sections) for s in range(half)])  12.7 us
    all_to_all x3, waiting for transfers between devices, gathered(): lax.all_to_all(jnp.broadcast_to(x[None], (peers, *x.shape)), axis, 0, 0,...  12.6 us
    ppermute x1, waiting for transfers between devices, shards(): ahead(values_far, perm=[(s, (s - step) % sections) for s in turned])  10.5 us
    all_to_all x1, starting transfers between devices, shards(): lax.all_to_all(acts.reshape(experts, cap, -1), AXES, split_axis=0, concat...  6.8 us
  transfers between devices with their start and end apart: 10, of which 6 were waited for; matrix products, arithmetic and copies ran while one was open for 5% of the time, Pallas kernels for 0%

profile of v3, /device:TPU:6, one launch (start us, length us, event | category | flops | bytes accessed | tf_op | source)
XLA Modules:
  0.0 192.3 jit_solution(8009884785369475084)
XLA Ops:
  0.0 0.8 pad_maximum_fusion.1
  0.8 0.9 broadcast_in_dim.30
  1.6 7.1 %all-to-all-start = ((bf16[8,2,16,1024]{3,2,1,0:T(8,128)(2,1)}), bf16[8,2,16,1024]{3,2,1,0:T(8,128)(2,1)S(1)}, u32[]{:S(2)}, u32[]{:S(2)}) async-start(bf16[8,2,16,1024]{3,2,1,0:T(8,128)(2,1)} %broadcast_in_dim.30), calls=%async_computation | async-start | bytes 1048576 | tf_op jit(solution)/shard_map/all_to_all | solution.py:20
  8.7 6.1 %collective-permute-start = (bf16[128,1024]{1,0:T(8,128)(2,1)}, bf16[128,1024]{1,0:T(8,128)(2,1)S(1)}, u32[]{:S(2)}, u32[]{:S(2)}) collective-permute-start(bf16[128,1024]{1,0:T(8,128)(2,1)} %bitcast.57), channel_id=1, source_target_pairs={{0,128},{64,192},{128,256},{192,320},{1,129},{65,193},{129,257},{1... | collective-permute-start | bytes 786440 | tf_op jit(solution)/shard_map/ppermute | solution.py:86
  14.8 5.5 %collective-permute-start.1 = (bf16[128,1024]{1,0:T(8,128)(2,1)}, bf16[128,1024]{1,0:T(8,128)(2,1)S(1)}, u32[]{:S(2)}, u32[]{:S(2)}) collective-permute-start(bf16[128,1024]{1,0:T(8,128)(2,1)} %bitcast.58), channel_id=1, source_target_pairs={{0,384},{64,448},{128,0},{192,64},{1,385},{65,449},{129,1},{193,65... | collective-permute-start | bytes 786440 | tf_op jit(solution)/shard_map/ppermute | solution.py:87
  20.4 12.7 %collective-permute-done.1 = bf16[128,1024]{1,0:T(8,128)(2,1)S(1)} collective-permute-done((bf16[128,1024]{1,0:T(8,128)(2,1)}, bf16[128,1024]{1,0:T(8,128)(2,1)S(1)}, u32[]{:S(2)}, u32[]{:S(2)}) %collective-permute-start.1) | collective-permute-done | bytes 262176 | tf_op jit(solution)/shard_map/ppermute | solution.py:87
  33.2 1.1 broadcast_in_dim.32
  34.3 4.8 %all-to-all-start.1 = ((bf16[4,8,16,1024]{3,2,1,0:T(8,128)(2,1)}), bf16[4,8,16,1024]{3,2,1,0:T(8,128)(2,1)S(1)}, u32[]{:S(2)}, u32[]{:S(2)}) async-start(bf16[4,8,16,1024]{3,2,1,0:T(8,128)(2,1)} %broadcast_in_dim.32), calls=%async_computation.1 | async-start | bytes 2097152 | tf_op jit(solution)/shard_map/all_to_all | solution.py:20
  39.0 1.9 collective-permute-start.2
  41.0 0.7 collective-permute-start.3
  41.6 6.1 %collective-permute-start.4 = (bf16[128,1024]{1,0:T(8,128)(2,1)S(1)}, bf16[128,1024]{1,0:T(8,128)(2,1)S(1)}, u32[]{:S(2)}, u32[]{:S(2)}) collective-permute-start(bf16[128,1024]{1,0:T(8,128)(2,1)S(1)} %collective-permute-done.1), channel_id=1, source_target_pairs={{384,256},{448,320},{0,384},{64,448},{385,257},{449,321},{1,385},{... | collective-permute-start | bytes 786440 | tf_op jit(solution)/shard_map/ppermute | solution.py:94
  47.8 10.5 %collective-permute-done.4 = bf16[128,1024]{1,0:T(8,128)(2,1)S(1)} collective-permute-done((bf16[128,1024]{1,0:T(8,128)(2,1)S(1)}, bf16[128,1024]{1,0:T(8,128)(2,1)S(1)}, u32[]{:S(2)}, u32[]{:S(2)}) %collective-permute-start.4) | collective-permute-done | bytes 262176 | tf_op jit(solution)/shard_map/ppermute | solution.py:94
  58.4 18.0 %all_to_all.30 = bf16[4,8,16,1024]{3,2,1,0:T(8,128)(2,1)} all-to-all(bf16[4,8,16,1024]{3,2,1,0:T(8,128)(2,1)S(1)} %broadcast_in_dim.59), channel_id=1, replica_groups=mesh['section'=8,'y'=8,'x'=4,'z'=2] {'x'}, dimensions={0} | all-to-all | bytes 2097152 | tf_op jit(solution)/shard_map/all_to_all | solution.py:20
  76.5 1.6 broadcast_in_dim.61
  78.1 5.6 %all-to-all-start.3 = ((bf16[8,8,16,1024]{3,2,1,0:T(8,128)(2,1)}), bf16[8,8,16,1024]{3,2,1,0:T(8,128)(2,1)S(1)}, u32[]{:S(2)}, u32[]{:S(2)}) async-start(bf16[8,8,16,1024]{3,2,1,0:T(8,128)(2,1)} %broadcast_in_dim.61), calls=%async_computation.3 | async-start | bytes 4194304 | tf_op jit(solution)/shard_map/all_to_all | solution.py:20
  83.9 0.8 copy.36
  85.8 1.1 copy.35
  86.9 1.7 select_bitcast_fusion.1
  88.9 0.8 convolution_convert_fusion
  89.7 0.8 fusion.13
  90.4 1.7 fusion.24
  92.2 1.3 fusion.9
  93.5 1.2 copy.45.context
  94.7 12.6 %all-to-all-done.3.weight = bf16[8,8,16,1024]{3,2,1,0:T(8,128)(2,1)S(1)} async-done(((bf16[8,8,16,1024]{3,2,1,0:T(8,128)(2,1)}), bf16[8,8,16,1024]{3,2,1,0:T(8,128)(2,1)S(1)}, u32[]{:S(2)}, u32[]{:S(2)}) %all-to-all-start.3) | async-done | bytes 2097184 | tf_op jit(solution)/shard_map/all_to_all | solution.py:20
  107.3 2.6 %mix.1 = bf16[512,1024]{1,0:T(8,128)(2,1)} custom-call(s32[1]{0:T(128)} %bitcast.2.decoding, bf16[256,1024]{1,0:T(8,128)(2,1)S(1)} %copy.45.context, bf16[256,1024]{1,0:T(8,128)(2,1)S(1)} %bitcast.51, bf16[8,8,16,1024]{3,2,1,0:T(8,128)(2,1)S(1)} %all-to-all-done.3.weight, s32[1,256]{1,0:T(1,128)S(1)} %bitcast_add_fusion.slot), custom_call_target="tpu_custom_call" | custom-call | tf_op jit(solution)/shard_map/mix/pallas_call | solution.py:120
  109.9 6.5 %all-to-all-start.4 = ((bf16[64,8,1024]{2,1,0:T(8,128)(2,1)}), bf16[64,8,1024]{2,1,0:T(8,128)(2,1)S(1)}, u32[]{:S(2)}, u32[]{:S(2)}) async-start(bf16[64,8,1024]{2,1,0:T(8,128)(2,1)} %bitcast.24), calls=%async_computation.4 | async-start | bytes 2097152 | tf_op jit(solution)/shard_map/all_to_all | solution.py:128
  117.1 26.6 %all-to-all-done.4 = bf16[64,8,1024]{2,1,0:T(8,128)(2,1)S(1)} async-done(((bf16[64,8,1024]{2,1,0:T(8,128)(2,1)}), bf16[64,8,1024]{2,1,0:T(8,128)(2,1)S(1)}, u32[]{:S(2)}, u32[]{:S(2)}) %all-to-all-start.4) | async-done | bytes 1048608 | tf_op jit(solution)/shard_map/all_to_all | solution.py:128
  143.7 1.8 copy-done
  145.5 3.1 %expert.1 = bf16[512,1408]{1,0:T(8,128)(2,1)} custom-call(s32[1]{0:T(128)} %bitcast.47.capacity, bf16[512,1024]{1,0:T(8,128)(2,1)S(1)} %bitcast.49, bf16[1024,1408]{1,0:T(8,128)(2,1)S(1)} %bitcast.50), custom_call_target="tpu_custom_call" | custom-call | tf_op jit(solution)/shard_map/expert/pallas_call | solution.py:131
  148.7 6.8 %all-to-all-start.5 = ((bf16[64,8,1408]{2,1,0:T(8,128)(2,1)}), bf16[64,8,1408]{2,1,0:T(8,128)(2,1)S(1)}, u32[]{:S(2)}, u32[]{:S(2)}) async-start(bf16[64,8,1408]{2,1,0:T(8,128)(2,1)} %bitcast.27), calls=%async_computation.5 | async-start | bytes 2883584 | tf_op jit(solution)/shard_map/all_to_all | solution.py:139
  155.5 35.3 %all-to-all-done.5 = bf16[64,8,1408]{2,1,0:T(8,128)(2,1)S(1)} async-done(((bf16[64,8,1408]{2,1,0:T(8,128)(2,1)}), bf16[64,8,1408]{2,1,0:T(8,128)(2,1)S(1)}, u32[]{:S(2)}, u32[]{:S(2)}) %all-to-all-start.5) | async-done | bytes 1441824 | tf_op jit(solution)/shard_map/all_to_all | solution.py:139
  190.8 1.5 fusion.3
  (31 shorter events, 1.0 us)
Async XLA Ops:
  1.6 31.5 %all-to-all-start = ((bf16[8,2,16,1024]{3,2,1,0:T(8,128)(2,1)}), bf16[8,2,16,1024]{3,2,1,0:T(8,128)(2,1)S(1)}, u32[]{:S(2)}, u32[]{:S(2)}) async-start(bf16[8,2,16,1024]{3,2,1,0:T(8,128)(2,1)} %broadcast_in_dim.30), calls=%async_computation | async-start | bytes 1048576 | tf_op jit(solution)/shard_map/all_to_all | solution.py:20
  8.7 11.7 %collective-permute-start = (bf16[128,1024]{1,0:T(8,128)(2,1)}, bf16[128,1024]{1,0:T(8,128)(2,1)S(1)}, u32[]{:S(2)}, u32[]{:S(2)}) collective-permute-start(bf16[128,1024]{1,0:T(8,128)(2,1)} %bitcast.57), channel_id=1, source_target_pairs={{0,128},{64,192},{128,256},{192,320},{1,129},{65,193},{129,257},{1... | collective-permute-start | bytes 786440 | tf_op jit(solution)/shard_map/ppermute | solution.py:86
  14.8 18.3 %collective-permute-start.1 = (bf16[128,1024]{1,0:T(8,128)(2,1)}, bf16[128,1024]{1,0:T(8,128)(2,1)S(1)}, u32[]{:S(2)}, u32[]{:S(2)}) collective-permute-start(bf16[128,1024]{1,0:T(8,128)(2,1)} %bitcast.58), channel_id=1, source_target_pairs={{0,384},{64,448},{128,0},{192,64},{1,385},{65,449},{129,1},{193,65... | collective-permute-start | bytes 786440 | tf_op jit(solution)/shard_map/ppermute | solution.py:87
  34.3 24.0 %all-to-all-start.1 = ((bf16[4,8,16,1024]{3,2,1,0:T(8,128)(2,1)}), bf16[4,8,16,1024]{3,2,1,0:T(8,128)(2,1)S(1)}, u32[]{:S(2)}, u32[]{:S(2)}) async-start(bf16[4,8,16,1024]{3,2,1,0:T(8,128)(2,1)} %broadcast_in_dim.32), calls=%async_computation.1 | async-start | bytes 2097152 | tf_op jit(solution)/shard_map/all_to_all | solution.py:20
  39.0 8.8 %collective-permute-start.2 = (bf16[8,16,1024]{2,1,0:T(8,128)(2,1)S(1)}, bf16[8,16,1024]{2,1,0:T(8,128)(2,1)S(1)}, u32[]{:S(2)}, u32[]{:S(2)}) collective-permute-start(bf16[8,16,1024]{2,1,0:T(8,128)(2,1)S(1)} %get-tuple-element.30), channel_id=1, source_target_pairs={{0,1},{1,0},{2,3},{3,2},{4,5},{5,4},{6,7},{7,6},{8,9},{9,8},{10,11... | collective-permute-start | bytes 786440 | tf_op jit(solution)/shard_map/ppermute | solution.py:96
  41.0 6.9 %collective-permute-start.3 = (bf16[128,1024]{1,0:T(8,128)(2,1)S(1)}, bf16[128,1024]{1,0:T(8,128)(2,1)S(1)}, u32[]{:S(2)}, u32[]{:S(2)}) collective-permute-start(bf16[128,1024]{1,0:T(8,128)(2,1)S(1)} %collective-permute-done), channel_id=1, source_target_pairs={{128,256},{192,320},{256,384},{320,448},{129,257},{193,321},{257,3... | collective-permute-start | bytes 786440 | tf_op jit(solution)/shard_map/ppermute | solution.py:92
  41.6 16.6 %collective-permute-start.4 = (bf16[128,1024]{1,0:T(8,128)(2,1)S(1)}, bf16[128,1024]{1,0:T(8,128)(2,1)S(1)}, u32[]{:S(2)}, u32[]{:S(2)}) collective-permute-start(bf16[128,1024]{1,0:T(8,128)(2,1)S(1)} %collective-permute-done.1), channel_id=1, source_target_pairs={{384,256},{448,320},{0,384},{64,448},{385,257},{449,321},{1,385},{... | collective-permute-start | bytes 786440 | tf_op jit(solution)/shard_map/ppermute | solution.py:94
  58.3 19.8 %copy-start.5 = (bf16[128,1024]{1,0:T(8,128)(2,1)}, bf16[128,1024]{1,0:T(8,128)(2,1)S(1)}, u32[]{:S(2)}) copy-start(bf16[128,1024]{1,0:T(8,128)(2,1)S(1)} %collective-permute-done.4) | copy-start | bytes 786436
  58.3 19.8 %copy-start.2 = (bf16[4,8,16,1024]{3,2,1,0:T(8,128)(2,1)}, bf16[4,8,16,1024]{3,2,1,0:T(8,128)(2,1)S(1)}, u32[]{:S(2)}) copy-start(bf16[4,8,16,1024]{3,2,1,0:T(8,128)(2,1)S(1)} %all-to-all-done.1) | copy-start | bytes 3145732
  58.4 25.3 %copy-start.3 = (bf16[1,128,1024]{2,1,0:T(8,128)(2,1)S(1)}, bf16[1,128,1024]{2,1,0:T(8,128)(2,1)}, u32[]{:S(2)}) copy-start(bf16[1,128,1024]{2,1,0:T(8,128)(2,1)} %param.15) | copy-start | bytes 786436
  58.4 25.5 %copy-start.4 = (bf16[1,128,1024]{2,1,0:T(8,128)(2,1)S(1)}, bf16[1,128,1024]{2,1,0:T(8,128)(2,1)}, u32[]{:S(2)}) copy-start(bf16[1,128,1024]{2,1,0:T(8,128)(2,1)} %param.16) | copy-start | bytes 786436
  76.5 8.9 %copy-start.7 = (s32[1,256,1]{1,2,0:T(1,128)S(1)}, s32[1,256,1]{1,2,0:T(1,128)}, u32[]{:S(2)}) copy-start(s32[1,256,1]{1,2,0:T(1,128)} %param.12) | copy-start | bytes 3076
  78.1 29.2 %all-to-all-start.3 = ((bf16[8,8,16,1024]{3,2,1,0:T(8,128)(2,1)}), bf16[8,8,16,1024]{3,2,1,0:T(8,128)(2,1)S(1)}, u32[]{:S(2)}, u32[]{:S(2)}) async-start(bf16[8,8,16,1024]{3,2,1,0:T(8,128)(2,1)} %broadcast_in_dim.61), calls=%async_computation.3 | async-start | bytes 4194304 | tf_op jit(solution)/shard_map/all_to_all | solution.py:20
  86.9 2.0 %copy-start.1 = (bf16[1,256,1024]{2,1,0:T(8,128)(2,1)S(1)}, bf16[1,256,1024]{2,1,0:T(8,128)(2,1)}, u32[]{:S(2)}) copy-start(bf16[1,256,1024]{2,1,0:T(8,128)(2,1)} %param.10) | copy-start | bytes 1572868
  90.4 1.7 copy-start.6
  109.9 33.8 %all-to-all-start.4 = ((bf16[64,8,1024]{2,1,0:T(8,128)(2,1)}), bf16[64,8,1024]{2,1,0:T(8,128)(2,1)S(1)}, u32[]{:S(2)}, u32[]{:S(2)}) async-start(bf16[64,8,1024]{2,1,0:T(8,128)(2,1)} %bitcast.24), calls=%async_computation.4 | async-start | bytes 2097152 | tf_op jit(solution)/shard_map/all_to_all | solution.py:128
  116.5 74.3 %copy-start.8 = (f32[1,256]{1,0:T(1,128)S(1)}, f32[1,256]{1,0:T(1,128)}, u32[]{:S(2)}) copy-start(f32[1,256]{1,0:T(1,128)} %param.11) | copy-start | bytes 3076
  143.7 1.8 copy-start
  148.7 42.1 %all-to-all-start.5 = ((bf16[64,8,1408]{2,1,0:T(8,128)(2,1)}), bf16[64,8,1408]{2,1,0:T(8,128)(2,1)S(1)}, u32[]{:S(2)}, u32[]{:S(2)}) async-start(bf16[64,8,1408]{2,1,0:T(8,128)(2,1)} %bitcast.27), calls=%async_computation.5 | async-start | bytes 2883584 | tf_op jit(solution)/shard_map/all_to_all | solution.py:139

commit v4 on v3

--- a/solution.py
+++ b/solution.py
@@ -58,8 +58,15 @@
     out[...] = jnp.where(used, sent, EMPTY).astype(jnp.bfloat16)
 
 
-def expert_kernel(capacity, received, weight, out):
+def expert_kernel(capacity, received, weight, out, held, sems):
     rows = received.shape[0]
+    units = weight.shape[1]
+    cuts = [0, units // 256 * 128, units]
+    copies = []
+    for k in range(2):
+        part = slice(cuts[k], cuts[k + 1])
+        copies.append(pltpu.make_async_copy(weight.at[:, part], held.at[:, part], sems.at[k]))
+        copies[k].start()
     filled = received[:, 0:128].astype(jnp.float32)[:, 0:1] < EMPTY / 2
     later = lax.broadcasted_iota(jnp.int32, (rows, rows), 0)
     sooner = lax.broadcasted_iota(jnp.int32, (rows, rows), 1)
@@ -67,8 +74,11 @@
     ones = jnp.where(jnp.broadcast_to(filled, (rows, 128)), 1.0, 0.0).astype(jnp.bfloat16)
     rank = jnp.dot(before, ones, preferred_element_type=jnp.float32)[:, 0:1]
     kept = filled & (rank < capacity[0].astype(jnp.float32))
-    hidden = jnp.dot(received[...], weight[...], preferred_element_type=jnp.float32)
-    out[...] = jnp.where(kept, jnp.maximum(hidden, 0.0), 0.0).astype(jnp.bfloat16)
+    for k in range(2):
+        part = slice(cuts[k], cuts[k + 1])
+        copies[k].wait()
+        hidden = jnp.dot(received[...], held[:, part], preferred_element_type=jnp.float32)
+        out[:, part] = jnp.where(kept, jnp.maximum(hidden, 0.0), 0.0).astype(jnp.bfloat16)
 
 
 def shards(
@@ -82,28 +92,23 @@
     tok_dev, width = inputs.shape
     cap = max(8, 2 * tok_dev // experts)
 
-    ahead = functools.partial(lax.ppermute, axis_name="section")
-    keys_far = ahead(mem_keys[0], perm=[(s, s + step) for s in range(half)])
-    values_far = ahead(mem_values[0], perm=[(s, (s - step) % sections) for s in range(half)])
+    sides = lax.axis_size("z")
+    over = [
+        (s * sides + z, (s + half) * sides + (z + 1) % sides)
+        for s in range(half)
+        for z in range(sides)
+    ]
+    beside = [(z, (z + 1) % sides) for z in range(sides)]
+    keys_far, values_far = lax.ppermute((mem_keys[0], mem_values[0]), ("section", "z"), over)
 
     spread = gathered(jnp.stack([q_weight[0], out_weight[0]]), "y")
-    spread, keys_far, values_far = lax.optimization_barrier((spread, keys_far, values_far))
-
-    keys_far = ahead(keys_far, perm=[(s, s + step) for s in range(step, half + step)])
-    turned = [(s - step) % sections for s in range(half)]
-    values_far = ahead(values_far, perm=[(s, (s - step) % sections) for s in turned])
-    mine = spread[:, 0]
-    other = lax.ppermute(mine, "z", [(0, 1), (1, 0)])
-    wq_mine = gathered(mine, "x")
-    wq_mine, other, keys_far, values_far, out_spread = lax.optimization_barrier(
-        (wq_mine, other, keys_far, values_far, spread[:, 1])
+    wq = gathered(spread[:, 0], ("x", "z"))
+    wq, keys_far, values_far, out_spread = lax.optimization_barrier(
+        (wq, keys_far, values_far, spread[:, 1])
     )
-    wq_other = gathered(other, "x")
-    wq_mine, wq_other, out_spread = lax.optimization_barrier((wq_mine, wq_other, out_spread))
     wo = gathered(out_spread, ("x", "z"))
-    low = lax.axis_index("z") == 0
-    wq = jnp.stack([jnp.where(low, wq_mine, wq_other), jnp.where(low, wq_other, wq_mine)])
-    wq = wq.transpose(2, 1, 0, 3, 4).reshape(width, width)
+    keys_far, values_far = lax.ppermute((keys_far, values_far), "z", beside)
+    wq = wq.transpose(1, 0, 2, 3).reshape(width, width)
 
     keys = jnp.concatenate([keys_far, mem_keys[0]], axis=0)
     values = jnp.concatenate([values_far, mem_values[0]], axis=0)
@@ -131,8 +136,12 @@
     acts = pl.pallas_call(
         expert_kernel,
         out_shape=jax.ShapeDtypeStruct((experts * cap, w_in.shape[-1]), jnp.bfloat16),
-        in_specs=[SMEM, VMEM, VMEM],
+        in_specs=[SMEM, VMEM, pl.BlockSpec(memory_space=pltpu.HBM)],
         out_specs=VMEM,
+        scratch_shapes=[
+            pltpu.VMEM(w_in.shape[2:], jnp.bfloat16),
+            pltpu.SemaphoreType.DMA((2,)),
+        ],
         compiler_params=PARAMS,
         name="expert",
     )(capacity[0], received.reshape(experts * cap, width), w_in[0, 0])

time: 194 us -> 202 us (1.041)
  blocking collectives: 18 us -> 24.5 us
  starting transfers between devices: 51.1 us -> 45.5 us
  local copies, waits for them, and re-layouts: 9.15 us -> 12.5 us
  waiting for transfers between devices: 97.6 us -> 100 us
    ppermute x5 -> x4, waiting for transfers between devices: 23.2 us -> 38.3 us  [the longest x2 20.3 us: shards(): keys_far, values_far = lax.ppermute((keys_far, values_far), 'z', beside)]
    all_to_all x3 -> x2, waiting for transfers between devices: 12.6 us -> 3.76 us  [gathered(): lax.all_to_all(jnp.broadcast_to(x[None], (peers, *x.shape)), axis, 0, 0,...]
    all_to_all x1, blocking collectives: 18 us -> 24.5 us  [gathered(): lax.all_to_all(jnp.broadcast_to(x[None], (peers, *x.shape)), axis, 0, 0,...]
    all_to_all x3 -> x2, starting transfers between devices: 17.5 us -> 12.6 us  [gathered(): lax.all_to_all(jnp.broadcast_to(x[None], (peers, *x.shape)), axis, 0, 0,...]
    ppermute x5 -> x4, starting transfers between devices: 20.3 us -> 18 us  [the longest x2 12.2 us: shards(): lax.ppermute((mem_keys[0], mem_values[0]), ('section', 'z'), over)]
    unnamed x20 -> x24, local copies, waits for them, and re-layouts: 2.87 us -> 4.2 us
  transfers between devices with their start and end apart: 10 -> 8, of which waited for: 6 -> 7; matrix products, arithmetic and copies ran while one was open for 5% -> 6% of each run, Pallas kernels for 0% -> 0%
where the time goes in v4:
time: 202 us; the launch traced here: 200 us
  waiting for transfers between devices  100 us (50%)
  starting transfers between devices  45.5 us (23%)
  blocking collectives  24.5 us (12%)
  local copies, waits for them, and re-layouts  12.5 us (6%)
  Pallas kernels  6.85 us (3%)
  matrix products  6.16 us (3%)
  other arithmetic  2.7 us (1%)
    all_to_all x1, waiting for transfers between devices, shards(): lax.all_to_all(acts.reshape(experts, cap, -1), AXES, split_axis=0, concat...  33.4 us
    all_to_all x1, waiting for transfers between devices, shards(): lax.all_to_all(buffer.reshape(experts, cap, width), AXES, split_axis=0, c...  24.8 us
    all_to_all x1, blocking collectives, gathered(): lax.all_to_all(jnp.broadcast_to(x[None], (peers, *x.shape)), axis, 0, 0,...  24.5 us
    ppermute x2, waiting for transfers between devices, shards(): keys_far, values_far = lax.ppermute((keys_far, values_far), 'z', beside)  20.3 us
    ppermute x2, waiting for transfers between devices, shards(): lax.ppermute((mem_keys[0], mem_values[0]), ('section', 'z'), over)  18.1 us
    all_to_all x2, starting transfers between devices, gathered(): lax.all_to_all(jnp.broadcast_to(x[None], (peers, *x.shape)), axis, 0, 0,...  12.6 us
    ppermute x2, starting transfers between devices, shards(): lax.ppermute((mem_keys[0], mem_values[0]), ('section', 'z'), over)  12.2 us
    all_to_all x1, starting transfers between devices, shards(): lax.all_to_all(buffer.reshape(experts, cap, width), AXES, split_axis=0, c...  8.09 us
  transfers between devices with their start and end apart: 8, of which 7 were waited for; matrix products, arithmetic and copies ran while one was open for 6% of the time, Pallas kernels for 0%

profile of v4, /device:TPU:6, one launch (start us, length us, event | category | flops | bytes accessed | tf_op | source)
XLA Modules:
  0.0 200.1 jit_solution(12912943406500763659)
XLA Ops:
  0.9 24.5 %all_to_all.25 = bf16[8,2,16,1024]{3,2,1,0:T(8,128)(2,1)S(1)} all-to-all(bf16[8,2,16,1024]{3,2,1,0:T(8,128)(2,1)S(1)} %broadcast_in_dim.28), channel_id=1, replica_groups=mesh['section'=8,'y'=8,'x'=4,'z'=2] {'y'}, dimensions={0} | all-to-all | bytes 1048576 | tf_op jit(solution)/shard_map/all_to_all | solution.py:20
  25.4 1.6 broadcast_in_dim.51
  27.0 6.6 %all-to-all-start.1 = ((bf16[8,8,16,1024]{3,2,1,0:T(8,128)(2,1)}), bf16[8,8,16,1024]{3,2,1,0:T(8,128)(2,1)S(1)}, u32[]{:S(2)}, u32[]{:S(2)}) async-start(bf16[8,8,16,1024]{3,2,1,0:T(8,128)(2,1)} %broadcast_in_dim.51), calls=%async_computation.1 | async-start | bytes 4194304 | tf_op jit(solution)/shard_map/all_to_all | solution.py:20
  33.6 10.2 %collective-permute-start = (bf16[128,1024]{1,0:T(8,128)(2,1)S(1)}, bf16[128,1024]{1,0:T(8,128)(2,1)S(1)}, u32[]{:S(2)}, u32[]{:S(2)}) collective-permute-start(bf16[128,1024]{1,0:T(8,128)(2,1)S(1)} %bitcast.51), channel_id=1, source_target_pairs={{0,257},{1,256},{64,321},{65,320},{128,385},{129,384},{192,449},{1... | collective-permute-start | bytes 786440 | tf_op jit(solution)/shard_map/ppermute | solution.py:102
  43.8 2.0 collective-permute-start.1
  45.8 14.4 %collective-permute-done = bf16[128,1024]{1,0:T(8,128)(2,1)S(1)} collective-permute-done((bf16[128,1024]{1,0:T(8,128)(2,1)S(1)}, bf16[128,1024]{1,0:T(8,128)(2,1)S(1)}, u32[]{:S(2)}, u32[]{:S(2)}) %collective-permute-start) | collective-permute-done | bytes 262176 | tf_op jit(solution)/shard_map/ppermute | solution.py:102
  60.2 3.6 %collective-permute-done.1 = bf16[128,1024]{1,0:T(8,128)(2,1)} collective-permute-done((bf16[128,1024]{1,0:T(8,128)(2,1)S(1)}, bf16[128,1024]{1,0:T(8,128)(2,1)}, u32[]{:S(2)}, u32[]{:S(2)}) %collective-permute-start.1) | collective-permute-done | bytes 262176 | tf_op jit(solution)/shard_map/ppermute | solution.py:102
  63.9 3.8 %all-to-all-done.1 = bf16[8,8,16,1024]{3,2,1,0:T(8,128)(2,1)S(1)} async-done(((bf16[8,8,16,1024]{3,2,1,0:T(8,128)(2,1)}), bf16[8,8,16,1024]{3,2,1,0:T(8,128)(2,1)S(1)}, u32[]{:S(2)}, u32[]{:S(2)}) %all-to-all-start.1) | async-done | bytes 2097184 | tf_op jit(solution)/shard_map/all_to_all | solution.py:20
  67.6 1.3 copy-done.2
  69.0 1.6 broadcast_in_dim.54
  70.6 6.0 %all-to-all-start.2 = ((bf16[8,8,16,1024]{3,2,1,0:T(8,128)(2,1)}), bf16[8,8,16,1024]{3,2,1,0:T(8,128)(2,1)S(1)}, u32[]{:S(2)}, u32[]{:S(2)}) async-start(bf16[8,8,16,1024]{3,2,1,0:T(8,128)(2,1)} %broadcast_in_dim.54), calls=%async_computation.2 | async-start | bytes 4194304 | tf_op jit(solution)/shard_map/all_to_all | solution.py:20
  76.8 0.8 copy.31
  78.5 1.8 copy.32
  80.3 3.4 %collective-permute-start.3 = (bf16[128,1024]{1,0:T(8,128)(2,1)S(1)}, bf16[128,1024]{1,0:T(8,128)(2,1)}, u32[]{:S(2)}, u32[]{:S(2)}) collective-permute-start(bf16[128,1024]{1,0:T(8,128)(2,1)S(1)} %copy-done.9), channel_id=1, source_target_pairs={{0,1},{1,0},{2,3},{3,2},{4,5},{5,4},{6,7},{7,6},{8,9},{9,8},{10,11... | collective-permute-start | bytes 786440 | tf_op jit(solution)/shard_map/ppermute | solution.py:110
  83.7 2.5 %collective-permute-start.2 = (bf16[128,1024]{1,0:T(8,128)(2,1)}, bf16[128,1024]{1,0:T(8,128)(2,1)S(1)}, u32[]{:S(2)}, u32[]{:S(2)}) collective-permute-start(bf16[128,1024]{1,0:T(8,128)(2,1)} %collective-permute-done.1), channel_id=1, source_target_pairs={{0,1},{1,0},{2,3},{3,2},{4,5},{5,4},{6,7},{7,6},{8,9},{9,8},{10,11... | collective-permute-start | bytes 786440 | tf_op jit(solution)/shard_map/ppermute | solution.py:110
  86.2 1.6 convolution_convert_fusion
  87.8 18.7 %collective-permute-done.3 = bf16[128,1024]{1,0:T(8,128)(2,1)} collective-permute-done((bf16[128,1024]{1,0:T(8,128)(2,1)S(1)}, bf16[128,1024]{1,0:T(8,128)(2,1)}, u32[]{:S(2)}, u32[]{:S(2)}) %collective-permute-start.3) | collective-permute-done | bytes 262176 | tf_op jit(solution)/shard_map/ppermute | solution.py:110
  106.4 1.1 copy.33
  107.6 1.6 collective-permute-done.2
  109.2 0.9 copy.30
  110.0 1.8 fusion.13
  111.8 1.7 fusion.24
  113.6 1.3 fusion.9
  114.9 1.2 copy.36.context
  116.1 2.6 %mix.1 = bf16[512,1024]{1,0:T(8,128)(2,1)} custom-call(s32[1]{0:T(128)} %bitcast.2.decoding, bf16[256,1024]{1,0:T(8,128)(2,1)S(1)} %copy.36.context, bf16[256,1024]{1,0:T(8,128)(2,1)S(1)} %bitcast.45, bf16[8,8,16,1024]{3,2,1,0:T(8,128)(2,1)S(1)} %all-to-all-done.2.weight, s32[1,256]{1,0:T(1,128)S(1)} %bitcast_add_fusion.slot), custom_call_target="tpu_custom_call" | custom-call | tf_op jit(solution)/shard_map/mix/pallas_call | solution.py:125
  118.8 8.1 %all-to-all-start.3 = ((bf16[64,8,1024]{2,1,0:T(8,128)(2,1)}), bf16[64,8,1024]{2,1,0:T(8,128)(2,1)S(1)}, u32[]{:S(2)}, u32[]{:S(2)}) async-start(bf16[64,8,1024]{2,1,0:T(8,128)(2,1)} %bitcast.21), calls=%async_computation.3 | async-start | bytes 2097152 | tf_op jit(solution)/shard_map/all_to_all | solution.py:133
  127.5 24.8 %all-to-all-done.3 = bf16[64,8,1024]{2,1,0:T(8,128)(2,1)S(1)} async-done(((bf16[64,8,1024]{2,1,0:T(8,128)(2,1)}), bf16[64,8,1024]{2,1,0:T(8,128)(2,1)S(1)}, u32[]{:S(2)}, u32[]{:S(2)}) %all-to-all-start.3) | async-done | bytes 1048608 | tf_op jit(solution)/shard_map/all_to_all | solution.py:133
  152.4 1.8 copy-done
  154.2 4.2 %expert.1 = bf16[512,1408]{1,0:T(8,128)(2,1)} custom-call(s32[1]{0:T(128)} %bitcast.41.capacity, bf16[512,1024]{1,0:T(8,128)(2,1)S(1)} %bitcast.43, bf16[1024,1408]{1,0:T(8,128)(2,1)S(1)} %bitcast.44), custom_call_target="tpu_custom_call" | custom-call | tf_op jit(solution)/shard_map/expert/pallas_call | solution.py:136
  158.4 6.8 %all-to-all-start.4 = ((bf16[64,8,1408]{2,1,0:T(8,128)(2,1)}), bf16[64,8,1408]{2,1,0:T(8,128)(2,1)S(1)}, u32[]{:S(2)}, u32[]{:S(2)}) async-start(bf16[64,8,1408]{2,1,0:T(8,128)(2,1)} %bitcast.24), calls=%async_computation.4 | async-start | bytes 2883584 | tf_op jit(solution)/shard_map/all_to_all | solution.py:148
  165.3 33.4 %all-to-all-done.4 = bf16[64,8,1408]{2,1,0:T(8,128)(2,1)S(1)} async-done(((bf16[64,8,1408]{2,1,0:T(8,128)(2,1)}), bf16[64,8,1408]{2,1,0:T(8,128)(2,1)S(1)}, u32[]{:S(2)}, u32[]{:S(2)}) %all-to-all-start.4) | async-done | bytes 1441824 | tf_op jit(solution)/shard_map/all_to_all | solution.py:148
  198.6 1.5 fusion.3
  (29 shorter events, 1.3 us)
Async XLA Ops:
  0.8 32.8 %copy-start.3 = (bf16[1,128,1024]{2,1,0:T(8,128)(2,1)S(1)}, bf16[1,128,1024]{2,1,0:T(8,128)(2,1)}, u32[]{:S(2)}) copy-start(bf16[1,128,1024]{2,1,0:T(8,128)(2,1)} %param.15) | copy-start | bytes 786436
  0.9 42.9 %copy-start.4 = (bf16[1,128,1024]{2,1,0:T(8,128)(2,1)S(1)}, bf16[1,128,1024]{2,1,0:T(8,128)(2,1)}, u32[]{:S(2)}) copy-start(bf16[1,128,1024]{2,1,0:T(8,128)(2,1)} %param.16) | copy-start | bytes 786436
  27.0 40.6 %all-to-all-start.1 = ((bf16[8,8,16,1024]{3,2,1,0:T(8,128)(2,1)}), bf16[8,8,16,1024]{3,2,1,0:T(8,128)(2,1)S(1)}, u32[]{:S(2)}, u32[]{:S(2)}) async-start(bf16[8,8,16,1024]{3,2,1,0:T(8,128)(2,1)} %broadcast_in_dim.51), calls=%async_computation.1 | async-start | bytes 4194304 | tf_op jit(solution)/shard_map/all_to_all | solution.py:20
  33.6 44.7 %copy-start.7 = (s32[1,256,1]{1,2,0:T(1,128)S(1)}, s32[1,256,1]{1,2,0:T(1,128)}, u32[]{:S(2)}) copy-start(s32[1,256,1]{1,2,0:T(1,128)} %param.12) | copy-start | bytes 3076
  33.6 26.6 %collective-permute-start = (bf16[128,1024]{1,0:T(8,128)(2,1)S(1)}, bf16[128,1024]{1,0:T(8,128)(2,1)S(1)}, u32[]{:S(2)}, u32[]{:S(2)}) collective-permute-start(bf16[128,1024]{1,0:T(8,128)(2,1)S(1)} %bitcast.51), channel_id=1, source_target_pairs={{0,257},{1,256},{64,321},{65,320},{128,385},{129,384},{192,449},{1... | collective-permute-start | bytes 786440 | tf_op jit(solution)/shard_map/ppermute | solution.py:102
  43.8 20.1 %collective-permute-start.1 = (bf16[128,1024]{1,0:T(8,128)(2,1)S(1)}, bf16[128,1024]{1,0:T(8,128)(2,1)}, u32[]{:S(2)}, u32[]{:S(2)}) collective-permute-start(bf16[128,1024]{1,0:T(8,128)(2,1)S(1)} %bitcast.52), channel_id=1, source_target_pairs={{0,257},{1,256},{64,321},{65,320},{128,385},{129,384},{192,449},{1... | collective-permute-start | bytes 786440 | tf_op jit(solution)/shard_map/ppermute | solution.py:102
  60.2 10.3 %copy-start.8 = (bf16[128,1024]{1,0:T(8,128)(2,1)}, bf16[128,1024]{1,0:T(8,128)(2,1)S(1)}, u32[]{:S(2)}) copy-start(bf16[128,1024]{1,0:T(8,128)(2,1)S(1)} %collective-permute-done) | copy-start | bytes 786436
  67.6 1.3 copy-start.2
  70.5 15.6 %copy-start.1 = (bf16[1,256,1024]{2,1,0:T(8,128)(2,1)S(1)}, bf16[1,256,1024]{2,1,0:T(8,128)(2,1)}, u32[]{:S(2)}) copy-start(bf16[1,256,1024]{2,1,0:T(8,128)(2,1)} %param.10) | copy-start | bytes 1572868
  70.6 45.6 %all-to-all-start.2 = ((bf16[8,8,16,1024]{3,2,1,0:T(8,128)(2,1)}), bf16[8,8,16,1024]{3,2,1,0:T(8,128)(2,1)S(1)}, u32[]{:S(2)}, u32[]{:S(2)}) async-start(bf16[8,8,16,1024]{3,2,1,0:T(8,128)(2,1)} %broadcast_in_dim.54), calls=%async_computation.2 | async-start | bytes 4194304 | tf_op jit(solution)/shard_map/all_to_all | solution.py:20
  77.6 2.7 %copy-start.9 = (bf16[128,1024]{1,0:T(8,128)(2,1)S(1)}, bf16[128,1024]{1,0:T(8,128)(2,1)}, u32[]{:S(2)}) copy-start(bf16[128,1024]{1,0:T(8,128)(2,1)} %copy-done.8) | copy-start | bytes 786436
  80.3 26.1 %collective-permute-start.3 = (bf16[128,1024]{1,0:T(8,128)(2,1)S(1)}, bf16[128,1024]{1,0:T(8,128)(2,1)}, u32[]{:S(2)}, u32[]{:S(2)}) collective-permute-start(bf16[128,1024]{1,0:T(8,128)(2,1)S(1)} %copy-done.9), channel_id=1, source_target_pairs={{0,1},{1,0},{2,3},{3,2},{4,5},{5,4},{6,7},{7,6},{8,9},{9,8},{10,11... | collective-permute-start | bytes 786440 | tf_op jit(solution)/shard_map/ppermute | solution.py:110
  83.7 25.4 %collective-permute-start.2 = (bf16[128,1024]{1,0:T(8,128)(2,1)}, bf16[128,1024]{1,0:T(8,128)(2,1)S(1)}, u32[]{:S(2)}, u32[]{:S(2)}) collective-permute-start(bf16[128,1024]{1,0:T(8,128)(2,1)} %collective-permute-done.1), channel_id=1, source_target_pairs={{0,1},{1,0},{2,3},{3,2},{4,5},{5,4},{6,7},{7,6},{8,9},{9,8},{10,11... | collective-permute-start | bytes 786440 | tf_op jit(solution)/shard_map/ppermute | solution.py:110
  111.8 1.7 copy-start.5
  111.8 1.7 copy-start.6
  118.8 33.6 %all-to-all-start.3 = ((bf16[64,8,1024]{2,1,0:T(8,128)(2,1)}), bf16[64,8,1024]{2,1,0:T(8,128)(2,1)S(1)}, u32[]{:S(2)}, u32[]{:S(2)}) async-start(bf16[64,8,1024]{2,1,0:T(8,128)(2,1)} %bitcast.21), calls=%async_computation.3 | async-start | bytes 2097152 | tf_op jit(solution)/shard_map/all_to_all | solution.py:133
  126.9 71.8 %copy-start.10 = (f32[1,256]{1,0:T(1,128)S(1)}, f32[1,256]{1,0:T(1,128)}, u32[]{:S(2)}) copy-start(f32[1,256]{1,0:T(1,128)} %param.11) | copy-start | bytes 3076
  152.4 1.8 copy-start
  158.4 40.2 %all-to-all-start.4 = ((bf16[64,8,1408]{2,1,0:T(8,128)(2,1)}), bf16[64,8,1408]{2,1,0:T(8,128)(2,1)S(1)}, u32[]{:S(2)}, u32[]{:S(2)}) async-start(bf16[64,8,1408]{2,1,0:T(8,128)(2,1)} %bitcast.24), calls=%async_computation.4 | async-start | bytes 2883584 | tf_op jit(solution)/shard_map/all_to_all | solution.py:148

commit v5 on v3

--- a/solution.py
+++ b/solution.py
@@ -1,5 +1,3 @@
-import functools
-
 import jax
 import jax.numpy as jnp
 from jax import lax
@@ -12,7 +10,7 @@
 AXES = ("y", "x", "z")
 VMEM = pl.BlockSpec(memory_space=pltpu.VMEM)
 SMEM = pl.BlockSpec(memory_space=pltpu.SMEM)
-PARAMS = pltpu.CompilerParams(vmem_limit_bytes=48 << 20)
+PARAMS = pltpu.CompilerParams(vmem_limit_bytes=20 << 20)
 
 
 def gathered(x, axis):
@@ -39,8 +37,8 @@
 
 
 def mix_kernel(decoding, context, tokens, weight, slot, out):
-    many, few, rows, width = weight.shape
-    block = many * rows
+    many, few, sides, rows, width = weight.shape
+    block = many * sides * rows
     total = jnp.zeros((context.shape[0], width), jnp.float32)
     for k in range(few):
         piece = weight[:, k].reshape(block, width)
@@ -82,28 +80,20 @@
     tok_dev, width = inputs.shape
     cap = max(8, 2 * tok_dev // experts)
 
-    ahead = functools.partial(lax.ppermute, axis_name="section")
-    keys_far = ahead(mem_keys[0], perm=[(s, s + step) for s in range(half)])
-    values_far = ahead(mem_values[0], perm=[(s, (s - step) % sections) for s in range(half)])
+    across = [(s, s + half) for s in range(half)]
+    keys_far = lax.ppermute(mem_keys[0], "section", across)
+    values_far = lax.ppermute(mem_values[0], "section", across)
 
-    spread = gathered(jnp.stack([q_weight[0], out_weight[0]]), "y")
-    spread, keys_far, values_far = lax.optimization_barrier((spread, keys_far, values_far))
-
-    keys_far = ahead(keys_far, perm=[(s, s + step) for s in range(step, half + step)])
-    turned = [(s - step) % sections for s in range(half)]
-    values_far = ahead(values_far, perm=[(s, (s - step) % sections) for s in turned])
-    mine = spread[:, 0]
+    mine = jnp.stack([q_weight[0], out_weight[0]])
     other = lax.ppermute(mine, "z", [(0, 1), (1, 0)])
-    wq_mine = gathered(mine, "x")
-    wq_mine, other, keys_far, values_far, out_spread = lax.optimization_barrier(
-        (wq_mine, other, keys_far, values_far, spread[:, 1])
-    )
-    wq_other = gathered(other, "x")
-    wq_mine, wq_other, out_spread = lax.optimization_barrier((wq_mine, wq_other, out_spread))
-    wo = gathered(out_spread, ("x", "z"))
     low = lax.axis_index("z") == 0
-    wq = jnp.stack([jnp.where(low, wq_mine, wq_other), jnp.where(low, wq_other, wq_mine)])
-    wq = wq.transpose(2, 1, 0, 3, 4).reshape(width, width)
+    spread = jnp.stack([jnp.where(low, mine, other), jnp.where(low, other, mine)], axis=1)
+    spread = gathered(spread, "y")
+    spread, keys_far = lax.optimization_barrier((spread, keys_far))
+    wq = gathered(spread[:, 0], "x")
+    wq, values_far, out_spread = lax.optimization_barrier((wq, values_far, spread[:, 1]))
+    wo = gathered(out_spread, "x")
+    wq = wq.transpose(1, 0, 2, 3, 4).reshape(width, width)
 
     keys = jnp.concatenate([keys_far, mem_keys[0]], axis=0)
     values = jnp.concatenate([values_far, mem_values[0]], axis=0)

time: 194 us -> 193 us (level)
  blocking collectives: 18 us -> 0 us
  waiting for transfers between devices: 97.6 us -> 105 us
  starting transfers between devices: 51.1 us -> 57.2 us
  local copies, waits for them, and re-layouts: 9.15 us -> 14 us
  other arithmetic: 4.65 us -> 1.95 us
    all_to_all x3, waiting for transfers between devices: 12.6 us -> 38.1 us  [gathered(): lax.all_to_all(jnp.broadcast_to(x[None], (peers, *x.shape)), axis, 0, 0,...]
    ppermute x4 -> x2, waiting for transfers between devices: 23.2 us -> 4.85 us  [the longest x1 3.41 us: shards(): keys_far = lax.ppermute(mem_keys[0], 'section', across)]
    all_to_all x1 -> x0, blocking collectives: 18 us -> none  [gathered(): lax.all_to_all(jnp.broadcast_to(x[None], (peers, *x.shape)), axis, 0, 0,...]
    ppermute x4 -> x2, starting transfers between devices: 18.4 us -> 22.4 us  [the longest x1 11.4 us: shards(): keys_far = lax.ppermute(mem_keys[0], 'section', across)]
    another operation x3 -> x2, other arithmetic: 2.73 us -> 0.03 us  [shards(): jnp.stack([jnp.where(low, mine, other), jnp.where(low, other, mine)], axi...]
    optimization_barrier x2 -> x3, local copies, waits for them, and re-layouts: 1.31 us -> 3.9 us  [the longest x2 2.78 us: shards(): lax.optimization_barrier((wq, values_far, spread[:, 1]))]
    ppermute x1, starting transfers between devices: 1.91 us -> 4.27 us  [shards(): other = lax.ppermute(mine, 'z', [(0, 1), (1, 0)])]
    ppermute x1, waiting for transfers between devices: 0.01 us -> 2.22 us  [shards(): other = lax.ppermute(mine, 'z', [(0, 1), (1, 0)])]
  transfers between devices with their start and end apart: 10 -> 8, of which waited for: 6 -> 8; matrix products, arithmetic and copies ran while one was open for 5% -> 5% of each run, Pallas kernels for 0% -> 0%
where the time goes in v5:
time: 193 us; the launch traced here: 192 us
  waiting for transfers between devices  105 us (54%)
  starting transfers between devices  57.2 us (30%)
  local copies, waits for them, and re-layouts  14 us (7%)
  matrix products  5.91 us (3%)
  Pallas kernels  5.76 us (3%)
  other arithmetic  1.95 us (1%)
    all_to_all x3, waiting for transfers between devices, gathered(): lax.all_to_all(jnp.broadcast_to(x[None], (peers, *x.shape)), axis, 0, 0,...  38.1 us
    all_to_all x1, waiting for transfers between devices, shards(): lax.all_to_all(acts.reshape(experts, cap, -1), AXES, split_axis=0, concat...  34.5 us
    all_to_all x1, waiting for transfers between devices, shards(): lax.all_to_all(buffer.reshape(experts, cap, width), AXES, split_axis=0, c...  25.7 us
    all_to_all x3, starting transfers between devices, gathered(): lax.all_to_all(jnp.broadcast_to(x[None], (peers, *x.shape)), axis, 0, 0,...  17.5 us
    ppermute x1, starting transfers between devices, shards(): keys_far = lax.ppermute(mem_keys[0], 'section', across)  11.4 us
    ppermute x1, starting transfers between devices, shards(): values_far = lax.ppermute(mem_values[0], 'section', across)  11 us
    all_to_all x1, starting transfers between devices, shards(): lax.all_to_all(acts.reshape(experts, cap, -1), AXES, split_axis=0, concat...  6.8 us
    all_to_all x1, starting transfers between devices, shards(): lax.all_to_all(buffer.reshape(experts, cap, width), AXES, split_axis=0, c...  6.24 us
  transfers between devices with their start and end apart: 8, of which 8 were waited for; matrix products, arithmetic and copies ran while one was open for 5% of the time, Pallas kernels for 0%

profile of v5, /device:TPU:6, one launch (start us, length us, event | category | flops | bytes accessed | tf_op | source)
XLA Modules:
  0.0 191.7 jit_solution(6285221923045580232)
XLA Ops:
  0.0 0.8 constant_dynamic-update-slice_fusion.1
  1.6 4.3 %collective-permute-start = (bf16[2,16,1024]{2,1,0:T(8,128)(2,1)S(1)}, bf16[2,16,1024]{2,1,0:T(8,128)(2,1)S(1)}, u32[]{:S(2)}, u32[]{:S(2)}) collective-permute-start(bf16[2,16,1024]{2,1,0:T(8,128)(2,1)S(1)} %constant_dynamic-update-slice_fusion), channel_id=1, source_target_pairs={{0,1},{1,0},{2,3},{3,2},{4,5},{5,4},{6,7},{7,6},{8,9},{9,8},{10,11... | collective-permute-start | bytes 196616 | tf_op jit(solution)/shard_map/ppermute | solution.py:88
  5.8 2.2 %collective-permute-done = bf16[2,16,1024]{2,1,0:T(8,128)(2,1)S(1)} collective-permute-done((bf16[2,16,1024]{2,1,0:T(8,128)(2,1)S(1)}, bf16[2,16,1024]{2,1,0:T(8,128)(2,1)S(1)}, u32[]{:S(2)}, u32[]{:S(2)}) %collective-permute-start) | collective-permute-done | bytes 65568 | tf_op jit(solution)/shard_map/ppermute | solution.py:88
  8.1 1.1 broadcast_in_dim.28
  9.2 7.1 %all-to-all-start = ((bf16[8,2,2,16,1024]{4,3,2,1,0:T(8,128)(2,1)}), bf16[8,2,2,16,1024]{4,3,2,1,0:T(8,128)(2,1)S(1)}, u32[]{:S(2)}, u32[]{:S(2)}) async-start(bf16[8,2,2,16,1024]{4,3,2,1,0:T(8,128)(2,1)} %broadcast_in_dim.28), calls=%async_computation | async-start | bytes 2097152 | tf_op jit(solution)/shard_map/all_to_all | solution.py:18
  16.4 11.4 %collective-permute-start.1 = (bf16[128,1024]{1,0:T(8,128)(2,1)S(1)}, bf16[128,1024]{1,0:T(8,128)(2,1)}, u32[]{:S(2)}, u32[]{:S(2)}) collective-permute-start(bf16[128,1024]{1,0:T(8,128)(2,1)S(1)} %bitcast.55), channel_id=1, source_target_pairs={{0,256},{64,320},{128,384},{192,448},{1,257},{65,321},{129,385},{1... | collective-permute-start | bytes 786440 | tf_op jit(solution)/shard_map/ppermute | solution.py:84
  27.8 3.4 %collective-permute-done.1 = bf16[128,1024]{1,0:T(8,128)(2,1)} collective-permute-done((bf16[128,1024]{1,0:T(8,128)(2,1)S(1)}, bf16[128,1024]{1,0:T(8,128)(2,1)}, u32[]{:S(2)}, u32[]{:S(2)}) %collective-permute-start.1) | collective-permute-done | bytes 262176 | tf_op jit(solution)/shard_map/ppermute | solution.py:84
  31.2 13.0 %all-to-all-done = bf16[8,2,2,16,1024]{4,3,2,1,0:T(8,128)(2,1)S(1)} async-done(((bf16[8,2,2,16,1024]{4,3,2,1,0:T(8,128)(2,1)}), bf16[8,2,2,16,1024]{4,3,2,1,0:T(8,128)(2,1)S(1)}, u32[]{:S(2)}, u32[]{:S(2)}) %all-to-all-start) | async-done | bytes 1048608 | tf_op jit(solution)/shard_map/all_to_all | solution.py:18
  44.3 1.6 broadcast_in_dim.51
  45.9 4.8 %all-to-all-start.1 = ((bf16[4,8,2,16,1024]{4,3,2,1,0:T(8,128)(2,1)}), bf16[4,8,2,16,1024]{4,3,2,1,0:T(8,128)(2,1)S(1)}, u32[]{:S(2)}, u32[]{:S(2)}) async-start(bf16[4,8,2,16,1024]{4,3,2,1,0:T(8,128)(2,1)} %broadcast_in_dim.51), calls=%async_computation.1 | async-start | bytes 4194304 | tf_op jit(solution)/shard_map/all_to_all | solution.py:18
  50.7 11.0 %collective-permute-start.2 = (bf16[128,1024]{1,0:T(8,128)(2,1)S(1)}, bf16[128,1024]{1,0:T(8,128)(2,1)}, u32[]{:S(2)}, u32[]{:S(2)}) collective-permute-start(bf16[128,1024]{1,0:T(8,128)(2,1)S(1)} %bitcast.56), channel_id=1, source_target_pairs={{0,256},{64,320},{128,384},{192,448},{1,257},{65,321},{129,385},{1... | collective-permute-start | bytes 786440 | tf_op jit(solution)/shard_map/ppermute | solution.py:85
  62.7 0.8 copy.35
  63.6 1.1 copy.37
  64.7 1.4 collective-permute-done.2
  66.1 9.0 %all-to-all-done.1 = bf16[4,8,2,16,1024]{4,3,2,1,0:T(8,128)(2,1)S(1)} async-done(((bf16[4,8,2,16,1024]{4,3,2,1,0:T(8,128)(2,1)}), bf16[4,8,2,16,1024]{4,3,2,1,0:T(8,128)(2,1)S(1)}, u32[]{:S(2)}, u32[]{:S(2)}) %all-to-all-start.1) | async-done | bytes 2097184 | tf_op jit(solution)/shard_map/all_to_all | solution.py:18
  75.2 1.6 copy.36
  76.7 1.2 copy.34
  77.9 1.6 broadcast_in_dim.54
  79.5 5.6 %all-to-all-start.2 = ((bf16[4,8,2,16,1024]{4,3,2,1,0:T(8,128)(2,1)}), bf16[4,8,2,16,1024]{4,3,2,1,0:T(8,128)(2,1)S(1)}, u32[]{:S(2)}, u32[]{:S(2)}) async-start(bf16[4,8,2,16,1024]{4,3,2,1,0:T(8,128)(2,1)} %broadcast_in_dim.54), calls=%async_computation.2 | async-start | bytes 4194304 | tf_op jit(solution)/shard_map/all_to_all | solution.py:18
  85.2 2.4 %convolution_convert_fusion = bf16[1024,256]{1,0:T(8,128)(2,1)S(1)} fusion(bf16[1024,1024]{1,0:T(8,128)(2,1)} %bitcast.50, bf16[1,256,1024]{2,1,0:T(8,128)(2,1)S(1)} %copy-done.1), kind=kOutput, calls=%fused_computation.13 | convolution fusion | flops 537133056 | bytes 3145728 | tf_op jit(solution)/shard_map/dot_general | solution.py:100
  88.3 1.7 fusion.24
  90.1 1.3 fusion.9
  91.4 1.2 copy.40.context
  92.6 16.1 %all-to-all-done.2.weight = bf16[4,8,2,16,1024]{4,3,2,1,0:T(8,128)(2,1)S(1)} async-done(((bf16[4,8,2,16,1024]{4,3,2,1,0:T(8,128)(2,1)}), bf16[4,8,2,16,1024]{4,3,2,1,0:T(8,128)(2,1)S(1)}, u32[]{:S(2)}, u32[]{:S(2)}) %all-to-all-start.2) | async-done | bytes 2097184 | tf_op jit(solution)/shard_map/all_to_all | solution.py:18
  108.7 2.6 %mix.1 = bf16[512,1024]{1,0:T(8,128)(2,1)} custom-call(s32[1]{0:T(128)} %bitcast.2.decoding, bf16[256,1024]{1,0:T(8,128)(2,1)S(1)} %copy.40.context, bf16[256,1024]{1,0:T(8,128)(2,1)S(1)} %bitcast.49, bf16[4,8,2,16,1024]{4,3,2,1,0:T(8,128)(2,1)S(1)} %all-to-all-done.2.weight, s32[1,256]{1,0:T(1,128)S(1)} %bitcast_add_fusion.slot), custom_call_target="tpu_custom_call" | custom-call | tf_op jit(solution)/shard_map/mix/pallas_call | solution.py:110
  111.3 6.2 %all-to-all-start.3 = ((bf16[64,8,1024]{2,1,0:T(8,128)(2,1)}), bf16[64,8,1024]{2,1,0:T(8,128)(2,1)S(1)}, u32[]{:S(2)}, u32[]{:S(2)}) async-start(bf16[64,8,1024]{2,1,0:T(8,128)(2,1)} %bitcast.23), calls=%async_computation.3 | async-start | bytes 2097152 | tf_op jit(solution)/shard_map/all_to_all | solution.py:118
  118.3 25.7 %all-to-all-done.3 = bf16[64,8,1024]{2,1,0:T(8,128)(2,1)S(1)} async-done(((bf16[64,8,1024]{2,1,0:T(8,128)(2,1)}), bf16[64,8,1024]{2,1,0:T(8,128)(2,1)S(1)}, u32[]{:S(2)}, u32[]{:S(2)}) %all-to-all-start.3) | async-done | bytes 1048608 | tf_op jit(solution)/shard_map/all_to_all | solution.py:118
  144.0 1.8 copy-done
  145.8 3.1 %expert.1 = bf16[512,1408]{1,0:T(8,128)(2,1)} custom-call(s32[1]{0:T(128)} %bitcast.45.capacity, bf16[512,1024]{1,0:T(8,128)(2,1)S(1)} %bitcast.47, bf16[1024,1408]{1,0:T(8,128)(2,1)S(1)} %bitcast.48), custom_call_target="tpu_custom_call" | custom-call | tf_op jit(solution)/shard_map/expert/pallas_call | solution.py:121
  148.9 6.8 %all-to-all-start.4 = ((bf16[64,8,1408]{2,1,0:T(8,128)(2,1)}), bf16[64,8,1408]{2,1,0:T(8,128)(2,1)S(1)}, u32[]{:S(2)}, u32[]{:S(2)}) async-start(bf16[64,8,1408]{2,1,0:T(8,128)(2,1)} %bitcast.26), calls=%async_computation.4 | async-start | bytes 2883584 | tf_op jit(solution)/shard_map/all_to_all | solution.py:129
  155.7 34.5 %all-to-all-done.4 = bf16[64,8,1408]{2,1,0:T(8,128)(2,1)S(1)} async-done(((bf16[64,8,1408]{2,1,0:T(8,128)(2,1)}), bf16[64,8,1408]{2,1,0:T(8,128)(2,1)S(1)}, u32[]{:S(2)}, u32[]{:S(2)}) %all-to-all-start.4) | async-done | bytes 1441824 | tf_op jit(solution)/shard_map/all_to_all | solution.py:129
  190.2 1.5 fusion.3
  (24 shorter events, 2.1 us)
Async XLA Ops:
  0.0 16.3 %copy-start.2 = (bf16[1,128,1024]{2,1,0:T(8,128)(2,1)S(1)}, bf16[1,128,1024]{2,1,0:T(8,128)(2,1)}, u32[]{:S(2)}) copy-start(bf16[1,128,1024]{2,1,0:T(8,128)(2,1)} %param.15) | copy-start | bytes 786436
  1.6 6.5 %collective-permute-start = (bf16[2,16,1024]{2,1,0:T(8,128)(2,1)S(1)}, bf16[2,16,1024]{2,1,0:T(8,128)(2,1)S(1)}, u32[]{:S(2)}, u32[]{:S(2)}) collective-permute-start(bf16[2,16,1024]{2,1,0:T(8,128)(2,1)S(1)} %constant_dynamic-update-slice_fusion), channel_id=1, source_target_pairs={{0,1},{1,0},{2,3},{3,2},{4,5},{5,4},{6,7},{7,6},{8,9},{9,8},{10,11... | collective-permute-start | bytes 196616 | tf_op jit(solution)/shard_map/ppermute | solution.py:88
  9.2 35.0 %all-to-all-start = ((bf16[8,2,2,16,1024]{4,3,2,1,0:T(8,128)(2,1)}), bf16[8,2,2,16,1024]{4,3,2,1,0:T(8,128)(2,1)S(1)}, u32[]{:S(2)}, u32[]{:S(2)}) async-start(bf16[8,2,2,16,1024]{4,3,2,1,0:T(8,128)(2,1)} %broadcast_in_dim.28), calls=%async_computation | async-start | bytes 2097152 | tf_op jit(solution)/shard_map/all_to_all | solution.py:18
  16.4 34.4 %copy-start.3 = (bf16[1,128,1024]{2,1,0:T(8,128)(2,1)S(1)}, bf16[1,128,1024]{2,1,0:T(8,128)(2,1)}, u32[]{:S(2)}) copy-start(bf16[1,128,1024]{2,1,0:T(8,128)(2,1)} %param.16) | copy-start | bytes 786436
  16.4 46.0 %copy-start.5 = (s32[1,256,1]{1,2,0:T(1,128)S(1)}, s32[1,256,1]{1,2,0:T(1,128)}, u32[]{:S(2)}) copy-start(s32[1,256,1]{1,2,0:T(1,128)} %param.12) | copy-start | bytes 3076
  16.4 14.8 %collective-permute-start.1 = (bf16[128,1024]{1,0:T(8,128)(2,1)S(1)}, bf16[128,1024]{1,0:T(8,128)(2,1)}, u32[]{:S(2)}, u32[]{:S(2)}) collective-permute-start(bf16[128,1024]{1,0:T(8,128)(2,1)S(1)} %bitcast.55), channel_id=1, source_target_pairs={{0,256},{64,320},{128,384},{192,448},{1,257},{65,321},{129,385},{1... | collective-permute-start | bytes 786440 | tf_op jit(solution)/shard_map/ppermute | solution.py:84
  45.9 29.2 %all-to-all-start.1 = ((bf16[4,8,2,16,1024]{4,3,2,1,0:T(8,128)(2,1)}), bf16[4,8,2,16,1024]{4,3,2,1,0:T(8,128)(2,1)S(1)}, u32[]{:S(2)}, u32[]{:S(2)}) async-start(bf16[4,8,2,16,1024]{4,3,2,1,0:T(8,128)(2,1)} %broadcast_in_dim.51), calls=%async_computation.1 | async-start | bytes 4194304 | tf_op jit(solution)/shard_map/all_to_all | solution.py:18
  50.7 15.4 %collective-permute-start.2 = (bf16[128,1024]{1,0:T(8,128)(2,1)S(1)}, bf16[128,1024]{1,0:T(8,128)(2,1)}, u32[]{:S(2)}, u32[]{:S(2)}) collective-permute-start(bf16[128,1024]{1,0:T(8,128)(2,1)S(1)} %bitcast.56), channel_id=1, source_target_pairs={{0,256},{64,320},{128,384},{192,448},{1,257},{65,321},{129,385},{1... | collective-permute-start | bytes 786440 | tf_op jit(solution)/shard_map/ppermute | solution.py:85
  76.7 8.4 %copy-start.1 = (bf16[1,256,1024]{2,1,0:T(8,128)(2,1)S(1)}, bf16[1,256,1024]{2,1,0:T(8,128)(2,1)}, u32[]{:S(2)}) copy-start(bf16[1,256,1024]{2,1,0:T(8,128)(2,1)} %param.10) | copy-start | bytes 1572868
  79.5 29.2 %all-to-all-start.2 = ((bf16[4,8,2,16,1024]{4,3,2,1,0:T(8,128)(2,1)}), bf16[4,8,2,16,1024]{4,3,2,1,0:T(8,128)(2,1)S(1)}, u32[]{:S(2)}, u32[]{:S(2)}) async-start(bf16[4,8,2,16,1024]{4,3,2,1,0:T(8,128)(2,1)} %broadcast_in_dim.54), calls=%async_computation.2 | async-start | bytes 4194304 | tf_op jit(solution)/shard_map/all_to_all | solution.py:18
  88.3 1.7 copy-start.4
  111.3 32.6 %all-to-all-start.3 = ((bf16[64,8,1024]{2,1,0:T(8,128)(2,1)}), bf16[64,8,1024]{2,1,0:T(8,128)(2,1)S(1)}, u32[]{:S(2)}, u32[]{:S(2)}) async-start(bf16[64,8,1024]{2,1,0:T(8,128)(2,1)} %bitcast.23), calls=%async_computation.3 | async-start | bytes 2097152 | tf_op jit(solution)/shard_map/all_to_all | solution.py:118
  117.6 72.6 %copy-start.6 = (f32[1,256]{1,0:T(1,128)S(1)}, f32[1,256]{1,0:T(1,128)}, u32[]{:S(2)}) copy-start(f32[1,256]{1,0:T(1,128)} %param.11) | copy-start | bytes 3076
  144.0 1.8 copy-start
  148.9 41.3 %all-to-all-start.4 = ((bf16[64,8,1408]{2,1,0:T(8,128)(2,1)}), bf16[64,8,1408]{2,1,0:T(8,128)(2,1)S(1)}, u32[]{:S(2)}, u32[]{:S(2)}) async-start(bf16[64,8,1408]{2,1,0:T(8,128)(2,1)} %bitcast.26), calls=%async_computation.4 | async-start | bytes 2883584 | tf_op jit(solution)/shard_map/all_to_all | solution.py:129

commit v6 on v4

--- a/solution.py
+++ b/solution.py
@@ -1,5 +1,3 @@
-import functools
-
 import jax
 import jax.numpy as jnp
 from jax import lax
@@ -12,7 +10,7 @@
 AXES = ("y", "x", "z")
 VMEM = pl.BlockSpec(memory_space=pltpu.VMEM)
 SMEM = pl.BlockSpec(memory_space=pltpu.SMEM)
-PARAMS = pltpu.CompilerParams(vmem_limit_bytes=48 << 20)
+PARAMS = pltpu.CompilerParams(vmem_limit_bytes=20 << 20)
 
 
 def gathered(x, axis):
@@ -20,38 +18,52 @@
     return lax.all_to_all(jnp.broadcast_to(x[None], (peers, *x.shape)), axis, 0, 0, tiled=True)
 
 
-def attend_block(query, keys, values, length):
-    rows = query.shape[0]
-    span = keys.shape[0]
-    qh = query.reshape(rows, HEADS, -1)
-    kh = keys.reshape(span, HEADS, -1)
-    vh = values.reshape(span, HEADS, -1)
-    scores = jnp.einsum("qhd,khd->hqk", qh, kh, preferred_element_type=jnp.float32) / jnp.sqrt(
-        jnp.float32(qh.shape[2])
-    )
-    valid = jnp.arange(span, dtype=jnp.int32) < length
-    scores = jnp.where(valid[None, None, :], scores, jnp.float32(-1e30))
-    scores = scores - jnp.max(scores, axis=-1, keepdims=True)
-    weights = jnp.exp(scores)
-    probs = (weights / jnp.sum(weights, axis=-1, keepdims=True)).astype(jnp.bfloat16)
-    context = jnp.einsum("hqk,khd->qhd", probs, vh, preferred_element_type=jnp.float32)
-    return context.reshape(rows, -1).astype(jnp.bfloat16)
+def whole(mine, other, low, which):
+    first = jnp.where(low, mine[:, :, which], other[:, :, which])
+    second = jnp.where(low, other[:, :, which], mine[:, :, which])
+    both = jnp.stack([first, second], axis=2)
+    return jnp.swapaxes(both, 0, 1).reshape(-1, mine.shape[-1])
 
 
-def mix_kernel(decoding, context, tokens, weight, slot, out):
-    many, few, rows, width = weight.shape
-    block = many * rows
-    total = jnp.zeros((context.shape[0], width), jnp.float32)
-    for k in range(few):
-        piece = weight[:, k].reshape(block, width)
-        total += jnp.dot(
-            context[:, k * block : (k + 1) * block], piece, preferred_element_type=jnp.float32
-        )
+def decode_kernel(
+    facts, tokens, keys_far, keys_near, values_far, values_near, mine, other, slot, out, query, context
+):
+    decoding, length, low = facts[0] > 0, facts[1], facts[2] > 0
     own = tokens[...]
+    rows, width = own.shape
+    slab = 128
+    dim = width // HEADS
+    query[...] = jnp.dot(
+        own, whole(mine, other, low, 0), preferred_element_type=jnp.float32
+    ).astype(jnp.bfloat16)
+    span = keys_far.shape[0] + keys_near.shape[0]
+    valid = lax.broadcasted_iota(jnp.int32, (rows, span), 1) < length
+    lane = lax.broadcasted_iota(jnp.int32, (rows, slab), 1)
+    for p in range(width // slab):
+        part = slice(p * slab, (p + 1) * slab)
+        keys = jnp.concatenate([keys_far[:, part], keys_near[:, part]], axis=0)
+        values = jnp.concatenate([values_far[:, part], values_near[:, part]], axis=0)
+        pair = query[:, part]
+        found = jnp.zeros((rows, slab), jnp.float32)
+        for h in range(slab // dim):
+            here = (lane >= h * dim) & (lane < (h + 1) * dim)
+            asked = jnp.where(here, pair, jnp.zeros_like(pair))
+            scores = lax.dot_general(
+                asked, keys, (((1,), (1,)), ((), ())), preferred_element_type=jnp.float32
+            ) * (dim**-0.5)
+            scores = jnp.where(valid, scores, -1e30)
+            weights = jnp.exp(scores - jnp.max(scores, axis=1, keepdims=True))
+            probs = weights * (1.0 / jnp.sum(weights, axis=1, keepdims=True))
+            seen = jnp.dot(probs.astype(jnp.bfloat16), values, preferred_element_type=jnp.float32)
+            found = jnp.where(here, seen, found)
+        context[:, part] = found.astype(jnp.bfloat16)
+    total = jnp.dot(
+        context[...], whole(mine, other, low, 1), preferred_element_type=jnp.float32
+    )
     added = (own.astype(jnp.float32) + total).astype(jnp.bfloat16)
-    mixed = jnp.where(decoding[0] > 0, added, own)
+    mixed = jnp.where(decoding, added, own)
     slots = out.shape[0]
-    index = lax.broadcasted_iota(jnp.int32, (slots, own.shape[0]), 0)
+    index = lax.broadcasted_iota(jnp.int32, (slots, rows), 0)
     placed = (index == slot[...]).astype(jnp.float32)
     used = jnp.sum(placed, axis=1, keepdims=True) > 0.5
     sent = jnp.dot(placed.astype(jnp.bfloat16), mixed, preferred_element_type=jnp.float32)
@@ -92,28 +104,16 @@
     tok_dev, width = inputs.shape
     cap = max(8, 2 * tok_dev // experts)
 
-    sides = lax.axis_size("z")
-    over = [
-        (s * sides + z, (s + half) * sides + (z + 1) % sides)
-        for s in range(half)
-        for z in range(sides)
-    ]
-    beside = [(z, (z + 1) % sides) for z in range(sides)]
-    keys_far, values_far = lax.ppermute((mem_keys[0], mem_values[0]), ("section", "z"), over)
+    across = [(s, s + half) for s in range(half)]
+    keys_far = lax.ppermute(mem_keys[0], "section", across)
+    values_far = lax.ppermute(mem_values[0], "section", across)
 
     spread = gathered(jnp.stack([q_weight[0], out_weight[0]]), "y")
-    wq = gathered(spread[:, 0], ("x", "z"))
-    wq, keys_far, values_far, out_spread = lax.optimization_barrier(
-        (wq, keys_far, values_far, spread[:, 1])
-    )
-    wo = gathered(out_spread, ("x", "z"))
-    keys_far, values_far = lax.ppermute((keys_far, values_far), "z", beside)
-    wq = wq.transpose(1, 0, 2, 3).reshape(width, width)
-
-    keys = jnp.concatenate([keys_far, mem_keys[0]], axis=0)
-    values = jnp.concatenate([values_far, mem_values[0]], axis=0)
-    query = jnp.dot(inputs, wq, preferred_element_type=jnp.float32).astype(jnp.bfloat16)
-    context = attend_block(query, keys, values, mem_lengths[0, 0])
+    beside = lax.ppermute(spread, "z", [(0, 1), (1, 0)])
+    mine = gathered(spread, "x")
+    mine, beside, keys_far = lax.optimization_barrier((mine, beside, keys_far))
+    other = gathered(beside, "x")
+    mine, other, values_far = lax.optimization_barrier((mine, other, values_far))
 
     route = routes[0, :, 0]
     same = route[:, None] == route[None, :]
@@ -122,14 +122,27 @@
     slot = route * cap + lrank
     decoding = (lax.axis_index("section") >= half).astype(jnp.int32)
 
+    low = (lax.axis_index("z") == 0).astype(jnp.int32)
+    facts = jnp.stack([decoding, mem_lengths[0, 0], low])
     buffer = pl.pallas_call(
-        mix_kernel,
+        decode_kernel,
         out_shape=jax.ShapeDtypeStruct((experts * cap, width), jnp.bfloat16),
-        in_specs=[SMEM, VMEM, VMEM, VMEM, VMEM],
+        in_specs=[SMEM] + [VMEM] * 8,
         out_specs=VMEM,
-        compiler_params=PARAMS,
-        name="mix",
-    )(decoding[None], context, inputs, wo, slot[None, :])
+        scratch_shapes=[pltpu.VMEM((tok_dev, width), jnp.bfloat16)] * 2,
+        compiler_params=pltpu.CompilerParams(vmem_limit_bytes=32 << 20),
+        name="decode",
+    )(
+        facts,
+        inputs,
+        keys_far,
+        mem_keys[0],
+        values_far,
+        mem_values[0],
+        mine,
+        other,
+        slot[None, :],
+    )
     received = lax.all_to_all(
         buffer.reshape(experts, cap, width), AXES, split_axis=0, concat_axis=0, tiled=True
     )
@@ -144,7 +157,11 @@
         ],
         compiler_params=PARAMS,
         name="expert",
-    )(capacity[0], received.reshape(experts * cap, width), w_in[0, 0])
+    )(
+        capacity[0],
+        received.reshape(experts * cap, width),
+        pltpu.with_memory_space_constraint(w_in[0, 0], pltpu.HBM),
+    )
     back = lax.all_to_all(
         acts.reshape(experts, cap, -1), AXES, split_axis=0, concat_axis=0, tiled=True
     )

time: 202 us -> 174 us (0.86)
  waiting for transfers between devices: 100 us -> 75.1 us
  local copies, waits for them, and re-layouts: 12.5 us -> 4.31 us
  starting transfers between devices: 45.5 us -> 53.5 us
  matrix products: 6.16 us -> 1.48 us
  Pallas kernels: 6.85 us -> 11.5 us
    ppermute x4 -> x3, waiting for transfers between devices: 38.3 us -> 6.64 us  [the longest x1 4.39 us: shards(): keys_far = lax.ppermute(mem_keys[0], 'section', across)]
    ppermute x4 -> x3, starting transfers between devices: 18 us -> 25.9 us  [the longest x1 11.6 us: shards(): values_far = lax.ppermute(mem_values[0], 'section', across)]
    all_to_all x2, waiting for transfers between devices: 3.76 us -> 10.6 us  [gathered(): lax.all_to_all(jnp.broadcast_to(x[None], (peers, *x.shape)), axis, 0, 0,...]
    dot_general x3 -> x0, matrix products: 4.68 us -> none  [the longest x1 1.8 us: attend_block(): jnp.einsum('qhd,khd->hqk', qh, kh, preferred_element_type=jnp.float32)]
    unnamed x24 -> x10, local copies, waits for them, and re-layouts: 4.2 us -> 0.02 us
    pallas_call x1, Pallas kernels: 2.63 us -> 6.54 us  [shards(): pl.pallas_call(decode_kernel, out_shape=jax.ShapeDtypeStruct((experts * c...]
  transfers between devices with their start and end apart: 8 -> 7, of which waited for: 7 -> 6; matrix products, arithmetic and copies ran while one was open for 6% -> 0% of each run, Pallas kernels for 0% -> 0%
where the time goes in v6:
time: 174 us; the launch traced here: 173 us
  waiting for transfers between devices  75.1 us (43%)
  starting transfers between devices  53.5 us (31%)
  blocking collectives  24.4 us (14%)
  Pallas kernels  11.5 us (7%)
  local copies, waits for them, and re-layouts  4.31 us (2%)
    all_to_all x1, waiting for transfers between devices, shards(): lax.all_to_all(acts.reshape(experts, cap, -1), AXES, split_axis=0, concat...  33.1 us
    all_to_all x1, waiting for transfers between devices, shards(): lax.all_to_all(buffer.reshape(experts, cap, width), AXES, split_axis=0, c...  24.7 us
    all_to_all x1, blocking collectives, gathered(): lax.all_to_all(jnp.broadcast_to(x[None], (peers, *x.shape)), axis, 0, 0,...  24.4 us
    ppermute x1, starting transfers between devices, shards(): values_far = lax.ppermute(mem_values[0], 'section', across)  11.6 us
    all_to_all x2, starting transfers between devices, gathered(): lax.all_to_all(jnp.broadcast_to(x[None], (peers, *x.shape)), axis, 0, 0,...  11.5 us
    all_to_all x2, waiting for transfers between devices, gathered(): lax.all_to_all(jnp.broadcast_to(x[None], (peers, *x.shape)), axis, 0, 0,...  10.6 us
    ppermute x1, starting transfers between devices, shards(): keys_far = lax.ppermute(mem_keys[0], 'section', across)  10 us
    all_to_all x1, starting transfers between devices, shards(): lax.all_to_all(buffer.reshape(experts, cap, width), AXES, split_axis=0, c...  9.29 us
  transfers between devices with their start and end apart: 7, of which 6 were waited for; matrix products, arithmetic and copies ran while one was open for 0% of the time, Pallas kernels for 0%

profile of v6, /device:TPU:6, one launch (start us, length us, event | category | flops | bytes accessed | tf_op | source)
XLA Modules:
  0.0 172.7 jit_solution(17248942879383896276)
XLA Ops:
  0.0 0.8 pad_maximum_fusion
  0.8 24.4 %all_to_all.25 = bf16[8,2,16,1024]{3,2,1,0:T(8,128)(2,1)S(1)} all-to-all(bf16[8,2,16,1024]{3,2,1,0:T(8,128)(2,1)S(1)} %broadcast_in_dim.8), channel_id=1, replica_groups=mesh['section'=8,'y'=8,'x'=4,'z'=2] {'y'}, dimensions={0} | all-to-all | bytes 1048576 | tf_op jit(solution)/shard_map/all_to_all | solution.py:18
  25.2 1.6 broadcast_in_dim.9
  26.9 0.0 copy-start.1
  26.9 4.9 %all-to-all-start.1 = ((bf16[4,8,2,16,1024]{4,3,2,1,0:T(8,128)(2,1)}), bf16[4,8,2,16,1024]{4,3,2,1,0:T(8,128)(2,1)S(1)}, u32[]{:S(2)}, u32[]{:S(2)}) async-start(bf16[4,8,2,16,1024]{4,3,2,1,0:T(8,128)(2,1)} %broadcast_in_dim.9), calls=%async_computation.1 | async-start | bytes 4194304 | tf_op jit(solution)/shard_map/all_to_all | solution.py:18
  31.8 4.3 %collective-permute-start = (bf16[8,2,16,1024]{3,2,1,0:T(8,128)(2,1)S(1)}, bf16[8,2,16,1024]{3,2,1,0:T(8,128)(2,1)}, u32[]{:S(2)}, u32[]{:S(2)}) collective-permute-start(bf16[8,2,16,1024]{3,2,1,0:T(8,128)(2,1)S(1)} %all_to_all.25), channel_id=1, source_target_pairs={{0,1},{1,0},{2,3},{3,2},{4,5},{5,4},{6,7},{7,6},{8,9},{9,8},{10,11... | collective-permute-start | bytes 1572872 | tf_op jit(solution)/shard_map/ppermute | solution.py:112
  36.0 0.0 copy-done.1
  36.0 10.0 %collective-permute-start.1 = (bf16[128,1024]{1,0:T(8,128)(2,1)S(1)}, bf16[128,1024]{1,0:T(8,128)(2,1)S(1)}, u32[]{:S(2)}, u32[]{:S(2)}) collective-permute-start(bf16[128,1024]{1,0:T(8,128)(2,1)S(1)} %bitcast.25), channel_id=1, source_target_pairs={{0,256},{64,320},{128,384},{192,448},{1,257},{65,321},{129,385},{1... | collective-permute-start | bytes 786440 | tf_op jit(solution)/shard_map/ppermute | solution.py:108
  46.1 4.4 %collective-permute-done.1.keys_far = bf16[128,1024]{1,0:T(8,128)(2,1)S(1)} collective-permute-done((bf16[128,1024]{1,0:T(8,128)(2,1)S(1)}, bf16[128,1024]{1,0:T(8,128)(2,1)S(1)}, u32[]{:S(2)}, u32[]{:S(2)}) %collective-permute-start.1) | collective-permute-done | bytes 262176 | tf_op jit(solution)/shard_map/ppermute | solution.py:108
  50.5 0.0 collective-permute-done
  50.5 3.8 %all-to-all-done.1.mine = bf16[4,8,2,16,1024]{4,3,2,1,0:T(8,128)(2,1)S(1)} async-done(((bf16[4,8,2,16,1024]{4,3,2,1,0:T(8,128)(2,1)}), bf16[4,8,2,16,1024]{4,3,2,1,0:T(8,128)(2,1)S(1)}, u32[]{:S(2)}, u32[]{:S(2)}) %all-to-all-start.1) | async-done | bytes 2097184 | tf_op jit(solution)/shard_map/all_to_all | solution.py:18
  54.2 2.6 %broadcast_in_dim.10 = bf16[4,8,2,16,1024]{4,3,2,1,0:T(8,128)(2,1)} broadcast(bf16[8,2,16,1024]{3,2,1,0:T(8,128)(2,1)} %collective-permute-done), dimensions={1,2,3,4} | broadcast | bytes 2621440 | tf_op jit(solution)/shard_map/broadcast_in_dim | solution.py:18
  56.9 0.0 copy-start.2
  56.9 0.0 copy-start.3
  56.9 6.6 %all-to-all-start.2 = ((bf16[4,8,2,16,1024]{4,3,2,1,0:T(8,128)(2,1)}), bf16[4,8,2,16,1024]{4,3,2,1,0:T(8,128)(2,1)}, u32[]{:S(2)}, u32[]{:S(2)}) async-start(bf16[4,8,2,16,1024]{4,3,2,1,0:T(8,128)(2,1)} %broadcast_in_dim.10), calls=%async_computation.2 | async-start | bytes 4194304 | tf_op jit(solution)/shard_map/all_to_all | solution.py:18
  63.5 0.0 copy-done.2
  63.5 11.6 %collective-permute-start.2 = (bf16[128,1024]{1,0:T(8,128)(2,1)S(1)}, bf16[128,1024]{1,0:T(8,128)(2,1)}, u32[]{:S(2)}, u32[]{:S(2)}) collective-permute-start(bf16[128,1024]{1,0:T(8,128)(2,1)S(1)} %bitcast.27), channel_id=1, source_target_pairs={{0,256},{64,320},{128,384},{192,448},{1,257},{65,321},{129,385},{1... | collective-permute-start | bytes 786440 | tf_op jit(solution)/shard_map/ppermute | solution.py:109
  75.7 0.0 copy-done.3
  75.7 0.2 convert_reduce_fusion
  75.9 0.1 pad_add_fusion.facts
  76.0 2.3 %collective-permute-done.2.values_far = bf16[128,1024]{1,0:T(8,128)(2,1)} collective-permute-done((bf16[128,1024]{1,0:T(8,128)(2,1)S(1)}, bf16[128,1024]{1,0:T(8,128)(2,1)}, u32[]{:S(2)}, u32[]{:S(2)}) %collective-permute-start.2) | collective-permute-done | bytes 262176 | tf_op jit(solution)/shard_map/ppermute | solution.py:109
  78.3 6.9 %all-to-all-done.2.other = bf16[4,8,2,16,1024]{4,3,2,1,0:T(8,128)(2,1)} async-done(((bf16[4,8,2,16,1024]{4,3,2,1,0:T(8,128)(2,1)}), bf16[4,8,2,16,1024]{4,3,2,1,0:T(8,128)(2,1)}, u32[]{:S(2)}, u32[]{:S(2)}) %all-to-all-start.2) | async-done | bytes 2097184 | tf_op jit(solution)/shard_map/all_to_all | solution.py:18
  85.1 0.0 copy-done
  85.1 6.5 %decode.1 = bf16[512,1024]{1,0:T(8,128)(2,1)} custom-call(s32[3]{0:T(128)S(1)} %pad_add_fusion.facts, bf16[256,1024]{1,0:T(8,128)(2,1)S(1)} %bitcast.24, bf16[128,1024]{1,0:T(8,128)(2,1)S(1)} %collective-permute-done.1.keys_far, bf16[128,1024]{1,0:T(8,128)(2,1)S(1)} %bitcast.26, bf16[128,1024]{1,0:T(8,128)(2,1)} %collective-permute-done.2.values_far, ...), custom_call_target="tpu_custom_call" | custom-call | tf_op jit(solution)/shard_map/decode/pallas_call | solution.py:127
  91.7 9.3 %all-to-all-start.3 = ((bf16[64,8,1024]{2,1,0:T(8,128)(2,1)}), bf16[64,8,1024]{2,1,0:T(8,128)(2,1)S(1)}, u32[]{:S(2)}, u32[]{:S(2)}) async-start(bf16[64,8,1024]{2,1,0:T(8,128)(2,1)} %bitcast.10), calls=%async_computation.3 | async-start | bytes 2097152 | tf_op jit(solution)/shard_map/all_to_all | solution.py:146
  101.6 24.7 %all-to-all-done.3 = bf16[64,8,1024]{2,1,0:T(8,128)(2,1)S(1)} async-done(((bf16[64,8,1024]{2,1,0:T(8,128)(2,1)}), bf16[64,8,1024]{2,1,0:T(8,128)(2,1)S(1)}, u32[]{:S(2)}, u32[]{:S(2)}) %all-to-all-start.3) | async-done | bytes 1048608 | tf_op jit(solution)/shard_map/all_to_all | solution.py:146
  126.3 5.0 %expert.1 = bf16[512,1408]{1,0:T(8,128)(2,1)} custom-call(s32[1]{0:T(128)} %bitcast.21.capacity, bf16[512,1024]{1,0:T(8,128)(2,1)S(1)} %bitcast.23, bf16[1024,1408]{1,0:T(8,128)(2,1)} %bitcast.29), custom_call_target="tpu_custom_call" | custom-call | tf_op jit(solution)/shard_map/expert/pallas_call | solution.py:149
  131.3 0.0 copy-start.4
  131.3 6.8 %all-to-all-start.4 = ((bf16[64,8,1408]{2,1,0:T(8,128)(2,1)}), bf16[64,8,1408]{2,1,0:T(8,128)(2,1)S(1)}, u32[]{:S(2)}, u32[]{:S(2)}) async-start(bf16[64,8,1408]{2,1,0:T(8,128)(2,1)} %bitcast.13), calls=%async_computation.4 | async-start | bytes 2883584 | tf_op jit(solution)/shard_map/all_to_all | solution.py:165
  138.2 33.1 %all-to-all-done.4 = bf16[64,8,1408]{2,1,0:T(8,128)(2,1)S(1)} async-done(((bf16[64,8,1408]{2,1,0:T(8,128)(2,1)}), bf16[64,8,1408]{2,1,0:T(8,128)(2,1)S(1)}, u32[]{:S(2)}, u32[]{:S(2)}) %all-to-all-start.4) | async-done | bytes 1441824 | tf_op jit(solution)/shard_map/all_to_all | solution.py:165
  171.3 0.0 copy-done.4
  171.3 1.5 fusion.1
  (4 shorter events, 0.1 us)
Async XLA Ops:
  26.9 9.2 %copy-start.1 = (bf16[1,128,1024]{2,1,0:T(8,128)(2,1)S(1)}, bf16[1,128,1024]{2,1,0:T(8,128)(2,1)}, u32[]{:S(2)}) copy-start(bf16[1,128,1024]{2,1,0:T(8,128)(2,1)} %param.15) | copy-start | bytes 786436
  26.9 27.4 %all-to-all-start.1 = ((bf16[4,8,2,16,1024]{4,3,2,1,0:T(8,128)(2,1)}), bf16[4,8,2,16,1024]{4,3,2,1,0:T(8,128)(2,1)S(1)}, u32[]{:S(2)}, u32[]{:S(2)}) async-start(bf16[4,8,2,16,1024]{4,3,2,1,0:T(8,128)(2,1)} %broadcast_in_dim.9), calls=%async_computation.1 | async-start | bytes 4194304 | tf_op jit(solution)/shard_map/all_to_all | solution.py:18
  31.8 18.7 %collective-permute-start = (bf16[8,2,16,1024]{3,2,1,0:T(8,128)(2,1)S(1)}, bf16[8,2,16,1024]{3,2,1,0:T(8,128)(2,1)}, u32[]{:S(2)}, u32[]{:S(2)}) collective-permute-start(bf16[8,2,16,1024]{3,2,1,0:T(8,128)(2,1)S(1)} %all_to_all.25), channel_id=1, source_target_pairs={{0,1},{1,0},{2,3},{3,2},{4,5},{5,4},{6,7},{7,6},{8,9},{9,8},{10,11... | collective-permute-start | bytes 1572872 | tf_op jit(solution)/shard_map/ppermute | solution.py:112
  36.0 14.4 %collective-permute-start.1 = (bf16[128,1024]{1,0:T(8,128)(2,1)S(1)}, bf16[128,1024]{1,0:T(8,128)(2,1)S(1)}, u32[]{:S(2)}, u32[]{:S(2)}) collective-permute-start(bf16[128,1024]{1,0:T(8,128)(2,1)S(1)} %bitcast.25), channel_id=1, source_target_pairs={{0,256},{64,320},{128,384},{192,448},{1,257},{65,321},{129,385},{1... | collective-permute-start | bytes 786440 | tf_op jit(solution)/shard_map/ppermute | solution.py:108
  56.9 6.6 %copy-start.2 = (bf16[1,128,1024]{2,1,0:T(8,128)(2,1)S(1)}, bf16[1,128,1024]{2,1,0:T(8,128)(2,1)}, u32[]{:S(2)}) copy-start(bf16[1,128,1024]{2,1,0:T(8,128)(2,1)} %param.16) | copy-start | bytes 786436
  56.9 18.9 %copy-start.3 = (s32[1,256,1]{1,2,0:T(1,128)S(1)}, s32[1,256,1]{1,2,0:T(1,128)}, u32[]{:S(2)}) copy-start(s32[1,256,1]{1,2,0:T(1,128)} %param.12) | copy-start | bytes 3076
  56.9 28.3 %copy-start = (bf16[1,256,1024]{2,1,0:T(8,128)(2,1)S(1)}, bf16[1,256,1024]{2,1,0:T(8,128)(2,1)}, u32[]{:S(2)}) copy-start(bf16[1,256,1024]{2,1,0:T(8,128)(2,1)} %param.10) | copy-start | bytes 1572868
  56.9 28.3 %all-to-all-start.2 = ((bf16[4,8,2,16,1024]{4,3,2,1,0:T(8,128)(2,1)}), bf16[4,8,2,16,1024]{4,3,2,1,0:T(8,128)(2,1)}, u32[]{:S(2)}, u32[]{:S(2)}) async-start(bf16[4,8,2,16,1024]{4,3,2,1,0:T(8,128)(2,1)} %broadcast_in_dim.10), calls=%async_computation.2 | async-start | bytes 4194304 | tf_op jit(solution)/shard_map/all_to_all | solution.py:18
  63.5 14.8 %collective-permute-start.2 = (bf16[128,1024]{1,0:T(8,128)(2,1)S(1)}, bf16[128,1024]{1,0:T(8,128)(2,1)}, u32[]{:S(2)}, u32[]{:S(2)}) collective-permute-start(bf16[128,1024]{1,0:T(8,128)(2,1)S(1)} %bitcast.27), channel_id=1, source_target_pairs={{0,256},{64,320},{128,384},{192,448},{1,257},{65,321},{129,385},{1... | collective-permute-start | bytes 786440 | tf_op jit(solution)/shard_map/ppermute | solution.py:109
  91.7 34.7 %all-to-all-start.3 = ((bf16[64,8,1024]{2,1,0:T(8,128)(2,1)}), bf16[64,8,1024]{2,1,0:T(8,128)(2,1)S(1)}, u32[]{:S(2)}, u32[]{:S(2)}) async-start(bf16[64,8,1024]{2,1,0:T(8,128)(2,1)} %bitcast.10), calls=%async_computation.3 | async-start | bytes 2097152 | tf_op jit(solution)/shard_map/all_to_all | solution.py:146
  131.3 39.9 %copy-start.4 = (f32[1,256]{1,0:T(1,128)S(1)}, f32[1,256]{1,0:T(1,128)}, u32[]{:S(2)}) copy-start(f32[1,256]{1,0:T(1,128)} %param.11) | copy-start | bytes 3076
  131.3 39.9 %all-to-all-start.4 = ((bf16[64,8,1408]{2,1,0:T(8,128)(2,1)}), bf16[64,8,1408]{2,1,0:T(8,128)(2,1)S(1)}, u32[]{:S(2)}, u32[]{:S(2)}) async-start(bf16[64,8,1408]{2,1,0:T(8,128)(2,1)} %bitcast.13), calls=%async_computation.4 | async-start | bytes 2883584 | tf_op jit(solution)/shard_map/all_to_all | solution.py:165

commit v7 on v6

--- a/solution.py
+++ b/solution.py
@@ -13,9 +13,12 @@
 PARAMS = pltpu.CompilerParams(vmem_limit_bytes=20 << 20)
 
 
+def widened(x, axis):
+    return jnp.broadcast_to(x[None], (lax.axis_size(axis), *x.shape))
+
+
 def gathered(x, axis):
-    peers = lax.axis_size(axis)
-    return lax.all_to_all(jnp.broadcast_to(x[None], (peers, *x.shape)), axis, 0, 0, tiled=True)
+    return lax.all_to_all(widened(x, axis), axis, 0, 0, tiled=True)
 
 
 def whole(mine, other, low, which):
@@ -70,15 +73,14 @@
     out[...] = jnp.where(used, sent, EMPTY).astype(jnp.bfloat16)
 
 
-def expert_kernel(capacity, received, weight, out, held, sems):
+def fetch_kernel(stored, held, sem):
+    copy = pltpu.make_async_copy(stored, held, sem)
+    copy.start()
+    copy.wait()
+
+
+def expert_kernel(capacity, received, weight, out):
     rows = received.shape[0]
-    units = weight.shape[1]
-    cuts = [0, units // 256 * 128, units]
-    copies = []
-    for k in range(2):
-        part = slice(cuts[k], cuts[k + 1])
-        copies.append(pltpu.make_async_copy(weight.at[:, part], held.at[:, part], sems.at[k]))
-        copies[k].start()
     filled = received[:, 0:128].astype(jnp.float32)[:, 0:1] < EMPTY / 2
     later = lax.broadcasted_iota(jnp.int32, (rows, rows), 0)
     sooner = lax.broadcasted_iota(jnp.int32, (rows, rows), 1)
@@ -86,11 +88,8 @@
     ones = jnp.where(jnp.broadcast_to(filled, (rows, 128)), 1.0, 0.0).astype(jnp.bfloat16)
     rank = jnp.dot(before, ones, preferred_element_type=jnp.float32)[:, 0:1]
     kept = filled & (rank < capacity[0].astype(jnp.float32))
-    for k in range(2):
-        part = slice(cuts[k], cuts[k + 1])
-        copies[k].wait()
-        hidden = jnp.dot(received[...], held[:, part], preferred_element_type=jnp.float32)
-        out[:, part] = jnp.where(kept, jnp.maximum(hidden, 0.0), 0.0).astype(jnp.bfloat16)
+    hidden = jnp.dot(received[...], weight[...], preferred_element_type=jnp.float32)
+    out[...] = jnp.where(kept, jnp.maximum(hidden, 0.0), 0.0).astype(jnp.bfloat16)
 
 
 def shards(
@@ -109,11 +108,12 @@
     values_far = lax.ppermute(mem_values[0], "section", across)
 
     spread = gathered(jnp.stack([q_weight[0], out_weight[0]]), "y")
+    spread, keys_far = lax.optimization_barrier((spread, keys_far))
     beside = lax.ppermute(spread, "z", [(0, 1), (1, 0)])
     mine = gathered(spread, "x")
-    mine, beside, keys_far = lax.optimization_barrier((mine, beside, keys_far))
-    other = gathered(beside, "x")
-    mine, other, values_far = lax.optimization_barrier((mine, other, values_far))
+    beside = widened(beside, "x")
+    mine, beside, values_far = lax.optimization_barrier((mine, beside, values_far))
+    other = lax.all_to_all(beside, "x", 0, 0, tiled=True)
 
     route = routes[0, :, 0]
     same = route[:, None] == route[None, :]
@@ -146,22 +146,23 @@
     received = lax.all_to_all(
         buffer.reshape(experts, cap, width), AXES, split_axis=0, concat_axis=0, tiled=True
     )
+    hidden_weight = pl.pallas_call(
+        fetch_kernel,
+        out_shape=jax.ShapeDtypeStruct(w_in.shape[2:], jnp.bfloat16),
+        in_specs=[pl.BlockSpec(memory_space=pltpu.HBM)],
+        out_specs=VMEM,
+        scratch_shapes=[pltpu.SemaphoreType.DMA(())],
+        compiler_params=PARAMS,
+        name="fetch",
+    )(pltpu.with_memory_space_constraint(w_in[0, 0], pltpu.HBM))
     acts = pl.pallas_call(
         expert_kernel,
         out_shape=jax.ShapeDtypeStruct((experts * cap, w_in.shape[-1]), jnp.bfloat16),
-        in_specs=[SMEM, VMEM, pl.BlockSpec(memory_space=pltpu.HBM)],
+        in_specs=[SMEM, VMEM, VMEM],
         out_specs=VMEM,
-        scratch_shapes=[
-            pltpu.VMEM(w_in.shape[2:], jnp.bfloat16),
-            pltpu.SemaphoreType.DMA((2,)),
-        ],
         compiler_params=PARAMS,
         name="expert",
-    )(
-        capacity[0],
-        received.reshape(experts * cap, width),
-        pltpu.with_memory_space_constraint(w_in[0, 0], pltpu.HBM),
-    )
+    )(capacity[0], received.reshape(experts * cap, width), hidden_weight)
     back = lax.all_to_all(
         acts.reshape(experts, cap, -1), AXES, split_axis=0, concat_axis=0, tiled=True
     )

time: 174 us -> 185 us (1.063)
  the two profiles are of different devices: /device:TPU:6 before, /device:TPU:136 now
where the time goes in v7:
time: 185 us; the launch traced here: 184 us
  waiting for transfers between devices  110 us (59%)
  starting transfers between devices  50.7 us (27%)
  Pallas kernels  11.5 us (6%)
  local copies, waits for them, and re-layouts  7.87 us (4%)
    all_to_all x1, waiting for transfers between devices, shards(): lax.all_to_all(acts.reshape(experts, cap, -1), AXES, split_axis=0, concat...  34.5 us
    all_to_all x1, waiting for transfers between devices, shards(): other = lax.all_to_all(beside, 'x', 0, 0, tiled=True)  24.8 us
    all_to_all x1, waiting for transfers between devices, shards(): lax.all_to_all(buffer.reshape(experts, cap, width), AXES, split_axis=0, c...  24.2 us
    ppermute x1, waiting for transfers between devices, shards(): values_far = lax.ppermute(mem_values[0], 'section', across)  14.3 us
    all_to_all x2, starting transfers between devices, gathered(): return lax.all_to_all(widened(x, axis), axis, 0, 0, tiled=True)  12 us
    ppermute x1, waiting for transfers between devices, shards(): keys_far = lax.ppermute(mem_keys[0], 'section', across)  10.6 us
    ppermute x1, starting transfers between devices, shards(): keys_far = lax.ppermute(mem_keys[0], 'section', across)  9.12 us
    all_to_all x1, starting transfers between devices, shards(): lax.all_to_all(buffer.reshape(experts, cap, width), AXES, split_axis=0, c...  8.56 us
  transfers between devices with their start and end apart: 8, of which 6 were waited for; matrix products, arithmetic and copies ran while one was open for 0% of the time, Pallas kernels for 1%

profile of v7, /device:TPU:136, one launch (start us, length us, event | category | flops | bytes accessed | tf_op | source)
XLA Modules:
  0.0 183.7 jit_solution(1169281275727679170)
XLA Ops:
  0.0 0.8 pad_maximum_fusion
  0.8 0.9 broadcast_in_dim.8
  1.7 7.5 %all-to-all-start = ((bf16[8,2,16,1024]{3,2,1,0:T(8,128)(2,1)}), bf16[8,2,16,1024]{3,2,1,0:T(8,128)(2,1)S(1)}, u32[]{:S(2)}, u32[]{:S(2)}) async-start(bf16[8,2,16,1024]{3,2,1,0:T(8,128)(2,1)} %broadcast_in_dim.8), calls=%async_computation | async-start | bytes 1048576 | tf_op jit(solution)/shard_map/all_to_all | solution.py:21
  9.2 0.0 copy-done.2
  9.2 9.1 %collective-permute-start = (bf16[128,1024]{1,0:T(8,128)(2,1)S(1)}, bf16[128,1024]{1,0:T(8,128)(2,1)S(1)}, u32[]{:S(2)}, u32[]{:S(2)}) collective-permute-start(bf16[128,1024]{1,0:T(8,128)(2,1)S(1)} %bitcast.25), channel_id=1, source_target_pairs={{0,256},{64,320},{128,384},{192,448},{1,257},{65,321},{129,385},{1... | collective-permute-start | bytes 786440 | tf_op jit(solution)/shard_map/ppermute | solution.py:107
  18.4 10.6 %collective-permute-done.keys_far = bf16[128,1024]{1,0:T(8,128)(2,1)S(1)} collective-permute-done((bf16[128,1024]{1,0:T(8,128)(2,1)S(1)}, bf16[128,1024]{1,0:T(8,128)(2,1)S(1)}, u32[]{:S(2)}, u32[]{:S(2)}) %collective-permute-start) | collective-permute-done | bytes 262176 | tf_op jit(solution)/shard_map/ppermute | solution.py:107
  28.9 0.0 all-to-all-done
  28.9 1.6 broadcast_in_dim.9
  30.5 4.4 %all-to-all-start.1 = ((bf16[4,8,2,16,1024]{4,3,2,1,0:T(8,128)(2,1)}), bf16[4,8,2,16,1024]{4,3,2,1,0:T(8,128)(2,1)S(1)}, u32[]{:S(2)}, u32[]{:S(2)}) async-start(bf16[4,8,2,16,1024]{4,3,2,1,0:T(8,128)(2,1)} %broadcast_in_dim.9), calls=%async_computation.1 | async-start | bytes 4194304 | tf_op jit(solution)/shard_map/all_to_all | solution.py:21
  35.0 1.9 %collective-permute-start.1 = (bf16[8,2,16,1024]{3,2,1,0:T(8,128)(2,1)S(1)}, bf16[8,2,16,1024]{3,2,1,0:T(8,128)(2,1)}, u32[]{:S(2)}, u32[]{:S(2)}) collective-permute-start(bf16[8,2,16,1024]{3,2,1,0:T(8,128)(2,1)S(1)} %all-to-all-done), channel_id=1, source_target_pairs={{0,1},{1,0},{2,3},{3,2},{4,5},{5,4},{6,7},{7,6},{8,9},{9,8},{10,11... | collective-permute-start | bytes 1572872 | tf_op jit(solution)/shard_map/ppermute | solution.py:112
  36.9 0.0 copy-done.3
  36.9 8.3 %collective-permute-start.2 = (bf16[128,1024]{1,0:T(8,128)(2,1)S(1)}, bf16[128,1024]{1,0:T(8,128)(2,1)S(1)}, u32[]{:S(2)}, u32[]{:S(2)}) collective-permute-start(bf16[128,1024]{1,0:T(8,128)(2,1)S(1)} %bitcast.27), channel_id=1, source_target_pairs={{0,256},{64,320},{128,384},{192,448},{1,257},{65,321},{129,385},{1... | collective-permute-start | bytes 786440 | tf_op jit(solution)/shard_map/ppermute | solution.py:108
  45.2 14.3 %collective-permute-done.2.values_far = bf16[128,1024]{1,0:T(8,128)(2,1)S(1)} collective-permute-done((bf16[128,1024]{1,0:T(8,128)(2,1)S(1)}, bf16[128,1024]{1,0:T(8,128)(2,1)S(1)}, u32[]{:S(2)}, u32[]{:S(2)}) %collective-permute-start.2) | collective-permute-done | bytes 262176 | tf_op jit(solution)/shard_map/ppermute | solution.py:108
  59.5 0.7 copy-done.4
  60.2 0.0 collective-permute-done.1
  60.2 1.3 all-to-all-done.1.mine
  61.5 2.6 %broadcast_in_dim.10 = bf16[4,8,2,16,1024]{4,3,2,1,0:T(8,128)(2,1)} broadcast(bf16[8,2,16,1024]{3,2,1,0:T(8,128)(2,1)} %collective-permute-done.1), dimensions={1,2,3,4} | broadcast | bytes 2621440 | tf_op jit(solution)/shard_map/broadcast_in_dim | solution.py:17
  64.1 4.6 %all-to-all-start.2 = ((bf16[4,8,2,16,1024]{4,3,2,1,0:T(8,128)(2,1)}), bf16[4,8,2,16,1024]{4,3,2,1,0:T(8,128)(2,1)}, u32[]{:S(2)}, u32[]{:S(2)}) async-start(bf16[4,8,2,16,1024]{4,3,2,1,0:T(8,128)(2,1)} %broadcast_in_dim.10), calls=%async_computation.2 | async-start | bytes 4194304 | tf_op jit(solution)/shard_map/all_to_all | solution.py:116
  69.4 0.1 pad_add_fusion.facts
  69.4 0.0 copy-done.6
  69.4 0.2 convert_reduce_fusion
  69.6 24.8 %all-to-all-done.2.other = bf16[4,8,2,16,1024]{4,3,2,1,0:T(8,128)(2,1)} async-done(((bf16[4,8,2,16,1024]{4,3,2,1,0:T(8,128)(2,1)}), bf16[4,8,2,16,1024]{4,3,2,1,0:T(8,128)(2,1)}, u32[]{:S(2)}, u32[]{:S(2)}) %all-to-all-start.2) | async-done | bytes 2097184 | tf_op jit(solution)/shard_map/all_to_all | solution.py:116
  94.4 0.9 copy-done.5
  95.3 6.4 %decode.1 = bf16[512,1024]{1,0:T(8,128)(2,1)} custom-call(s32[3]{0:T(128)S(1)} %pad_add_fusion.facts, bf16[256,1024]{1,0:T(8,128)(2,1)S(1)} %bitcast.24, bf16[128,1024]{1,0:T(8,128)(2,1)S(1)} %collective-permute-done.keys_far, bf16[128,1024]{1,0:T(8,128)(2,1)S(1)} %bitcast.26, bf16[128,1024]{1,0:T(8,128)(2,1)S(1)} %copy-done.5, ...), custom_call_target="tpu_custom_call" | custom-call | tf_op jit(solution)/shard_map/decode/pallas_call | solution.py:127
  101.8 8.6 %all-to-all-start.3 = ((bf16[64,8,1024]{2,1,0:T(8,128)(2,1)}), bf16[64,8,1024]{2,1,0:T(8,128)(2,1)}, u32[]{:S(2)}, u32[]{:S(2)}) async-start(bf16[64,8,1024]{2,1,0:T(8,128)(2,1)} %bitcast.10), calls=%async_computation.3 | async-start | bytes 2097152 | tf_op jit(solution)/shard_map/all_to_all | solution.py:146
  110.4 1.8 fetch.1.weight
  112.8 24.2 %all-to-all-done.3 = bf16[64,8,1024]{2,1,0:T(8,128)(2,1)} async-done(((bf16[64,8,1024]{2,1,0:T(8,128)(2,1)}), bf16[64,8,1024]{2,1,0:T(8,128)(2,1)}, u32[]{:S(2)}, u32[]{:S(2)}) %all-to-all-start.3) | async-done | bytes 1048608 | tf_op jit(solution)/shard_map/all_to_all | solution.py:146
  137.0 3.3 %expert.1 = bf16[512,1408]{1,0:T(8,128)(2,1)S(1)} custom-call(s32[1]{0:T(128)} %bitcast.21.capacity, bf16[512,1024]{1,0:T(8,128)(2,1)} %bitcast.11.received, bf16[1024,1408]{1,0:T(8,128)(2,1)S(1)} %fetch.1.weight), custom_call_target="tpu_custom_call" | custom-call | tf_op jit(solution)/shard_map/expert/pallas_call | solution.py:158
  140.3 1.1 copy-done
  141.4 6.2 %all-to-all-start.4 = ((bf16[64,8,1408]{2,1,0:T(8,128)(2,1)}), bf16[64,8,1408]{2,1,0:T(8,128)(2,1)S(1)}, u32[]{:S(2)}, u32[]{:S(2)}) async-start(bf16[64,8,1408]{2,1,0:T(8,128)(2,1)} %bitcast.23), calls=%async_computation.4 | async-start | bytes 2883584 | tf_op jit(solution)/shard_map/all_to_all | solution.py:166
  147.7 34.5 %all-to-all-done.4 = bf16[64,8,1408]{2,1,0:T(8,128)(2,1)S(1)} async-done(((bf16[64,8,1408]{2,1,0:T(8,128)(2,1)}), bf16[64,8,1408]{2,1,0:T(8,128)(2,1)S(1)}, u32[]{:S(2)}, u32[]{:S(2)}) %all-to-all-start.4) | async-done | bytes 1441824 | tf_op jit(solution)/shard_map/all_to_all | solution.py:166
  182.2 1.5 fusion.1
  (12 shorter events, 0.0 us)
Async XLA Ops:
  0.0 9.2 %copy-start.2 = (bf16[1,128,1024]{2,1,0:T(8,128)(2,1)S(1)}, bf16[1,128,1024]{2,1,0:T(8,128)(2,1)}, u32[]{:S(2)}) copy-start(bf16[1,128,1024]{2,1,0:T(8,128)(2,1)} %param.15) | copy-start | bytes 786436
  1.7 27.2 %all-to-all-start = ((bf16[8,2,16,1024]{3,2,1,0:T(8,128)(2,1)}), bf16[8,2,16,1024]{3,2,1,0:T(8,128)(2,1)S(1)}, u32[]{:S(2)}, u32[]{:S(2)}) async-start(bf16[8,2,16,1024]{3,2,1,0:T(8,128)(2,1)} %broadcast_in_dim.8), calls=%async_computation | async-start | bytes 1048576 | tf_op jit(solution)/shard_map/all_to_all | solution.py:21
  9.2 19.7 %collective-permute-start = (bf16[128,1024]{1,0:T(8,128)(2,1)S(1)}, bf16[128,1024]{1,0:T(8,128)(2,1)S(1)}, u32[]{:S(2)}, u32[]{:S(2)}) collective-permute-start(bf16[128,1024]{1,0:T(8,128)(2,1)S(1)} %bitcast.25), channel_id=1, source_target_pairs={{0,256},{64,320},{128,384},{192,448},{1,257},{65,321},{129,385},{1... | collective-permute-start | bytes 786440 | tf_op jit(solution)/shard_map/ppermute | solution.py:107
  30.5 6.3 %copy-start.3 = (bf16[1,128,1024]{2,1,0:T(8,128)(2,1)S(1)}, bf16[1,128,1024]{2,1,0:T(8,128)(2,1)}, u32[]{:S(2)}) copy-start(bf16[1,128,1024]{2,1,0:T(8,128)(2,1)} %param.16) | copy-start | bytes 786436
  30.5 30.9 %all-to-all-start.1 = ((bf16[4,8,2,16,1024]{4,3,2,1,0:T(8,128)(2,1)}), bf16[4,8,2,16,1024]{4,3,2,1,0:T(8,128)(2,1)S(1)}, u32[]{:S(2)}, u32[]{:S(2)}) async-start(bf16[4,8,2,16,1024]{4,3,2,1,0:T(8,128)(2,1)} %broadcast_in_dim.9), calls=%async_computation.1 | async-start | bytes 4194304 | tf_op jit(solution)/shard_map/all_to_all | solution.py:21
  35.0 25.2 %collective-permute-start.1 = (bf16[8,2,16,1024]{3,2,1,0:T(8,128)(2,1)S(1)}, bf16[8,2,16,1024]{3,2,1,0:T(8,128)(2,1)}, u32[]{:S(2)}, u32[]{:S(2)}) collective-permute-start(bf16[8,2,16,1024]{3,2,1,0:T(8,128)(2,1)S(1)} %all-to-all-done), channel_id=1, source_target_pairs={{0,1},{1,0},{2,3},{3,2},{4,5},{5,4},{6,7},{7,6},{8,9},{9,8},{10,11... | collective-permute-start | bytes 1572872 | tf_op jit(solution)/shard_map/ppermute | solution.py:112
  36.9 22.6 %collective-permute-start.2 = (bf16[128,1024]{1,0:T(8,128)(2,1)S(1)}, bf16[128,1024]{1,0:T(8,128)(2,1)S(1)}, u32[]{:S(2)}, u32[]{:S(2)}) collective-permute-start(bf16[128,1024]{1,0:T(8,128)(2,1)S(1)} %bitcast.27), channel_id=1, source_target_pairs={{0,256},{64,320},{128,384},{192,448},{1,257},{65,321},{129,385},{1... | collective-permute-start | bytes 786440 | tf_op jit(solution)/shard_map/ppermute | solution.py:108
  59.5 0.7 copy-start.4
  64.1 5.3 %copy-start.6 = (s32[1,256,1]{1,2,0:T(1,128)S(1)}, s32[1,256,1]{1,2,0:T(1,128)}, u32[]{:S(2)}) copy-start(s32[1,256,1]{1,2,0:T(1,128)} %param.12) | copy-start | bytes 3076
  64.1 30.3 %copy-start.1 = (bf16[1,256,1024]{2,1,0:T(8,128)(2,1)S(1)}, bf16[1,256,1024]{2,1,0:T(8,128)(2,1)}, u32[]{:S(2)}) copy-start(bf16[1,256,1024]{2,1,0:T(8,128)(2,1)} %param.10) | copy-start | bytes 1572868
  64.1 30.3 %all-to-all-start.2 = ((bf16[4,8,2,16,1024]{4,3,2,1,0:T(8,128)(2,1)}), bf16[4,8,2,16,1024]{4,3,2,1,0:T(8,128)(2,1)}, u32[]{:S(2)}, u32[]{:S(2)}) async-start(bf16[4,8,2,16,1024]{4,3,2,1,0:T(8,128)(2,1)} %broadcast_in_dim.10), calls=%async_computation.2 | async-start | bytes 4194304 | tf_op jit(solution)/shard_map/all_to_all | solution.py:116
  94.4 1.0 copy-start.5
  101.8 35.2 %all-to-all-start.3 = ((bf16[64,8,1024]{2,1,0:T(8,128)(2,1)}), bf16[64,8,1024]{2,1,0:T(8,128)(2,1)}, u32[]{:S(2)}, u32[]{:S(2)}) async-start(bf16[64,8,1024]{2,1,0:T(8,128)(2,1)} %bitcast.10), calls=%async_computation.3 | async-start | bytes 2097152 | tf_op jit(solution)/shard_map/all_to_all | solution.py:146
  140.3 1.1 copy-start
  141.4 40.8 %copy-start.7 = (f32[1,256]{1,0:T(1,128)S(1)}, f32[1,256]{1,0:T(1,128)}, u32[]{:S(2)}) copy-start(f32[1,256]{1,0:T(1,128)} %param.11) | copy-start | bytes 3076
  141.4 40.8 %all-to-all-start.4 = ((bf16[64,8,1408]{2,1,0:T(8,128)(2,1)}), bf16[64,8,1408]{2,1,0:T(8,128)(2,1)S(1)}, u32[]{:S(2)}, u32[]{:S(2)}) async-start(bf16[64,8,1408]{2,1,0:T(8,128)(2,1)} %bitcast.23), calls=%async_computation.4 | async-start | bytes 2883584 | tf_op jit(solution)/shard_map/all_to_all | solution.py:166

commit v8 on v7

--- a/solution.py
+++ b/solution.py
@@ -11,10 +11,28 @@
 VMEM = pl.BlockSpec(memory_space=pltpu.VMEM)
 SMEM = pl.BlockSpec(memory_space=pltpu.SMEM)
 PARAMS = pltpu.CompilerParams(vmem_limit_bytes=20 << 20)
+SMALL = pltpu.CompilerParams(vmem_limit_bytes=4 << 20)
+
+
+def widen_kernel(x, out, sems):
+    copies = [pltpu.make_async_copy(x, out.at[i], sems.at[i]) for i in range(out.shape[0])]
+    for copy in copies:
+        copy.start()
+    for copy in copies:
+        copy.wait()
 
 
 def widened(x, axis):
-    return jnp.broadcast_to(x[None], (lax.axis_size(axis), *x.shape))
+    peers = lax.axis_size(axis)
+    return pl.pallas_call(
+        widen_kernel,
+        out_shape=jax.ShapeDtypeStruct((peers, *x.shape), x.dtype),
+        in_specs=[pl.BlockSpec(memory_space=pl.ANY)],
+        out_specs=pl.BlockSpec(memory_space=pltpu.HBM),
+        scratch_shapes=[pltpu.SemaphoreType.DMA((peers,))],
+        compiler_params=SMALL,
+        name="widen",
+    )(x)
 
 
 def gathered(x, axis):
@@ -42,6 +60,8 @@
     span = keys_far.shape[0] + keys_near.shape[0]
     valid = lax.broadcasted_iota(jnp.int32, (rows, span), 1) < length
     lane = lax.broadcasted_iota(jnp.int32, (rows, slab), 1)
+    lane_all = lax.broadcasted_iota(jnp.int32, (span, slab), 1)
+    here_all = [(lane_all >= h * dim) & (lane_all < (h + 1) * dim) for h in range(slab // dim)]
     for p in range(width // slab):
         part = slice(p * slab, (p + 1) * slab)
         keys = jnp.concatenate([keys_far[:, part], keys_near[:, part]], axis=0)
@@ -56,9 +76,10 @@
             ) * (dim**-0.5)
             scores = jnp.where(valid, scores, -1e30)
             weights = jnp.exp(scores - jnp.max(scores, axis=1, keepdims=True))
-            probs = weights * (1.0 / jnp.sum(weights, axis=1, keepdims=True))
-            seen = jnp.dot(probs.astype(jnp.bfloat16), values, preferred_element_type=jnp.float32)
-            found = jnp.where(here, seen, found)
+            columns = jnp.where(here_all[h], values, jnp.ones_like(values))
+            seen = jnp.dot(weights.astype(jnp.bfloat16), columns, preferred_element_type=jnp.float32)
+            sums = pltpu.roll(seen, dim, 1)
+            found = jnp.where(here, seen / sums, found)
         context[:, part] = found.astype(jnp.bfloat16)
     total = jnp.dot(
         context[...], whole(mine, other, low, 1), preferred_element_type=jnp.float32
@@ -74,13 +95,16 @@
 
 
 def fetch_kernel(stored, held, sem):
-    copy = pltpu.make_async_copy(stored, held, sem)
+    copy = pltpu.make_async_copy(stored.at[:, 0 : held.shape[1]], held, sem)
     copy.start()
     copy.wait()
 
 
-def expert_kernel(capacity, received, weight, out):
-    rows = received.shape[0]
+def expert_kernel(capacity, received, first, stored, out, rest, acts, sems):
+    rows, units = acts.shape
+    cut = first.shape[1]
+    loading = pltpu.make_async_copy(stored.at[:, cut:units], rest, sems.at[0])
+    loading.start()
     filled = received[:, 0:128].astype(jnp.float32)[:, 0:1] < EMPTY / 2
     later = lax.broadcasted_iota(jnp.int32, (rows, rows), 0)
     sooner = lax.broadcasted_iota(jnp.int32, (rows, rows), 1)
@@ -88,8 +112,17 @@
     ones = jnp.where(jnp.broadcast_to(filled, (rows, 128)), 1.0, 0.0).astype(jnp.bfloat16)
     rank = jnp.dot(before, ones, preferred_element_type=jnp.float32)[:, 0:1]
     kept = filled & (rank < capacity[0].astype(jnp.float32))
-    hidden = jnp.dot(received[...], weight[...], preferred_element_type=jnp.float32)
-    out[...] = jnp.where(kept, jnp.maximum(hidden, 0.0), 0.0).astype(jnp.bfloat16)
+    storing = []
+    for k, weight in enumerate((first, rest)):
+        part = slice(k * cut, k * cut + weight.shape[1])
+        if k == 1:
+            loading.wait()
+        hidden = jnp.dot(received[...], weight[...], preferred_element_type=jnp.float32)
+        acts[:, part] = jnp.where(kept, jnp.maximum(hidden, 0.0), 0.0).astype(jnp.bfloat16)
+        storing.append(pltpu.make_async_copy(acts.at[:, part], out.at[:, part], sems.at[1 + k]))
+        storing[k].start()
+    for copy in storing:
+        copy.wait()
 
 
 def shards(
@@ -108,12 +141,11 @@
     values_far = lax.ppermute(mem_values[0], "section", across)
 
     spread = gathered(jnp.stack([q_weight[0], out_weight[0]]), "y")
-    spread, keys_far = lax.optimization_barrier((spread, keys_far))
     beside = lax.ppermute(spread, "z", [(0, 1), (1, 0)])
     mine = gathered(spread, "x")
-    beside = widened(beside, "x")
-    mine, beside, values_far = lax.optimization_barrier((mine, beside, values_far))
-    other = lax.all_to_all(beside, "x", 0, 0, tiled=True)
+    mine, beside, keys_far = lax.optimization_barrier((mine, beside, keys_far))
+    other = gathered(beside, "x")
+    mine, other, values_far = lax.optimization_barrier((mine, other, values_far))
 
     route = routes[0, :, 0]
     same = route[:, None] == route[None, :]
@@ -146,23 +178,31 @@
     received = lax.all_to_all(
         buffer.reshape(experts, cap, width), AXES, split_axis=0, concat_axis=0, tiled=True
     )
-    hidden_weight = pl.pallas_call(
+    units = w_in.shape[-1]
+    cut = units // 256 * 128
+    stored = pltpu.with_memory_space_constraint(w_in[0, 0], pltpu.HBM)
+    first = pl.pallas_call(
         fetch_kernel,
-        out_shape=jax.ShapeDtypeStruct(w_in.shape[2:], jnp.bfloat16),
+        out_shape=jax.ShapeDtypeStruct((width, cut), jnp.bfloat16),
         in_specs=[pl.BlockSpec(memory_space=pltpu.HBM)],
         out_specs=VMEM,
         scratch_shapes=[pltpu.SemaphoreType.DMA(())],
-        compiler_params=PARAMS,
+        compiler_params=SMALL,
         name="fetch",
-    )(pltpu.with_memory_space_constraint(w_in[0, 0], pltpu.HBM))
+    )(stored)
     acts = pl.pallas_call(
         expert_kernel,
-        out_shape=jax.ShapeDtypeStruct((experts * cap, w_in.shape[-1]), jnp.bfloat16),
-        in_specs=[SMEM, VMEM, VMEM],
-        out_specs=VMEM,
+        out_shape=pltpu.HBM((experts * cap, units), jnp.bfloat16),
+        in_specs=[SMEM, VMEM, VMEM, pl.BlockSpec(memory_space=pltpu.HBM)],
+        out_specs=pl.BlockSpec(memory_space=pltpu.HBM),
+        scratch_shapes=[
+            pltpu.VMEM((width, units - cut), jnp.bfloat16),
+            pltpu.VMEM((experts * cap, units), jnp.bfloat16),
+            pltpu.SemaphoreType.DMA((3,)),
+        ],
         compiler_params=PARAMS,
         name="expert",
-    )(capacity[0], received.reshape(experts * cap, width), hidden_weight)
+    )(capacity[0], received.reshape(experts * cap, width), first, stored)
     back = lax.all_to_all(
         acts.reshape(experts, cap, -1), AXES, split_axis=0, concat_axis=0, tiled=True
     )

time: 185 us -> 176 us (0.951)
  the two profiles are of different devices: /device:TPU:136 before, /device:TPU:6 now
where the time goes in v8:
time: 176 us; the launch traced here: 174 us
  waiting for transfers between devices  73.1 us (42%)
  starting transfers between devices  53.5 us (30%)
  blocking collectives  24.4 us (14%)
  Pallas kernels  18.6 us (11%)
    all_to_all x1, waiting for transfers between devices, shards(): lax.all_to_all(acts.reshape(experts, cap, -1), AXES, split_axis=0, concat...  33.1 us
    all_to_all x1, blocking collectives, gathered(): return lax.all_to_all(widened(x, axis), axis, 0, 0, tiled=True)  24.4 us
    all_to_all x1, waiting for transfers between devices, shards(): lax.all_to_all(buffer.reshape(experts, cap, width), AXES, split_axis=0, c...  23.4 us
    ppermute x1, starting transfers between devices, shards(): values_far = lax.ppermute(mem_values[0], 'section', across)  11.6 us
    all_to_all x2, starting transfers between devices, gathered(): return lax.all_to_all(widened(x, axis), axis, 0, 0, tiled=True)  11.5 us
    ppermute x1, starting transfers between devices, shards(): keys_far = lax.ppermute(mem_keys[0], 'section', across)  10 us
    all_to_all x2, waiting for transfers between devices, gathered(): return lax.all_to_all(widened(x, axis), axis, 0, 0, tiled=True)  9.94 us
    all_to_all x1, starting transfers between devices, shards(): lax.all_to_all(buffer.reshape(experts, cap, width), AXES, split_axis=0, c...  9.29 us
  transfers between devices with their start and end apart: 7, of which 6 were waited for; matrix products, arithmetic and copies ran while one was open for 0% of the time, Pallas kernels for 1%

profile of v8, /device:TPU:6, one launch (start us, length us, event | category | flops | bytes accessed | tf_op | source)
XLA Modules:
  0.0 174.3 jit_solution(8100598822326690625)
XLA Ops:
  0.0 0.8 pad_maximum_fusion.x
  0.8 0.8 widen.3
  1.5 24.4 %all_to_all.25.x = bf16[8,2,16,1024]{3,2,1,0:T(8,128)(2,1)S(1)} all-to-all(bf16[8,2,16,1024]{3,2,1,0:T(8,128)(2,1)S(1)} %widen.3), channel_id=1, replica_groups=mesh['section'=8,'y'=8,'x'=4,'z'=2] {'y'}, dimensions={0} | all-to-all | bytes 1048576 | tf_op jit(solution)/shard_map/all_to_all | solution.py:39
  25.9 1.4 widen.4
  27.3 0.0 copy-start.1
  27.3 4.9 %all-to-all-start.1 = ((bf16[4,8,2,16,1024]{4,3,2,1,0:T(8,128)(2,1)}), bf16[4,8,2,16,1024]{4,3,2,1,0:T(8,128)(2,1)S(1)}, u32[]{:S(2)}, u32[]{:S(2)}) async-start(bf16[4,8,2,16,1024]{4,3,2,1,0:T(8,128)(2,1)} %widen.4), calls=%async_computation.1 | async-start | bytes 4194304 | tf_op jit(solution)/shard_map/all_to_all | solution.py:39
  32.2 4.3 %collective-permute-start = (bf16[8,2,16,1024]{3,2,1,0:T(8,128)(2,1)S(1)}, bf16[8,2,16,1024]{3,2,1,0:T(8,128)(2,1)S(1)}, u32[]{:S(2)}, u32[]{:S(2)}) collective-permute-start(bf16[8,2,16,1024]{3,2,1,0:T(8,128)(2,1)S(1)} %all_to_all.25.x), channel_id=1, source_target_pairs={{0,1},{1,0},{2,3},{3,2},{4,5},{5,4},{6,7},{7,6},{8,9},{9,8},{10,11... | collective-permute-start | bytes 1572872 | tf_op jit(solution)/shard_map/ppermute | solution.py:144
  36.5 10.0 %collective-permute-start.1 = (bf16[128,1024]{1,0:T(8,128)(2,1)S(1)}, bf16[128,1024]{1,0:T(8,128)(2,1)S(1)}, u32[]{:S(2)}, u32[]{:S(2)}) collective-permute-start(bf16[128,1024]{1,0:T(8,128)(2,1)S(1)} %bitcast.25), channel_id=1, source_target_pairs={{0,256},{64,320},{128,384},{192,448},{1,257},{65,321},{129,385},{1... | collective-permute-start | bytes 786440 | tf_op jit(solution)/shard_map/ppermute | solution.py:140
  46.6 4.4 %collective-permute-done.1.keys_far = bf16[128,1024]{1,0:T(8,128)(2,1)S(1)} collective-permute-done((bf16[128,1024]{1,0:T(8,128)(2,1)S(1)}, bf16[128,1024]{1,0:T(8,128)(2,1)S(1)}, u32[]{:S(2)}, u32[]{:S(2)}) %collective-permute-start.1) | collective-permute-done | bytes 262176 | tf_op jit(solution)/shard_map/ppermute | solution.py:140
  51.0 0.7 copy-done.3
  51.7 0.0 collective-permute-done.x
  51.7 3.1 %all-to-all-done.1.mine = bf16[4,8,2,16,1024]{4,3,2,1,0:T(8,128)(2,1)S(1)} async-done(((bf16[4,8,2,16,1024]{4,3,2,1,0:T(8,128)(2,1)}), bf16[4,8,2,16,1024]{4,3,2,1,0:T(8,128)(2,1)S(1)}, u32[]{:S(2)}, u32[]{:S(2)}) %all-to-all-start.1) | async-done | bytes 2097184 | tf_op jit(solution)/shard_map/all_to_all | solution.py:39
  54.7 1.4 widen.5
  56.1 0.0 copy-start.2
  56.1 0.0 copy-start.5
  56.1 0.0 copy-start
  56.1 0.0 copy-start.4
  56.1 6.6 %all-to-all-start.2 = ((bf16[4,8,2,16,1024]{4,3,2,1,0:T(8,128)(2,1)}), bf16[4,8,2,16,1024]{4,3,2,1,0:T(8,128)(2,1)}, u32[]{:S(2)}, u32[]{:S(2)}) async-start(bf16[4,8,2,16,1024]{4,3,2,1,0:T(8,128)(2,1)} %widen.5), calls=%async_computation.2 | async-start | bytes 4194304 | tf_op jit(solution)/shard_map/all_to_all | solution.py:39
  62.7 11.6 %collective-permute-start.2 = (bf16[128,1024]{1,0:T(8,128)(2,1)S(1)}, bf16[128,1024]{1,0:T(8,128)(2,1)}, u32[]{:S(2)}, u32[]{:S(2)}) collective-permute-start(bf16[128,1024]{1,0:T(8,128)(2,1)S(1)} %bitcast.27), channel_id=1, source_target_pairs={{0,256},{64,320},{128,384},{192,448},{1,257},{65,321},{129,385},{1... | collective-permute-start | bytes 786440 | tf_op jit(solution)/shard_map/ppermute | solution.py:141
  75.0 0.2 convert_reduce_fusion
  75.2 0.1 pad_add_fusion.facts
  75.3 2.3 %collective-permute-done.2.values_far = bf16[128,1024]{1,0:T(8,128)(2,1)} collective-permute-done((bf16[128,1024]{1,0:T(8,128)(2,1)S(1)}, bf16[128,1024]{1,0:T(8,128)(2,1)}, u32[]{:S(2)}, u32[]{:S(2)}) %collective-permute-start.2) | collective-permute-done | bytes 262176 | tf_op jit(solution)/shard_map/ppermute | solution.py:141
  77.5 6.9 %all-to-all-done.2.other = bf16[4,8,2,16,1024]{4,3,2,1,0:T(8,128)(2,1)} async-done(((bf16[4,8,2,16,1024]{4,3,2,1,0:T(8,128)(2,1)}), bf16[4,8,2,16,1024]{4,3,2,1,0:T(8,128)(2,1)}, u32[]{:S(2)}, u32[]{:S(2)}) %all-to-all-start.2) | async-done | bytes 2097184 | tf_op jit(solution)/shard_map/all_to_all | solution.py:39
  84.4 8.8 %decode.1 = bf16[512,1024]{1,0:T(8,128)(2,1)} custom-call(s32[3]{0:T(128)S(1)} %pad_add_fusion.facts, bf16[256,1024]{1,0:T(8,128)(2,1)S(1)} %bitcast.24, bf16[128,1024]{1,0:T(8,128)(2,1)S(1)} %copy-done.4, bf16[128,1024]{1,0:T(8,128)(2,1)S(1)} %bitcast.26, bf16[128,1024]{1,0:T(8,128)(2,1)} %collective-permute-done.2.values_far, ...), custom_call_target="tpu_custom_call" | custom-call | tf_op jit(solution)/shard_map/decode/pallas_call | solution.py:159
  93.2 9.3 %all-to-all-start.3 = ((bf16[64,8,1024]{2,1,0:T(8,128)(2,1)}), bf16[64,8,1024]{2,1,0:T(8,128)(2,1)S(1)}, u32[]{:S(2)}, u32[]{:S(2)}) async-start(bf16[64,8,1024]{2,1,0:T(8,128)(2,1)} %bitcast.10), calls=%async_computation.3 | async-start | bytes 2097152 | tf_op jit(solution)/shard_map/all_to_all | solution.py:178
  102.5 1.3 fetch.1.first
  104.5 23.4 %all-to-all-done.3 = bf16[64,8,1024]{2,1,0:T(8,128)(2,1)S(1)} async-done(((bf16[64,8,1024]{2,1,0:T(8,128)(2,1)}), bf16[64,8,1024]{2,1,0:T(8,128)(2,1)S(1)}, u32[]{:S(2)}, u32[]{:S(2)}) %all-to-all-start.3) | async-done | bytes 1048608 | tf_op jit(solution)/shard_map/all_to_all | solution.py:178
  127.9 4.9 %expert.1 = bf16[512,1408]{1,0:T(8,128)(2,1)} custom-call(s32[1]{0:T(128)} %bitcast.21.capacity, bf16[512,1024]{1,0:T(8,128)(2,1)S(1)} %bitcast.23, bf16[1024,640]{1,0:T(8,128)(2,1)S(1)} %fetch.1.first, bf16[1024,1408]{1,0:T(8,128)(2,1)} %bitcast.30), custom_call_target="tpu_custom_call" | custom-call | tf_op jit(solution)/shard_map/expert/pallas_call | solution.py:193
  132.8 0.0 copy-start.6
  132.9 6.8 %all-to-all-start.4 = ((bf16[64,8,1408]{2,1,0:T(8,128)(2,1)}), bf16[64,8,1408]{2,1,0:T(8,128)(2,1)S(1)}, u32[]{:S(2)}, u32[]{:S(2)}) async-start(bf16[64,8,1408]{2,1,0:T(8,128)(2,1)} %bitcast.31), calls=%async_computation.4 | async-start | bytes 2883584 | tf_op jit(solution)/shard_map/all_to_all | solution.py:206
  139.7 33.1 %all-to-all-done.4 = bf16[64,8,1408]{2,1,0:T(8,128)(2,1)S(1)} async-done(((bf16[64,8,1408]{2,1,0:T(8,128)(2,1)}), bf16[64,8,1408]{2,1,0:T(8,128)(2,1)S(1)}, u32[]{:S(2)}, u32[]{:S(2)}) %all-to-all-start.4) | async-done | bytes 1441824 | tf_op jit(solution)/shard_map/all_to_all | solution.py:206
  172.8 1.5 fusion.1
  (9 shorter events, 0.0 us)
Async XLA Ops:
  27.3 9.2 %copy-start.1 = (bf16[1,128,1024]{2,1,0:T(8,128)(2,1)S(1)}, bf16[1,128,1024]{2,1,0:T(8,128)(2,1)}, u32[]{:S(2)}) copy-start(bf16[1,128,1024]{2,1,0:T(8,128)(2,1)} %param.15) | copy-start | bytes 786436
  27.3 27.4 %all-to-all-start.1 = ((bf16[4,8,2,16,1024]{4,3,2,1,0:T(8,128)(2,1)}), bf16[4,8,2,16,1024]{4,3,2,1,0:T(8,128)(2,1)S(1)}, u32[]{:S(2)}, u32[]{:S(2)}) async-start(bf16[4,8,2,16,1024]{4,3,2,1,0:T(8,128)(2,1)} %widen.4), calls=%async_computation.1 | async-start | bytes 4194304 | tf_op jit(solution)/shard_map/all_to_all | solution.py:39
  32.2 19.4 %collective-permute-start = (bf16[8,2,16,1024]{3,2,1,0:T(8,128)(2,1)S(1)}, bf16[8,2,16,1024]{3,2,1,0:T(8,128)(2,1)S(1)}, u32[]{:S(2)}, u32[]{:S(2)}) collective-permute-start(bf16[8,2,16,1024]{3,2,1,0:T(8,128)(2,1)S(1)} %all_to_all.25.x), channel_id=1, source_target_pairs={{0,1},{1,0},{2,3},{3,2},{4,5},{5,4},{6,7},{7,6},{8,9},{9,8},{10,11... | collective-permute-start | bytes 1572872 | tf_op jit(solution)/shard_map/ppermute | solution.py:144
  36.5 14.4 %collective-permute-start.1 = (bf16[128,1024]{1,0:T(8,128)(2,1)S(1)}, bf16[128,1024]{1,0:T(8,128)(2,1)S(1)}, u32[]{:S(2)}, u32[]{:S(2)}) collective-permute-start(bf16[128,1024]{1,0:T(8,128)(2,1)S(1)} %bitcast.25), channel_id=1, source_target_pairs={{0,256},{64,320},{128,384},{192,448},{1,257},{65,321},{129,385},{1... | collective-permute-start | bytes 786440 | tf_op jit(solution)/shard_map/ppermute | solution.py:140
  51.0 0.7 copy-start.3
  56.1 6.7 %copy-start.2 = (bf16[1,128,1024]{2,1,0:T(8,128)(2,1)S(1)}, bf16[1,128,1024]{2,1,0:T(8,128)(2,1)}, u32[]{:S(2)}) copy-start(bf16[1,128,1024]{2,1,0:T(8,128)(2,1)} %param.16) | copy-start | bytes 786436
  56.1 18.9 %copy-start.5 = (s32[1,256,1]{1,2,0:T(1,128)S(1)}, s32[1,256,1]{1,2,0:T(1,128)}, u32[]{:S(2)}) copy-start(s32[1,256,1]{1,2,0:T(1,128)} %param.12) | copy-start | bytes 3076
  56.1 28.3 %copy-start = (bf16[1,256,1024]{2,1,0:T(8,128)(2,1)S(1)}, bf16[1,256,1024]{2,1,0:T(8,128)(2,1)}, u32[]{:S(2)}) copy-start(bf16[1,256,1024]{2,1,0:T(8,128)(2,1)} %param.10) | copy-start | bytes 1572868
  56.1 28.3 %copy-start.4 = (bf16[128,1024]{1,0:T(8,128)(2,1)S(1)}, bf16[128,1024]{1,0:T(8,128)(2,1)}, u32[]{:S(2)}) copy-start(bf16[128,1024]{1,0:T(8,128)(2,1)} %copy-done.3) | copy-start | bytes 786436
  56.1 28.3 %all-to-all-start.2 = ((bf16[4,8,2,16,1024]{4,3,2,1,0:T(8,128)(2,1)}), bf16[4,8,2,16,1024]{4,3,2,1,0:T(8,128)(2,1)}, u32[]{:S(2)}, u32[]{:S(2)}) async-start(bf16[4,8,2,16,1024]{4,3,2,1,0:T(8,128)(2,1)} %widen.5), calls=%async_computation.2 | async-start | bytes 4194304 | tf_op jit(solution)/shard_map/all_to_all | solution.py:39
  62.7 14.8 %collective-permute-start.2 = (bf16[128,1024]{1,0:T(8,128)(2,1)S(1)}, bf16[128,1024]{1,0:T(8,128)(2,1)}, u32[]{:S(2)}, u32[]{:S(2)}) collective-permute-start(bf16[128,1024]{1,0:T(8,128)(2,1)S(1)} %bitcast.27), channel_id=1, source_target_pairs={{0,256},{64,320},{128,384},{192,448},{1,257},{65,321},{129,385},{1... | collective-permute-start | bytes 786440 | tf_op jit(solution)/shard_map/ppermute | solution.py:141
  93.2 34.7 %all-to-all-start.3 = ((bf16[64,8,1024]{2,1,0:T(8,128)(2,1)}), bf16[64,8,1024]{2,1,0:T(8,128)(2,1)S(1)}, u32[]{:S(2)}, u32[]{:S(2)}) async-start(bf16[64,8,1024]{2,1,0:T(8,128)(2,1)} %bitcast.10), calls=%async_computation.3 | async-start | bytes 2097152 | tf_op jit(solution)/shard_map/all_to_all | solution.py:178
  132.8 39.9 %copy-start.6 = (f32[1,256]{1,0:T(1,128)S(1)}, f32[1,256]{1,0:T(1,128)}, u32[]{:S(2)}) copy-start(f32[1,256]{1,0:T(1,128)} %param.11) | copy-start | bytes 3076
  132.9 39.9 %all-to-all-start.4 = ((bf16[64,8,1408]{2,1,0:T(8,128)(2,1)}), bf16[64,8,1408]{2,1,0:T(8,128)(2,1)S(1)}, u32[]{:S(2)}, u32[]{:S(2)}) async-start(bf16[64,8,1408]{2,1,0:T(8,128)(2,1)} %bitcast.31), calls=%async_computation.4 | async-start | bytes 2883584 | tf_op jit(solution)/shard_map/all_to_all | solution.py:206

commit v9 on v8

--- a/solution.py
+++ b/solution.py
@@ -14,29 +14,32 @@
 SMALL = pltpu.CompilerParams(vmem_limit_bytes=4 << 20)
 
 
-def widen_kernel(x, out, sems):
-    copies = [pltpu.make_async_copy(x, out.at[i], sems.at[i]) for i in range(out.shape[0])]
+def widen_kernel(*refs):
+    *pieces, out, sems = refs
+    copies = []
+    for i in range(out.shape[0]):
+        for k, piece in enumerate(pieces):
+            to = out.at[i, k] if len(pieces) > 1 else out.at[i]
+            copies.append(pltpu.make_async_copy(piece, to, sems.at[i, k]))
     for copy in copies:
         copy.start()
     for copy in copies:
         copy.wait()
 
 
-def widened(x, axis):
-    peers = lax.axis_size(axis)
-    return pl.pallas_call(
+def gathered(pieces, axis):
+    peers, first = lax.axis_size(axis), pieces[0]
+    inner = (len(pieces), *first.shape) if len(pieces) > 1 else first.shape
+    wide = pl.pallas_call(
         widen_kernel,
-        out_shape=jax.ShapeDtypeStruct((peers, *x.shape), x.dtype),
-        in_specs=[pl.BlockSpec(memory_space=pl.ANY)],
+        out_shape=jax.ShapeDtypeStruct((peers, *inner), first.dtype),
+        in_specs=[pl.BlockSpec(memory_space=pl.ANY)] * len(pieces),
         out_specs=pl.BlockSpec(memory_space=pltpu.HBM),
-        scratch_shapes=[pltpu.SemaphoreType.DMA((peers,))],
+        scratch_shapes=[pltpu.SemaphoreType.DMA((peers, len(pieces)))],
         compiler_params=SMALL,
         name="widen",
-    )(x)
-
-
-def gathered(x, axis):
-    return lax.all_to_all(widened(x, axis), axis, 0, 0, tiled=True)
+    )(*pieces)
+    return lax.all_to_all(wide, axis, 0, 0, tiled=True)
 
 
 def whole(mine, other, low, which):
@@ -60,8 +63,6 @@
     span = keys_far.shape[0] + keys_near.shape[0]
     valid = lax.broadcasted_iota(jnp.int32, (rows, span), 1) < length
     lane = lax.broadcasted_iota(jnp.int32, (rows, slab), 1)
-    lane_all = lax.broadcasted_iota(jnp.int32, (span, slab), 1)
-    here_all = [(lane_all >= h * dim) & (lane_all < (h + 1) * dim) for h in range(slab // dim)]
     for p in range(width // slab):
         part = slice(p * slab, (p + 1) * slab)
         keys = jnp.concatenate([keys_far[:, part], keys_near[:, part]], axis=0)
@@ -76,10 +77,9 @@
             ) * (dim**-0.5)
             scores = jnp.where(valid, scores, -1e30)
             weights = jnp.exp(scores - jnp.max(scores, axis=1, keepdims=True))
-            columns = jnp.where(here_all[h], values, jnp.ones_like(values))
-            seen = jnp.dot(weights.astype(jnp.bfloat16), columns, preferred_element_type=jnp.float32)
-            sums = pltpu.roll(seen, dim, 1)
-            found = jnp.where(here, seen / sums, found)
+            probs = weights * (1.0 / jnp.sum(weights, axis=1, keepdims=True))
+            seen = jnp.dot(probs.astype(jnp.bfloat16), values, preferred_element_type=jnp.float32)
+            found = jnp.where(here, seen, found)
         context[:, part] = found.astype(jnp.bfloat16)
     total = jnp.dot(
         context[...], whole(mine, other, low, 1), preferred_element_type=jnp.float32
@@ -112,12 +112,14 @@
     ones = jnp.where(jnp.broadcast_to(filled, (rows, 128)), 1.0, 0.0).astype(jnp.bfloat16)
     rank = jnp.dot(before, ones, preferred_element_type=jnp.float32)[:, 0:1]
     kept = filled & (rank < capacity[0].astype(jnp.float32))
+    middle = cut // 256 * 128
+    parts = [(0, first, 0, middle), (0, first, middle, cut), (cut, rest, 0, units - cut)]
     storing = []
-    for k, weight in enumerate((first, rest)):
-        part = slice(k * cut, k * cut + weight.shape[1])
-        if k == 1:
+    for k, (base, weight, low, high) in enumerate(parts):
+        part = slice(base + low, base + high)
+        if weight is rest:
             loading.wait()
-        hidden = jnp.dot(received[...], weight[...], preferred_element_type=jnp.float32)
+        hidden = jnp.dot(received[...], weight[:, low:high], preferred_element_type=jnp.float32)
         acts[:, part] = jnp.where(kept, jnp.maximum(hidden, 0.0), 0.0).astype(jnp.bfloat16)
         storing.append(pltpu.make_async_copy(acts.at[:, part], out.at[:, part], sems.at[1 + k]))
         storing[k].start()
@@ -140,11 +142,11 @@
     keys_far = lax.ppermute(mem_keys[0], "section", across)
     values_far = lax.ppermute(mem_values[0], "section", across)
 
-    spread = gathered(jnp.stack([q_weight[0], out_weight[0]]), "y")
+    spread = gathered([q_weight[0], out_weight[0]], "y")
     beside = lax.ppermute(spread, "z", [(0, 1), (1, 0)])
-    mine = gathered(spread, "x")
+    mine = gathered([spread], "x")
     mine, beside, keys_far = lax.optimization_barrier((mine, beside, keys_far))
-    other = gathered(beside, "x")
+    other = gathered([beside], "x")
     mine, other, values_far = lax.optimization_barrier((mine, other, values_far))
 
     route = routes[0, :, 0]
@@ -179,7 +181,7 @@
         buffer.reshape(experts, cap, width), AXES, split_axis=0, concat_axis=0, tiled=True
     )
     units = w_in.shape[-1]
-    cut = units // 256 * 128
+    cut = units // 512 * 512
     stored = pltpu.with_memory_space_constraint(w_in[0, 0], pltpu.HBM)
     first = pl.pallas_call(
         fetch_kernel,
@@ -198,7 +200,7 @@
         scratch_shapes=[
             pltpu.VMEM((width, units - cut), jnp.bfloat16),
             pltpu.VMEM((experts * cap, units), jnp.bfloat16),
-            pltpu.SemaphoreType.DMA((3,)),
+            pltpu.SemaphoreType.DMA((4,)),
         ],
         compiler_params=PARAMS,
         name="expert",

time: 176 us -> 173 us (0.983)
  Pallas kernels: 18.6 us -> 15.9 us
    pallas_call x1, Pallas kernels: 8.82 us -> 6.54 us  [shards(): pl.pallas_call(decode_kernel, out_shape=jax.ShapeDtypeStruct((experts * c...]
where the time goes in v9:
time: 173 us; the launch traced here: 172 us
  waiting for transfers between devices  72.8 us (42%)
  starting transfers between devices  53.5 us (31%)
  blocking collectives  24.4 us (14%)
  Pallas kernels  15.9 us (9%)
  local copies, waits for them, and re-layouts  2.25 us (1%)
    all_to_all x1, waiting for transfers between devices, shards(): lax.all_to_all(acts.reshape(experts, cap, -1), AXES, split_axis=0, concat...  33.1 us
    all_to_all x1, blocking collectives, gathered(): return lax.all_to_all(wide, axis, 0, 0, tiled=True)  24.4 us
    all_to_all x1, waiting for transfers between devices, shards(): lax.all_to_all(buffer.reshape(experts, cap, width), AXES, split_axis=0, c...  23.1 us
    ppermute x1, starting transfers between devices, shards(): values_far = lax.ppermute(mem_values[0], 'section', across)  11.6 us
    all_to_all x2, starting transfers between devices, gathered(): return lax.all_to_all(wide, axis, 0, 0, tiled=True)  11.5 us
    ppermute x1, starting transfers between devices, shards(): keys_far = lax.ppermute(mem_keys[0], 'section', across)  10 us
    all_to_all x2, waiting for transfers between devices, gathered(): return lax.all_to_all(wide, axis, 0, 0, tiled=True)  9.94 us
    all_to_all x1, starting transfers between devices, shards(): lax.all_to_all(buffer.reshape(experts, cap, width), AXES, split_axis=0, c...  9.28 us
  transfers between devices with their start and end apart: 7, of which 6 were waited for; matrix products, arithmetic and copies ran while one was open for 0% of the time, Pallas kernels for 1%

profile of v9, /device:TPU:6, one launch (start us, length us, event | category | flops | bytes accessed | tf_op | source)
XLA Modules:
  0.0 172.0 jit_solution(3158341077211450383)
XLA Ops:
  0.0 0.8 copy-done.5
  0.8 0.8 copy-done.6
  1.5 0.8 widen.3
  2.3 24.4 %all_to_all.25.refs_0_ = bf16[8,2,16,1024]{3,2,1,0:T(8,128)(2,1)S(1)} all-to-all(bf16[8,2,16,1024]{3,2,1,0:T(8,128)(2,1)S(1)} %widen.3), channel_id=1, replica_groups=mesh['section'=8,'y'=8,'x'=4,'z'=2] {'y'}, dimensions={0} | all-to-all | bytes 1048576 | tf_op jit(solution)/shard_map/all_to_all | solution.py:42
  26.7 1.4 widen.4
  28.1 0.0 copy-start.1
  28.1 4.9 %all-to-all-start.1 = ((bf16[4,8,2,16,1024]{4,3,2,1,0:T(8,128)(2,1)}), bf16[4,8,2,16,1024]{4,3,2,1,0:T(8,128)(2,1)S(1)}, u32[]{:S(2)}, u32[]{:S(2)}) async-start(bf16[4,8,2,16,1024]{4,3,2,1,0:T(8,128)(2,1)} %widen.4), calls=%async_computation.1 | async-start | bytes 4194304 | tf_op jit(solution)/shard_map/all_to_all | solution.py:42
  33.0 4.3 %collective-permute-start = (bf16[8,2,16,1024]{3,2,1,0:T(8,128)(2,1)S(1)}, bf16[8,2,16,1024]{3,2,1,0:T(8,128)(2,1)S(1)}, u32[]{:S(2)}, u32[]{:S(2)}) collective-permute-start(bf16[8,2,16,1024]{3,2,1,0:T(8,128)(2,1)S(1)} %all_to_all.25.refs_0_), channel_id=1, source_target_pairs={{0,1},{1,0},{2,3},{3,2},{4,5},{5,4},{6,7},{7,6},{8,9},{9,8},{10,11... | collective-permute-start | bytes 1572872 | tf_op jit(solution)/shard_map/ppermute | solution.py:146
  37.3 10.0 %collective-permute-start.1 = (bf16[128,1024]{1,0:T(8,128)(2,1)S(1)}, bf16[128,1024]{1,0:T(8,128)(2,1)S(1)}, u32[]{:S(2)}, u32[]{:S(2)}) collective-permute-start(bf16[128,1024]{1,0:T(8,128)(2,1)S(1)} %bitcast.27), channel_id=1, source_target_pairs={{0,256},{64,320},{128,384},{192,448},{1,257},{65,321},{129,385},{1... | collective-permute-start | bytes 786440 | tf_op jit(solution)/shard_map/ppermute | solution.py:142
  47.4 4.4 %collective-permute-done.1.keys_far = bf16[128,1024]{1,0:T(8,128)(2,1)S(1)} collective-permute-done((bf16[128,1024]{1,0:T(8,128)(2,1)S(1)}, bf16[128,1024]{1,0:T(8,128)(2,1)S(1)}, u32[]{:S(2)}, u32[]{:S(2)}) %collective-permute-start.1) | collective-permute-done | bytes 262176 | tf_op jit(solution)/shard_map/ppermute | solution.py:142
  51.8 0.7 copy-done.3
  52.5 3.1 %all-to-all-done.1.mine = bf16[4,8,2,16,1024]{4,3,2,1,0:T(8,128)(2,1)S(1)} async-done(((bf16[4,8,2,16,1024]{4,3,2,1,0:T(8,128)(2,1)}), bf16[4,8,2,16,1024]{4,3,2,1,0:T(8,128)(2,1)S(1)}, u32[]{:S(2)}, u32[]{:S(2)}) %all-to-all-start.1) | async-done | bytes 2097184 | tf_op jit(solution)/shard_map/all_to_all | solution.py:42
  55.5 1.4 widen.5
  56.9 0.0 copy-start.2
  56.9 0.0 copy-start.7
  56.9 0.0 copy-start
  56.9 0.0 copy-start.4
  56.9 6.6 %all-to-all-start.2 = ((bf16[4,8,2,16,1024]{4,3,2,1,0:T(8,128)(2,1)}), bf16[4,8,2,16,1024]{4,3,2,1,0:T(8,128)(2,1)}, u32[]{:S(2)}, u32[]{:S(2)}) async-start(bf16[4,8,2,16,1024]{4,3,2,1,0:T(8,128)(2,1)} %widen.5), calls=%async_computation.2 | async-start | bytes 4194304 | tf_op jit(solution)/shard_map/all_to_all | solution.py:42
  63.6 11.6 %collective-permute-start.2 = (bf16[128,1024]{1,0:T(8,128)(2,1)S(1)}, bf16[128,1024]{1,0:T(8,128)(2,1)}, u32[]{:S(2)}, u32[]{:S(2)}) collective-permute-start(bf16[128,1024]{1,0:T(8,128)(2,1)S(1)} %bitcast.29), channel_id=1, source_target_pairs={{0,256},{64,320},{128,384},{192,448},{1,257},{65,321},{129,385},{1... | collective-permute-start | bytes 786440 | tf_op jit(solution)/shard_map/ppermute | solution.py:143
  75.8 0.2 convert_reduce_fusion
  76.0 0.1 pad_add_fusion.facts
  76.1 2.2 %collective-permute-done.2.values_far = bf16[128,1024]{1,0:T(8,128)(2,1)} collective-permute-done((bf16[128,1024]{1,0:T(8,128)(2,1)S(1)}, bf16[128,1024]{1,0:T(8,128)(2,1)}, u32[]{:S(2)}, u32[]{:S(2)}) %collective-permute-start.2) | collective-permute-done | bytes 262176 | tf_op jit(solution)/shard_map/ppermute | solution.py:143
  78.3 6.9 %all-to-all-done.2.other = bf16[4,8,2,16,1024]{4,3,2,1,0:T(8,128)(2,1)} async-done(((bf16[4,8,2,16,1024]{4,3,2,1,0:T(8,128)(2,1)}), bf16[4,8,2,16,1024]{4,3,2,1,0:T(8,128)(2,1)}, u32[]{:S(2)}, u32[]{:S(2)}) %all-to-all-start.2) | async-done | bytes 2097184 | tf_op jit(solution)/shard_map/all_to_all | solution.py:42
  85.2 6.5 %decode.1 = bf16[512,1024]{1,0:T(8,128)(2,1)} custom-call(s32[3]{0:T(128)S(1)} %pad_add_fusion.facts, bf16[256,1024]{1,0:T(8,128)(2,1)S(1)} %bitcast.26, bf16[128,1024]{1,0:T(8,128)(2,1)S(1)} %copy-done.4, bf16[128,1024]{1,0:T(8,128)(2,1)S(1)} %bitcast.28, bf16[128,1024]{1,0:T(8,128)(2,1)} %collective-permute-done.2.values_far, ...), custom_call_target="tpu_custom_call" | custom-call | tf_op jit(solution)/shard_map/decode/pallas_call | solution.py:161
  91.8 9.3 %all-to-all-start.3 = ((bf16[64,8,1024]{2,1,0:T(8,128)(2,1)}), bf16[64,8,1024]{2,1,0:T(8,128)(2,1)S(1)}, u32[]{:S(2)}, u32[]{:S(2)}) async-start(bf16[64,8,1024]{2,1,0:T(8,128)(2,1)} %bitcast.12), calls=%async_computation.3 | async-start | bytes 2097152 | tf_op jit(solution)/shard_map/all_to_all | solution.py:180
  101.1 1.6 fetch.1.first
  103.3 23.1 %all-to-all-done.3 = bf16[64,8,1024]{2,1,0:T(8,128)(2,1)S(1)} async-done(((bf16[64,8,1024]{2,1,0:T(8,128)(2,1)}), bf16[64,8,1024]{2,1,0:T(8,128)(2,1)S(1)}, u32[]{:S(2)}, u32[]{:S(2)}) %all-to-all-start.3) | async-done | bytes 1048608 | tf_op jit(solution)/shard_map/all_to_all | solution.py:180
  126.4 4.2 %expert.1 = bf16[512,1408]{1,0:T(8,128)(2,1)} custom-call(s32[1]{0:T(128)} %bitcast.23.capacity, bf16[512,1024]{1,0:T(8,128)(2,1)S(1)} %bitcast.25, bf16[1024,1024]{1,0:T(8,128)(2,1)S(1)} %fetch.1.first, bf16[1024,1408]{1,0:T(8,128)(2,1)} %bitcast.34), custom_call_target="tpu_custom_call" | custom-call | tf_op jit(solution)/shard_map/expert/pallas_call | solution.py:195
  130.6 0.0 copy-start.8
  130.6 6.8 %all-to-all-start.4 = ((bf16[64,8,1408]{2,1,0:T(8,128)(2,1)}), bf16[64,8,1408]{2,1,0:T(8,128)(2,1)S(1)}, u32[]{:S(2)}, u32[]{:S(2)}) async-start(bf16[64,8,1408]{2,1,0:T(8,128)(2,1)} %bitcast.35), calls=%async_computation.4 | async-start | bytes 2883584 | tf_op jit(solution)/shard_map/all_to_all | solution.py:208
  137.4 33.1 %all-to-all-done.4 = bf16[64,8,1408]{2,1,0:T(8,128)(2,1)S(1)} async-done(((bf16[64,8,1408]{2,1,0:T(8,128)(2,1)}), bf16[64,8,1408]{2,1,0:T(8,128)(2,1)S(1)}, u32[]{:S(2)}, u32[]{:S(2)}) %all-to-all-start.4) | async-done | bytes 1441824 | tf_op jit(solution)/shard_map/all_to_all | solution.py:208
  170.6 1.5 fusion.1
  (12 shorter events, 0.0 us)
Async XLA Ops:
  0.0 0.8 copy-start.5
  0.8 0.8 copy-start.6
  28.1 9.2 %copy-start.1 = (bf16[1,128,1024]{2,1,0:T(8,128)(2,1)S(1)}, bf16[1,128,1024]{2,1,0:T(8,128)(2,1)}, u32[]{:S(2)}) copy-start(bf16[1,128,1024]{2,1,0:T(8,128)(2,1)} %param.15) | copy-start | bytes 786436
  28.1 27.4 %all-to-all-start.1 = ((bf16[4,8,2,16,1024]{4,3,2,1,0:T(8,128)(2,1)}), bf16[4,8,2,16,1024]{4,3,2,1,0:T(8,128)(2,1)S(1)}, u32[]{:S(2)}, u32[]{:S(2)}) async-start(bf16[4,8,2,16,1024]{4,3,2,1,0:T(8,128)(2,1)} %widen.4), calls=%async_computation.1 | async-start | bytes 4194304 | tf_op jit(solution)/shard_map/all_to_all | solution.py:42
  33.0 19.4 %collective-permute-start = (bf16[8,2,16,1024]{3,2,1,0:T(8,128)(2,1)S(1)}, bf16[8,2,16,1024]{3,2,1,0:T(8,128)(2,1)S(1)}, u32[]{:S(2)}, u32[]{:S(2)}) collective-permute-start(bf16[8,2,16,1024]{3,2,1,0:T(8,128)(2,1)S(1)} %all_to_all.25.refs_0_), channel_id=1, source_target_pairs={{0,1},{1,0},{2,3},{3,2},{4,5},{5,4},{6,7},{7,6},{8,9},{9,8},{10,11... | collective-permute-start | bytes 1572872 | tf_op jit(solution)/shard_map/ppermute | solution.py:146
  37.3 14.4 %collective-permute-start.1 = (bf16[128,1024]{1,0:T(8,128)(2,1)S(1)}, bf16[128,1024]{1,0:T(8,128)(2,1)S(1)}, u32[]{:S(2)}, u32[]{:S(2)}) collective-permute-start(bf16[128,1024]{1,0:T(8,128)(2,1)S(1)} %bitcast.27), channel_id=1, source_target_pairs={{0,256},{64,320},{128,384},{192,448},{1,257},{65,321},{129,385},{1... | collective-permute-start | bytes 786440 | tf_op jit(solution)/shard_map/ppermute | solution.py:142
  51.8 0.7 copy-start.3
  56.9 6.7 %copy-start.2 = (bf16[1,128,1024]{2,1,0:T(8,128)(2,1)S(1)}, bf16[1,128,1024]{2,1,0:T(8,128)(2,1)}, u32[]{:S(2)}) copy-start(bf16[1,128,1024]{2,1,0:T(8,128)(2,1)} %param.16) | copy-start | bytes 786436
  56.9 18.9 %copy-start.7 = (s32[1,256,1]{1,2,0:T(1,128)S(1)}, s32[1,256,1]{1,2,0:T(1,128)}, u32[]{:S(2)}) copy-start(s32[1,256,1]{1,2,0:T(1,128)} %param.12) | copy-start | bytes 3076
  56.9 28.3 %copy-start = (bf16[1,256,1024]{2,1,0:T(8,128)(2,1)S(1)}, bf16[1,256,1024]{2,1,0:T(8,128)(2,1)}, u32[]{:S(2)}) copy-start(bf16[1,256,1024]{2,1,0:T(8,128)(2,1)} %param.10) | copy-start | bytes 1572868
  56.9 28.3 %copy-start.4 = (bf16[128,1024]{1,0:T(8,128)(2,1)S(1)}, bf16[128,1024]{1,0:T(8,128)(2,1)}, u32[]{:S(2)}) copy-start(bf16[128,1024]{1,0:T(8,128)(2,1)} %copy-done.3) | copy-start | bytes 786436
  56.9 28.3 %all-to-all-start.2 = ((bf16[4,8,2,16,1024]{4,3,2,1,0:T(8,128)(2,1)}), bf16[4,8,2,16,1024]{4,3,2,1,0:T(8,128)(2,1)}, u32[]{:S(2)}, u32[]{:S(2)}) async-start(bf16[4,8,2,16,1024]{4,3,2,1,0:T(8,128)(2,1)} %widen.5), calls=%async_computation.2 | async-start | bytes 4194304 | tf_op jit(solution)/shard_map/all_to_all | solution.py:42
  63.6 14.8 %collective-permute-start.2 = (bf16[128,1024]{1,0:T(8,128)(2,1)S(1)}, bf16[128,1024]{1,0:T(8,128)(2,1)}, u32[]{:S(2)}, u32[]{:S(2)}) collective-permute-start(bf16[128,1024]{1,0:T(8,128)(2,1)S(1)} %bitcast.29), channel_id=1, source_target_pairs={{0,256},{64,320},{128,384},{192,448},{1,257},{65,321},{129,385},{1... | collective-permute-start | bytes 786440 | tf_op jit(solution)/shard_map/ppermute | solution.py:143
  91.8 34.7 %all-to-all-start.3 = ((bf16[64,8,1024]{2,1,0:T(8,128)(2,1)}), bf16[64,8,1024]{2,1,0:T(8,128)(2,1)S(1)}, u32[]{:S(2)}, u32[]{:S(2)}) async-start(bf16[64,8,1024]{2,1,0:T(8,128)(2,1)} %bitcast.12), calls=%async_computation.3 | async-start | bytes 2097152 | tf_op jit(solution)/shard_map/all_to_all | solution.py:180
  130.6 40.0 %copy-start.8 = (f32[1,256]{1,0:T(1,128)S(1)}, f32[1,256]{1,0:T(1,128)}, u32[]{:S(2)}) copy-start(f32[1,256]{1,0:T(1,128)} %param.11) | copy-start | bytes 3076
  130.6 39.9 %all-to-all-start.4 = ((bf16[64,8,1408]{2,1,0:T(8,128)(2,1)}), bf16[64,8,1408]{2,1,0:T(8,128)(2,1)S(1)}, u32[]{:S(2)}, u32[]{:S(2)}) async-start(bf16[64,8,1408]{2,1,0:T(8,128)(2,1)} %bitcast.35), calls=%async_computation.4 | async-start | bytes 2883584 | tf_op jit(solution)/shard_map/all_to_all | solution.py:208

commit v10 on v9

--- a/solution.py
+++ b/solution.py
@@ -27,19 +27,25 @@
         copy.wait()
 
 
-def gathered(pieces, axis):
+def widened(pieces, axis):
     peers, first = lax.axis_size(axis), pieces[0]
     inner = (len(pieces), *first.shape) if len(pieces) > 1 else first.shape
-    wide = pl.pallas_call(
+    return pl.pallas_call(
         widen_kernel,
         out_shape=jax.ShapeDtypeStruct((peers, *inner), first.dtype),
         in_specs=[pl.BlockSpec(memory_space=pl.ANY)] * len(pieces),
         out_specs=pl.BlockSpec(memory_space=pltpu.HBM),
         scratch_shapes=[pltpu.SemaphoreType.DMA((peers, len(pieces)))],
         compiler_params=SMALL,
+        cost_estimate=pl.CostEstimate(
+            flops=0, transcendentals=0, bytes_accessed=4 * peers * len(pieces) * first.size
+        ),
         name="widen",
     )(*pieces)
-    return lax.all_to_all(wide, axis, 0, 0, tiled=True)
+
+
+def gathered(pieces, axis):
+    return lax.all_to_all(widened(pieces, axis), axis, 0, 0, tiled=True)
 
 
 def whole(mine, other, low, which):
@@ -142,11 +148,14 @@
     keys_far = lax.ppermute(mem_keys[0], "section", across)
     values_far = lax.ppermute(mem_values[0], "section", across)
 
-    spread = gathered([q_weight[0], out_weight[0]], "y")
+    spread = gathered(
+        [pltpu.with_memory_space_constraint(w[0], pltpu.HBM) for w in (q_weight, out_weight)], "y"
+    )
     beside = lax.ppermute(spread, "z", [(0, 1), (1, 0)])
+    beside = widened([beside], "x")
     mine = gathered([spread], "x")
     mine, beside, keys_far = lax.optimization_barrier((mine, beside, keys_far))
-    other = gathered([beside], "x")
+    other = lax.all_to_all(beside, "x", 0, 0, tiled=True)
     mine, other, values_far = lax.optimization_barrier((mine, other, values_far))
 
     route = routes[0, :, 0]

time: 173 us -> 171 us (0.988)
  local copies, waits for them, and re-layouts: 2.25 us -> 0.03 us
    ppermute x1, waiting for transfers between devices: 4.39 us -> 1.85 us  [shards(): keys_far = lax.ppermute(mem_keys[0], 'section', across)]
    unnamed x18 -> x10, local copies, waits for them, and re-layouts: 2.25 us -> 0.03 us
  transfers between devices with their start and end apart: 7 -> 7, of which waited for: 6 -> 7; matrix products, arithmetic and copies ran while one was open for 0% -> 0% of each run, Pallas kernels for 1% -> 2%
where the time goes in v10:
time: 171 us; the launch traced here: 170 us
  waiting for transfers between devices  72.1 us (42%)
  starting transfers between devices  53.4 us (31%)
  blocking collectives  24.4 us (14%)
  Pallas kernels  16.4 us (10%)
    all_to_all x1, waiting for transfers between devices, shards(): lax.all_to_all(acts.reshape(experts, cap, -1), AXES, split_axis=0, concat...  33.1 us
    all_to_all x1, blocking collectives, gathered(): return lax.all_to_all(widened(pieces, axis), axis, 0, 0, tiled=True)  24.4 us
    all_to_all x1, waiting for transfers between devices, shards(): lax.all_to_all(buffer.reshape(experts, cap, width), AXES, split_axis=0, c...  23.1 us
    ppermute x1, starting transfers between devices, shards(): values_far = lax.ppermute(mem_values[0], 'section', across)  11.6 us
    ppermute x1, starting transfers between devices, shards(): keys_far = lax.ppermute(mem_keys[0], 'section', across)  10 us
    all_to_all x1, starting transfers between devices, shards(): lax.all_to_all(buffer.reshape(experts, cap, width), AXES, split_axis=0, c...  9.28 us
    all_to_all x1, waiting for transfers between devices, shards(): other = lax.all_to_all(beside, 'x', 0, 0, tiled=True)  6.88 us
    all_to_all x1, starting transfers between devices, shards(): lax.all_to_all(acts.reshape(experts, cap, -1), AXES, split_axis=0, concat...  6.81 us
  transfers between devices with their start and end apart: 7, of which 7 were waited for; matrix products, arithmetic and copies ran while one was open for 0% of the time, Pallas kernels for 2%

profile of v10, /device:TPU:6, one launch (start us, length us, event | category | flops | bytes accessed | tf_op | source)
XLA Modules:
  0.0 169.5 jit_solution(4831006574475428864)
XLA Ops:
  0.0 1.4 widen.3
  1.4 24.4 %all_to_all.25.refs_0_ = bf16[8,2,16,1024]{3,2,1,0:T(8,128)(2,1)S(1)} all-to-all(bf16[8,2,16,1024]{3,2,1,0:T(8,128)(2,1)S(1)} %widen.3), channel_id=1, replica_groups=mesh['section'=8,'y'=8,'x'=4,'z'=2] {'y'}, dimensions={0} | all-to-all | bytes 1048576 | tf_op jit(solution)/shard_map/all_to_all | solution.py:48
  25.8 1.4 widen.4
  27.1 0.0 copy-start.1
  27.2 4.9 %all-to-all-start.1 = ((bf16[4,8,2,16,1024]{4,3,2,1,0:T(8,128)(2,1)}), bf16[4,8,2,16,1024]{4,3,2,1,0:T(8,128)(2,1)S(1)}, u32[]{:S(2)}, u32[]{:S(2)}) async-start(bf16[4,8,2,16,1024]{4,3,2,1,0:T(8,128)(2,1)} %widen.4), calls=%async_computation.1 | async-start | bytes 4194304 | tf_op jit(solution)/shard_map/all_to_all | solution.py:48
  32.1 4.3 %collective-permute-start = (bf16[8,2,16,1024]{3,2,1,0:T(8,128)(2,1)S(1)}, bf16[8,2,16,1024]{3,2,1,0:T(8,128)(2,1)S(1)}, u32[]{:S(2)}, u32[]{:S(2)}) collective-permute-start(bf16[8,2,16,1024]{3,2,1,0:T(8,128)(2,1)S(1)} %all_to_all.25.refs_0_), channel_id=1, source_target_pairs={{0,1},{1,0},{2,3},{3,2},{4,5},{5,4},{6,7},{7,6},{8,9},{9,8},{10,11... | collective-permute-start | bytes 1572872 | tf_op jit(solution)/shard_map/ppermute | solution.py:154
  36.3 0.0 copy-done.1
  36.4 10.0 %collective-permute-start.1 = (bf16[128,1024]{1,0:T(8,128)(2,1)S(1)}, bf16[128,1024]{1,0:T(8,128)(2,1)S(1)}, u32[]{:S(2)}, u32[]{:S(2)}) collective-permute-start(bf16[128,1024]{1,0:T(8,128)(2,1)S(1)} %bitcast.27), channel_id=1, source_target_pairs={{0,256},{64,320},{128,384},{192,448},{1,257},{65,321},{129,385},{1... | collective-permute-start | bytes 786440 | tf_op jit(solution)/shard_map/ppermute | solution.py:148
  46.4 1.2 collective-permute-done.refs_0_
  47.5 1.3 widen.5
  48.9 0.0 copy-start.2
  48.9 0.0 copy-start.3
  48.9 0.0 copy-start
  48.9 1.8 %collective-permute-done.1.keys_far = bf16[128,1024]{1,0:T(8,128)(2,1)S(1)} collective-permute-done((bf16[128,1024]{1,0:T(8,128)(2,1)S(1)}, bf16[128,1024]{1,0:T(8,128)(2,1)S(1)}, u32[]{:S(2)}, u32[]{:S(2)}) %collective-permute-start.1) | collective-permute-done | bytes 262176 | tf_op jit(solution)/shard_map/ppermute | solution.py:148
  50.8 3.8 %all-to-all-done.1.mine = bf16[4,8,2,16,1024]{4,3,2,1,0:T(8,128)(2,1)S(1)} async-done(((bf16[4,8,2,16,1024]{4,3,2,1,0:T(8,128)(2,1)}), bf16[4,8,2,16,1024]{4,3,2,1,0:T(8,128)(2,1)S(1)}, u32[]{:S(2)}, u32[]{:S(2)}) %all-to-all-start.1) | async-done | bytes 2097184 | tf_op jit(solution)/shard_map/all_to_all | solution.py:48
  54.6 6.5 %all-to-all-start.2 = ((bf16[4,8,2,16,1024]{4,3,2,1,0:T(8,128)(2,1)}), bf16[4,8,2,16,1024]{4,3,2,1,0:T(8,128)(2,1)}, u32[]{:S(2)}, u32[]{:S(2)}) async-start(bf16[4,8,2,16,1024]{4,3,2,1,0:T(8,128)(2,1)} %widen.5), calls=%async_computation.2 | async-start | bytes 4194304 | tf_op jit(solution)/shard_map/all_to_all | solution.py:158
  61.0 0.0 copy-done.2
  61.0 11.6 %collective-permute-start.2 = (bf16[128,1024]{1,0:T(8,128)(2,1)S(1)}, bf16[128,1024]{1,0:T(8,128)(2,1)}, u32[]{:S(2)}, u32[]{:S(2)}) collective-permute-start(bf16[128,1024]{1,0:T(8,128)(2,1)S(1)} %bitcast.29), channel_id=1, source_target_pairs={{0,256},{64,320},{128,384},{192,448},{1,257},{65,321},{129,385},{1... | collective-permute-start | bytes 786440 | tf_op jit(solution)/shard_map/ppermute | solution.py:149
  73.3 0.2 convert_reduce_fusion
  73.5 0.1 pad_add_fusion.facts
  73.6 2.3 %collective-permute-done.2.values_far = bf16[128,1024]{1,0:T(8,128)(2,1)} collective-permute-done((bf16[128,1024]{1,0:T(8,128)(2,1)S(1)}, bf16[128,1024]{1,0:T(8,128)(2,1)}, u32[]{:S(2)}, u32[]{:S(2)}) %collective-permute-start.2) | collective-permute-done | bytes 262176 | tf_op jit(solution)/shard_map/ppermute | solution.py:149
  75.8 6.9 %all-to-all-done.2.other = bf16[4,8,2,16,1024]{4,3,2,1,0:T(8,128)(2,1)} async-done(((bf16[4,8,2,16,1024]{4,3,2,1,0:T(8,128)(2,1)}), bf16[4,8,2,16,1024]{4,3,2,1,0:T(8,128)(2,1)}, u32[]{:S(2)}, u32[]{:S(2)}) %all-to-all-start.2) | async-done | bytes 2097184 | tf_op jit(solution)/shard_map/all_to_all | solution.py:158
  82.7 0.0 copy-done
  82.7 6.5 %decode.1 = bf16[512,1024]{1,0:T(8,128)(2,1)} custom-call(s32[3]{0:T(128)S(1)} %pad_add_fusion.facts, bf16[256,1024]{1,0:T(8,128)(2,1)S(1)} %bitcast.26, bf16[128,1024]{1,0:T(8,128)(2,1)S(1)} %collective-permute-done.1.keys_far, bf16[128,1024]{1,0:T(8,128)(2,1)S(1)} %bitcast.28, bf16[128,1024]{1,0:T(8,128)(2,1)} %collective-permute-done.2.values_far, ...), custom_call_target="tpu_custom_call" | custom-call | tf_op jit(solution)/shard_map/decode/pallas_call | solution.py:170
  89.2 9.3 %all-to-all-start.3 = ((bf16[64,8,1024]{2,1,0:T(8,128)(2,1)}), bf16[64,8,1024]{2,1,0:T(8,128)(2,1)S(1)}, u32[]{:S(2)}, u32[]{:S(2)}) async-start(bf16[64,8,1024]{2,1,0:T(8,128)(2,1)} %bitcast.12), calls=%async_computation.3 | async-start | bytes 2097152 | tf_op jit(solution)/shard_map/all_to_all | solution.py:189
  98.5 1.6 fetch.1.first
  100.8 23.1 %all-to-all-done.3 = bf16[64,8,1024]{2,1,0:T(8,128)(2,1)S(1)} async-done(((bf16[64,8,1024]{2,1,0:T(8,128)(2,1)}), bf16[64,8,1024]{2,1,0:T(8,128)(2,1)S(1)}, u32[]{:S(2)}, u32[]{:S(2)}) %all-to-all-start.3) | async-done | bytes 1048608 | tf_op jit(solution)/shard_map/all_to_all | solution.py:189
  123.9 4.2 %expert.1 = bf16[512,1408]{1,0:T(8,128)(2,1)} custom-call(s32[1]{0:T(128)} %bitcast.23.capacity, bf16[512,1024]{1,0:T(8,128)(2,1)S(1)} %bitcast.25, bf16[1024,1024]{1,0:T(8,128)(2,1)S(1)} %fetch.1.first, bf16[1024,1408]{1,0:T(8,128)(2,1)} %bitcast.32), custom_call_target="tpu_custom_call" | custom-call | tf_op jit(solution)/shard_map/expert/pallas_call | solution.py:204
  128.1 0.0 copy-start.4
  128.1 6.8 %all-to-all-start.4 = ((bf16[64,8,1408]{2,1,0:T(8,128)(2,1)}), bf16[64,8,1408]{2,1,0:T(8,128)(2,1)S(1)}, u32[]{:S(2)}, u32[]{:S(2)}) async-start(bf16[64,8,1408]{2,1,0:T(8,128)(2,1)} %bitcast.33), calls=%async_computation.4 | async-start | bytes 2883584 | tf_op jit(solution)/shard_map/all_to_all | solution.py:217
  135.0 33.1 %all-to-all-done.4 = bf16[64,8,1408]{2,1,0:T(8,128)(2,1)S(1)} async-done(((bf16[64,8,1408]{2,1,0:T(8,128)(2,1)}), bf16[64,8,1408]{2,1,0:T(8,128)(2,1)S(1)}, u32[]{:S(2)}, u32[]{:S(2)}) %all-to-all-start.4) | async-done | bytes 1441824 | tf_op jit(solution)/shard_map/all_to_all | solution.py:217
  168.1 1.5 fusion.1
  (4 shorter events, 0.0 us)
Async XLA Ops:
  27.1 9.2 %copy-start.1 = (bf16[1,128,1024]{2,1,0:T(8,128)(2,1)S(1)}, bf16[1,128,1024]{2,1,0:T(8,128)(2,1)}, u32[]{:S(2)}) copy-start(bf16[1,128,1024]{2,1,0:T(8,128)(2,1)} %param.15) | copy-start | bytes 786436
  27.2 27.4 %all-to-all-start.1 = ((bf16[4,8,2,16,1024]{4,3,2,1,0:T(8,128)(2,1)}), bf16[4,8,2,16,1024]{4,3,2,1,0:T(8,128)(2,1)S(1)}, u32[]{:S(2)}, u32[]{:S(2)}) async-start(bf16[4,8,2,16,1024]{4,3,2,1,0:T(8,128)(2,1)} %widen.4), calls=%async_computation.1 | async-start | bytes 4194304 | tf_op jit(solution)/shard_map/all_to_all | solution.py:48
  32.1 15.5 %collective-permute-start = (bf16[8,2,16,1024]{3,2,1,0:T(8,128)(2,1)S(1)}, bf16[8,2,16,1024]{3,2,1,0:T(8,128)(2,1)S(1)}, u32[]{:S(2)}, u32[]{:S(2)}) collective-permute-start(bf16[8,2,16,1024]{3,2,1,0:T(8,128)(2,1)S(1)} %all_to_all.25.refs_0_), channel_id=1, source_target_pairs={{0,1},{1,0},{2,3},{3,2},{4,5},{5,4},{6,7},{7,6},{8,9},{9,8},{10,11... | collective-permute-start | bytes 1572872 | tf_op jit(solution)/shard_map/ppermute | solution.py:154
  36.4 14.4 %collective-permute-start.1 = (bf16[128,1024]{1,0:T(8,128)(2,1)S(1)}, bf16[128,1024]{1,0:T(8,128)(2,1)S(1)}, u32[]{:S(2)}, u32[]{:S(2)}) collective-permute-start(bf16[128,1024]{1,0:T(8,128)(2,1)S(1)} %bitcast.27), channel_id=1, source_target_pairs={{0,256},{64,320},{128,384},{192,448},{1,257},{65,321},{129,385},{1... | collective-permute-start | bytes 786440 | tf_op jit(solution)/shard_map/ppermute | solution.py:148
  48.9 12.1 %copy-start.2 = (bf16[1,128,1024]{2,1,0:T(8,128)(2,1)S(1)}, bf16[1,128,1024]{2,1,0:T(8,128)(2,1)}, u32[]{:S(2)}) copy-start(bf16[1,128,1024]{2,1,0:T(8,128)(2,1)} %param.16) | copy-start | bytes 786436
  48.9 24.4 %copy-start.3 = (s32[1,256,1]{1,2,0:T(1,128)S(1)}, s32[1,256,1]{1,2,0:T(1,128)}, u32[]{:S(2)}) copy-start(s32[1,256,1]{1,2,0:T(1,128)} %param.12) | copy-start | bytes 3076
  48.9 33.8 %copy-start = (bf16[1,256,1024]{2,1,0:T(8,128)(2,1)S(1)}, bf16[1,256,1024]{2,1,0:T(8,128)(2,1)}, u32[]{:S(2)}) copy-start(bf16[1,256,1024]{2,1,0:T(8,128)(2,1)} %param.10) | copy-start | bytes 1572868
  54.6 28.1 %all-to-all-start.2 = ((bf16[4,8,2,16,1024]{4,3,2,1,0:T(8,128)(2,1)}), bf16[4,8,2,16,1024]{4,3,2,1,0:T(8,128)(2,1)}, u32[]{:S(2)}, u32[]{:S(2)}) async-start(bf16[4,8,2,16,1024]{4,3,2,1,0:T(8,128)(2,1)} %widen.5), calls=%async_computation.2 | async-start | bytes 4194304 | tf_op jit(solution)/shard_map/all_to_all | solution.py:158
  61.0 14.8 %collective-permute-start.2 = (bf16[128,1024]{1,0:T(8,128)(2,1)S(1)}, bf16[128,1024]{1,0:T(8,128)(2,1)}, u32[]{:S(2)}, u32[]{:S(2)}) collective-permute-start(bf16[128,1024]{1,0:T(8,128)(2,1)S(1)} %bitcast.29), channel_id=1, source_target_pairs={{0,256},{64,320},{128,384},{192,448},{1,257},{65,321},{129,385},{1... | collective-permute-start | bytes 786440 | tf_op jit(solution)/shard_map/ppermute | solution.py:149
  89.2 34.7 %all-to-all-start.3 = ((bf16[64,8,1024]{2,1,0:T(8,128)(2,1)}), bf16[64,8,1024]{2,1,0:T(8,128)(2,1)S(1)}, u32[]{:S(2)}, u32[]{:S(2)}) async-start(bf16[64,8,1024]{2,1,0:T(8,128)(2,1)} %bitcast.12), calls=%async_computation.3 | async-start | bytes 2097152 | tf_op jit(solution)/shard_map/all_to_all | solution.py:189
  128.1 39.9 %copy-start.4 = (f32[1,256]{1,0:T(1,128)S(1)}, f32[1,256]{1,0:T(1,128)}, u32[]{:S(2)}) copy-start(f32[1,256]{1,0:T(1,128)} %param.11) | copy-start | bytes 3076
  128.1 39.9 %all-to-all-start.4 = ((bf16[64,8,1408]{2,1,0:T(8,128)(2,1)}), bf16[64,8,1408]{2,1,0:T(8,128)(2,1)S(1)}, u32[]{:S(2)}, u32[]{:S(2)}) async-start(bf16[64,8,1408]{2,1,0:T(8,128)(2,1)} %bitcast.33), calls=%async_computation.4 | async-start | bytes 2883584 | tf_op jit(solution)/shard_map/all_to_all | solution.py:217

commit v11 on v10

--- a/solution.py
+++ b/solution.py
@@ -56,12 +56,19 @@
 
 
 def decode_kernel(
-    facts, tokens, keys_far, keys_near, values_far, values_near, mine, other, slot, out, query, context
+    facts, tokens, keys_far, keys_near, values_far, values_near, other, slot, stored, out,
+    query, context, mine, sems
 ):
     decoding, length, low = facts[0] > 0, facts[1], facts[2] > 0
+    loading = [
+        pltpu.make_async_copy(stored.at[:, :, k], mine.at[:, :, k], sems.at[k]) for k in range(2)
+    ]
+    loading[0].start()
+    loading[1].start()
     own = tokens[...]
     rows, width = own.shape
     slab = 128
+    loading[0].wait()
     dim = width // HEADS
     query[...] = jnp.dot(
         own, whole(mine, other, low, 0), preferred_element_type=jnp.float32
@@ -87,6 +94,7 @@
             seen = jnp.dot(probs.astype(jnp.bfloat16), values, preferred_element_type=jnp.float32)
             found = jnp.where(here, seen, found)
         context[:, part] = found.astype(jnp.bfloat16)
+    loading[1].wait()
     total = jnp.dot(
         context[...], whole(mine, other, low, 1), preferred_element_type=jnp.float32
     )
@@ -170,9 +178,10 @@
     buffer = pl.pallas_call(
         decode_kernel,
         out_shape=jax.ShapeDtypeStruct((experts * cap, width), jnp.bfloat16),
-        in_specs=[SMEM] + [VMEM] * 8,
+        in_specs=[SMEM] + [VMEM] * 7 + [pl.BlockSpec(memory_space=pltpu.HBM)],
         out_specs=VMEM,
-        scratch_shapes=[pltpu.VMEM((tok_dev, width), jnp.bfloat16)] * 2,
+        scratch_shapes=[pltpu.VMEM((tok_dev, width), jnp.bfloat16)] * 2
+        + [pltpu.VMEM(mine.shape, jnp.bfloat16), pltpu.SemaphoreType.DMA((2,))],
         compiler_params=pltpu.CompilerParams(vmem_limit_bytes=32 << 20),
         name="decode",
     )(
@@ -182,9 +191,9 @@
         mem_keys[0],
         values_far,
         mem_values[0],
-        mine,
         other,
         slot[None, :],
+        pltpu.with_memory_space_constraint(mine, pltpu.HBM),
     )
     received = lax.all_to_all(
         buffer.reshape(experts, cap, width), AXES, split_axis=0, concat_axis=0, tiled=True

time: 171 us -> 172 us (level)
  no operation moved by 1% of the time
where the time goes in v11:
time: 172 us; the launch traced here: 170 us
  waiting for transfers between devices  72.5 us (42%)
  starting transfers between devices  53.3 us (31%)
  blocking collectives  24.4 us (14%)
  Pallas kernels  17 us (10%)
    all_to_all x1, waiting for transfers between devices, shards(): lax.all_to_all(acts.reshape(experts, cap, -1), AXES, split_axis=0, concat...  33.3 us
    all_to_all x1, blocking collectives, gathered(): return lax.all_to_all(widened(pieces, axis), axis, 0, 0, tiled=True)  24.4 us
    all_to_all x1, waiting for transfers between devices, shards(): lax.all_to_all(buffer.reshape(experts, cap, width), AXES, split_axis=0, c...  23.4 us
    ppermute x1, starting transfers between devices, shards(): values_far = lax.ppermute(mem_values[0], 'section', across)  11.8 us
    ppermute x1, starting transfers between devices, shards(): keys_far = lax.ppermute(mem_keys[0], 'section', across)  10 us
    all_to_all x1, starting transfers between devices, shards(): lax.all_to_all(buffer.reshape(experts, cap, width), AXES, split_axis=0, c...  9.67 us
    pallas_call x1, Pallas kernels, shards(): pl.pallas_call(decode_kernel, out_shape=jax.ShapeDtypeStruct((experts * c...  7.17 us
    all_to_all x1, starting transfers between devices, shards(): lax.all_to_all(acts.reshape(experts, cap, -1), AXES, split_axis=0, concat...  6.81 us
  transfers between devices with their start and end apart: 7, of which 7 were waited for; matrix products, arithmetic and copies ran while one was open for 0% of the time, Pallas kernels for 2%

profile of v11, /device:TPU:6, one launch (start us, length us, event | category | flops | bytes accessed | tf_op | source)
XLA Modules:
  0.0 170.5 jit_solution(13379031741420709751)
XLA Ops:
  0.0 1.4 widen.3
  1.4 24.4 %all_to_all.25.refs_0_ = bf16[8,2,16,1024]{3,2,1,0:T(8,128)(2,1)S(1)} all-to-all(bf16[8,2,16,1024]{3,2,1,0:T(8,128)(2,1)S(1)} %widen.3), channel_id=1, replica_groups=mesh['section'=8,'y'=8,'x'=4,'z'=2] {'y'}, dimensions={0} | all-to-all | bytes 1048576 | tf_op jit(solution)/shard_map/all_to_all | solution.py:48
  25.8 1.4 widen.4
  27.1 0.0 copy-start.1
  27.1 5.0 %all-to-all-start.1 = ((bf16[4,8,2,16,1024]{4,3,2,1,0:T(8,128)(2,1)}), bf16[4,8,2,16,1024]{4,3,2,1,0:T(8,128)(2,1)}, u32[]{:S(2)}, u32[]{:S(2)}) async-start(bf16[4,8,2,16,1024]{4,3,2,1,0:T(8,128)(2,1)} %widen.4), calls=%async_computation.1 | async-start | bytes 4194304 | tf_op jit(solution)/shard_map/all_to_all | solution.py:48
  32.2 4.3 %collective-permute-start = (bf16[8,2,16,1024]{3,2,1,0:T(8,128)(2,1)S(1)}, bf16[8,2,16,1024]{3,2,1,0:T(8,128)(2,1)S(1)}, u32[]{:S(2)}, u32[]{:S(2)}) collective-permute-start(bf16[8,2,16,1024]{3,2,1,0:T(8,128)(2,1)S(1)} %all_to_all.25.refs_0_), channel_id=1, source_target_pairs={{0,1},{1,0},{2,3},{3,2},{4,5},{5,4},{6,7},{7,6},{8,9},{9,8},{10,11... | collective-permute-start | bytes 1572872 | tf_op jit(solution)/shard_map/ppermute | solution.py:162
  36.4 0.0 copy-done.1
  36.5 10.0 %collective-permute-start.1 = (bf16[128,1024]{1,0:T(8,128)(2,1)S(1)}, bf16[128,1024]{1,0:T(8,128)(2,1)S(1)}, u32[]{:S(2)}, u32[]{:S(2)}) collective-permute-start(bf16[128,1024]{1,0:T(8,128)(2,1)S(1)} %bitcast.27), channel_id=1, source_target_pairs={{0,256},{64,320},{128,384},{192,448},{1,257},{65,321},{129,385},{1... | collective-permute-start | bytes 786440 | tf_op jit(solution)/shard_map/ppermute | solution.py:156
  46.5 1.5 collective-permute-done.refs_0_
  48.0 1.3 widen.5
  49.3 0.0 copy-start.2
  49.3 0.0 copy-start.3
  49.3 0.0 copy-start
  49.3 1.8 %collective-permute-done.1.keys_far = bf16[128,1024]{1,0:T(8,128)(2,1)S(1)} collective-permute-done((bf16[128,1024]{1,0:T(8,128)(2,1)S(1)}, bf16[128,1024]{1,0:T(8,128)(2,1)S(1)}, u32[]{:S(2)}, u32[]{:S(2)}) %collective-permute-start.1) | collective-permute-done | bytes 262176 | tf_op jit(solution)/shard_map/ppermute | solution.py:156
  51.2 3.6 %all-to-all-done.1.stored = bf16[4,8,2,16,1024]{4,3,2,1,0:T(8,128)(2,1)} async-done(((bf16[4,8,2,16,1024]{4,3,2,1,0:T(8,128)(2,1)}), bf16[4,8,2,16,1024]{4,3,2,1,0:T(8,128)(2,1)}, u32[]{:S(2)}, u32[]{:S(2)}) %all-to-all-start.1) | async-done | bytes 2097184 | tf_op jit(solution)/shard_map/all_to_all | solution.py:48
  54.8 5.7 %all-to-all-start.2 = ((bf16[4,8,2,16,1024]{4,3,2,1,0:T(8,128)(2,1)}), bf16[4,8,2,16,1024]{4,3,2,1,0:T(8,128)(2,1)S(1)}, u32[]{:S(2)}, u32[]{:S(2)}) async-start(bf16[4,8,2,16,1024]{4,3,2,1,0:T(8,128)(2,1)} %widen.5), calls=%async_computation.2 | async-start | bytes 4194304 | tf_op jit(solution)/shard_map/all_to_all | solution.py:166
  60.5 11.8 %collective-permute-start.2 = (bf16[128,1024]{1,0:T(8,128)(2,1)S(1)}, bf16[128,1024]{1,0:T(8,128)(2,1)}, u32[]{:S(2)}, u32[]{:S(2)}) collective-permute-start(bf16[128,1024]{1,0:T(8,128)(2,1)S(1)} %bitcast.29), channel_id=1, source_target_pairs={{0,256},{64,320},{128,384},{192,448},{1,257},{65,321},{129,385},{1... | collective-permute-start | bytes 786440 | tf_op jit(solution)/shard_map/ppermute | solution.py:157
  72.9 0.0 copy-done.3
  73.0 0.2 convert_reduce_fusion
  73.1 0.1 pad_add_fusion.facts
  73.2 2.3 %collective-permute-done.2.values_far = bf16[128,1024]{1,0:T(8,128)(2,1)} collective-permute-done((bf16[128,1024]{1,0:T(8,128)(2,1)S(1)}, bf16[128,1024]{1,0:T(8,128)(2,1)}, u32[]{:S(2)}, u32[]{:S(2)}) %collective-permute-start.2) | collective-permute-done | bytes 262176 | tf_op jit(solution)/shard_map/ppermute | solution.py:157
  75.5 6.7 %all-to-all-done.2.other = bf16[4,8,2,16,1024]{4,3,2,1,0:T(8,128)(2,1)S(1)} async-done(((bf16[4,8,2,16,1024]{4,3,2,1,0:T(8,128)(2,1)}), bf16[4,8,2,16,1024]{4,3,2,1,0:T(8,128)(2,1)S(1)}, u32[]{:S(2)}, u32[]{:S(2)}) %all-to-all-start.2) | async-done | bytes 2097184 | tf_op jit(solution)/shard_map/all_to_all | solution.py:166
  82.1 0.0 copy-done
  82.2 7.2 %decode.1 = bf16[512,1024]{1,0:T(8,128)(2,1)} custom-call(s32[3]{0:T(128)S(1)} %pad_add_fusion.facts, bf16[256,1024]{1,0:T(8,128)(2,1)S(1)} %bitcast.26, bf16[128,1024]{1,0:T(8,128)(2,1)S(1)} %collective-permute-done.1.keys_far, bf16[128,1024]{1,0:T(8,128)(2,1)S(1)} %bitcast.28, bf16[128,1024]{1,0:T(8,128)(2,1)} %collective-permute-done.2.values_far, ...), custom_call_target="tpu_custom_call" | custom-call | tf_op jit(solution)/shard_map/decode/pallas_call | solution.py:178
  89.3 9.7 %all-to-all-start.3 = ((bf16[64,8,1024]{2,1,0:T(8,128)(2,1)}), bf16[64,8,1024]{2,1,0:T(8,128)(2,1)S(1)}, u32[]{:S(2)}, u32[]{:S(2)}) async-start(bf16[64,8,1024]{2,1,0:T(8,128)(2,1)} %bitcast.12), calls=%async_computation.3 | async-start | bytes 2097152 | tf_op jit(solution)/shard_map/all_to_all | solution.py:198
  99.0 1.6 fetch.1.first
  101.3 23.4 %all-to-all-done.3 = bf16[64,8,1024]{2,1,0:T(8,128)(2,1)S(1)} async-done(((bf16[64,8,1024]{2,1,0:T(8,128)(2,1)}), bf16[64,8,1024]{2,1,0:T(8,128)(2,1)S(1)}, u32[]{:S(2)}, u32[]{:S(2)}) %all-to-all-start.3) | async-done | bytes 1048608 | tf_op jit(solution)/shard_map/all_to_all | solution.py:198
  124.7 4.2 %expert.1 = bf16[512,1408]{1,0:T(8,128)(2,1)} custom-call(s32[1]{0:T(128)} %bitcast.23.capacity, bf16[512,1024]{1,0:T(8,128)(2,1)S(1)} %bitcast.25, bf16[1024,1024]{1,0:T(8,128)(2,1)S(1)} %fetch.1.first, bf16[1024,1408]{1,0:T(8,128)(2,1)} %bitcast.32), custom_call_target="tpu_custom_call" | custom-call | tf_op jit(solution)/shard_map/expert/pallas_call | solution.py:213
  128.9 0.0 copy-start.4
  128.9 6.8 %all-to-all-start.4 = ((bf16[64,8,1408]{2,1,0:T(8,128)(2,1)}), bf16[64,8,1408]{2,1,0:T(8,128)(2,1)S(1)}, u32[]{:S(2)}, u32[]{:S(2)}) async-start(bf16[64,8,1408]{2,1,0:T(8,128)(2,1)} %bitcast.33), calls=%async_computation.4 | async-start | bytes 2883584 | tf_op jit(solution)/shard_map/all_to_all | solution.py:226
  135.7 33.3 %all-to-all-done.4 = bf16[64,8,1408]{2,1,0:T(8,128)(2,1)S(1)} async-done(((bf16[64,8,1408]{2,1,0:T(8,128)(2,1)}), bf16[64,8,1408]{2,1,0:T(8,128)(2,1)S(1)}, u32[]{:S(2)}, u32[]{:S(2)}) %all-to-all-start.4) | async-done | bytes 1441824 | tf_op jit(solution)/shard_map/all_to_all | solution.py:226
  169.0 1.5 fusion.1
  (4 shorter events, 0.0 us)
Async XLA Ops:
  27.1 9.3 %copy-start.1 = (bf16[1,128,1024]{2,1,0:T(8,128)(2,1)S(1)}, bf16[1,128,1024]{2,1,0:T(8,128)(2,1)}, u32[]{:S(2)}) copy-start(bf16[1,128,1024]{2,1,0:T(8,128)(2,1)} %param.15) | copy-start | bytes 786436
  27.1 27.7 %all-to-all-start.1 = ((bf16[4,8,2,16,1024]{4,3,2,1,0:T(8,128)(2,1)}), bf16[4,8,2,16,1024]{4,3,2,1,0:T(8,128)(2,1)}, u32[]{:S(2)}, u32[]{:S(2)}) async-start(bf16[4,8,2,16,1024]{4,3,2,1,0:T(8,128)(2,1)} %widen.4), calls=%async_computation.1 | async-start | bytes 4194304 | tf_op jit(solution)/shard_map/all_to_all | solution.py:48
  32.2 15.8 %collective-permute-start = (bf16[8,2,16,1024]{3,2,1,0:T(8,128)(2,1)S(1)}, bf16[8,2,16,1024]{3,2,1,0:T(8,128)(2,1)S(1)}, u32[]{:S(2)}, u32[]{:S(2)}) collective-permute-start(bf16[8,2,16,1024]{3,2,1,0:T(8,128)(2,1)S(1)} %all_to_all.25.refs_0_), channel_id=1, source_target_pairs={{0,1},{1,0},{2,3},{3,2},{4,5},{5,4},{6,7},{7,6},{8,9},{9,8},{10,11... | collective-permute-start | bytes 1572872 | tf_op jit(solution)/shard_map/ppermute | solution.py:162
  36.5 14.7 %collective-permute-start.1 = (bf16[128,1024]{1,0:T(8,128)(2,1)S(1)}, bf16[128,1024]{1,0:T(8,128)(2,1)S(1)}, u32[]{:S(2)}, u32[]{:S(2)}) collective-permute-start(bf16[128,1024]{1,0:T(8,128)(2,1)S(1)} %bitcast.27), channel_id=1, source_target_pairs={{0,256},{64,320},{128,384},{192,448},{1,257},{65,321},{129,385},{1... | collective-permute-start | bytes 786440 | tf_op jit(solution)/shard_map/ppermute | solution.py:156
  49.3 11.2 %copy-start.2 = (bf16[1,128,1024]{2,1,0:T(8,128)(2,1)S(1)}, bf16[1,128,1024]{2,1,0:T(8,128)(2,1)}, u32[]{:S(2)}) copy-start(bf16[1,128,1024]{2,1,0:T(8,128)(2,1)} %param.16) | copy-start | bytes 786436
  49.3 23.6 %copy-start.3 = (s32[1,256,1]{1,2,0:T(1,128)S(1)}, s32[1,256,1]{1,2,0:T(1,128)}, u32[]{:S(2)}) copy-start(s32[1,256,1]{1,2,0:T(1,128)} %param.12) | copy-start | bytes 3076
  49.3 32.8 %copy-start = (bf16[1,256,1024]{2,1,0:T(8,128)(2,1)S(1)}, bf16[1,256,1024]{2,1,0:T(8,128)(2,1)}, u32[]{:S(2)}) copy-start(bf16[1,256,1024]{2,1,0:T(8,128)(2,1)} %param.10) | copy-start | bytes 1572868
  54.8 27.4 %all-to-all-start.2 = ((bf16[4,8,2,16,1024]{4,3,2,1,0:T(8,128)(2,1)}), bf16[4,8,2,16,1024]{4,3,2,1,0:T(8,128)(2,1)S(1)}, u32[]{:S(2)}, u32[]{:S(2)}) async-start(bf16[4,8,2,16,1024]{4,3,2,1,0:T(8,128)(2,1)} %widen.5), calls=%async_computation.2 | async-start | bytes 4194304 | tf_op jit(solution)/shard_map/all_to_all | solution.py:166
  60.5 15.0 %collective-permute-start.2 = (bf16[128,1024]{1,0:T(8,128)(2,1)S(1)}, bf16[128,1024]{1,0:T(8,128)(2,1)}, u32[]{:S(2)}, u32[]{:S(2)}) collective-permute-start(bf16[128,1024]{1,0:T(8,128)(2,1)S(1)} %bitcast.29), channel_id=1, source_target_pairs={{0,256},{64,320},{128,384},{192,448},{1,257},{65,321},{129,385},{1... | collective-permute-start | bytes 786440 | tf_op jit(solution)/shard_map/ppermute | solution.py:157
  89.3 35.3 %all-to-all-start.3 = ((bf16[64,8,1024]{2,1,0:T(8,128)(2,1)}), bf16[64,8,1024]{2,1,0:T(8,128)(2,1)S(1)}, u32[]{:S(2)}, u32[]{:S(2)}) async-start(bf16[64,8,1024]{2,1,0:T(8,128)(2,1)} %bitcast.12), calls=%async_computation.3 | async-start | bytes 2097152 | tf_op jit(solution)/shard_map/all_to_all | solution.py:198
  128.9 40.1 %copy-start.4 = (f32[1,256]{1,0:T(1,128)S(1)}, f32[1,256]{1,0:T(1,128)}, u32[]{:S(2)}) copy-start(f32[1,256]{1,0:T(1,128)} %param.11) | copy-start | bytes 3076
  128.9 40.1 %all-to-all-start.4 = ((bf16[64,8,1408]{2,1,0:T(8,128)(2,1)}), bf16[64,8,1408]{2,1,0:T(8,128)(2,1)S(1)}, u32[]{:S(2)}, u32[]{:S(2)}) async-start(bf16[64,8,1408]{2,1,0:T(8,128)(2,1)} %bitcast.33), calls=%async_computation.4 | async-start | bytes 2883584 | tf_op jit(solution)/shard_map/all_to_all | solution.py:226
